TPU v7x, 256 devices: a whole 4x4x8 slice. The times are simulated.
256 devices in a mesh: section: 8 (over z), seq: 32 (over x, y, core).
Axes of the slice: x: 4, y: 4, z: 8, core: 2. Of those that a mesh axis runs over, the one named last changes fastest.
Arguments:
- section_input: bfloat16 [8, 8192, 1024], P('section', 'seq'), may hold values from -6 to 6
- stashed_input: bfloat16 [8, 8192, 1024], P('section', 'seq'), may hold values from -6 to 6
- output_grad: bfloat16 [8, 8192, 1024], P('section', 'seq'), may hold values from -6 to 6
- gain_mixer: float32 [8, 1024], P('section'), may hold values from 0.1 to 1.9
- gain_channel: float32 [8, 1024], P('section'), may hold values from 0.1 to 1.9
- factor_first: bfloat16 [8, 64, 128, 128], P('section', 'seq'), may hold values from -0.5 to 0.5
- factor_second: bfloat16 [8, 128, 64, 64], P('section', 'seq'), may hold values from -0.75 to 0.75
- spectrum: bfloat16 [8, 64, 128, 1024], P('section', None, 'seq'), may hold values from -6 to 6
- factor_third: bfloat16 [8, 128, 64, 64], P('section', 'seq'), may hold values from -0.75 to 0.75
- factor_fourth: bfloat16 [8, 64, 128, 128], P('section', 'seq'), may hold values from -0.5 to 0.5
- mixer_gate: bfloat16 [8, 1024, 256], P('section'), may hold values from -0.375 to 0.375
- channel_up: bfloat16 [8, 1024, 512], P('section'), may hold values from -0.375 to 0.375
- channel_gate: bfloat16 [8, 1024, 512], P('section'), may hold values from -0.375 to 0.375
- channel_down: bfloat16 [8, 2048, 256], P('section'), may hold values from -0.25 to 0.25
Outputs:
- next_input: bfloat16 [8, 8192, 1024], P('section', 'seq')
- upstream_grad: bfloat16 [8, 8192, 1024], P('section', 'seq')
- spectrum_grad: bfloat16 [8, 64, 128, 1024], P('section', None, 'seq')
- mixer_gate_grad: bfloat16 [8, 1024, 256], P('section', 'seq')
- channel_up_grad: bfloat16 [8, 1024, 512], P('section', 'seq')
- channel_gate_grad: bfloat16 [8, 1024, 512], P('section', 'seq')
- channel_down_grad: bfloat16 [8, 2048, 256], P('section', 'seq')
All inputs are finite; a program needn't handle non-finite values.
Results may differ from a plain program's by a relative error of at most 0.017.
Values may be sent and summed in bfloat16 or wider, within the bound.
No kernel may reach another device: no remote copies, remote signals or barrier semaphores. Data moves between devices by JAX's collectives and lax.ppermute only.
A program may use at most 128 MiB of HBM per device.

v0:
```python
import math

import jax
import jax.numpy as jnp
from jax import lax
from jax.sharding import PartitionSpec as P

NB = 4
NI = 64
NJ = 128


epsilon = 1e-06


def from_behind(array, axis, by):
    length = lax.axis_size(axis)
    pairs = [(i, i + by) for i in range(length) if 0 <= i + by < length]
    return lax.ppermute(array, axis, pairs)


def bround(value):
    return lax.optimization_barrier(value.astype(jnp.bfloat16))


def rms_scale(value_array):
    return lax.rsqrt(jnp.mean(value_array * value_array, axis=-1, keepdims=True) + epsilon)


def norm_back(value_array, scale, gain, incoming_gradient):
    scaled = gain * incoming_gradient
    return scale * scaled - value_array * (scale * scale * scale) * jnp.mean(
        scaled * value_array, axis=-1, keepdims=True
    )


def block_apply(value_array, weight, block_list):
    item_count = value_array.shape[0]
    reshaped_array = weight.reshape(block_list, weight.shape[0] // block_list, weight.shape[1])
    final_output = jnp.einsum(
        "ynq,nqd->ynd",
        value_array.reshape(item_count, block_list, -1),
        reshaped_array,
        preferred_element_type=jnp.float32,
    )
    return final_output.reshape(item_count, -1)


def block_back(incoming_gradient, weight, block_list):
    item_count = incoming_gradient.shape[0]
    reshaped_array = weight.reshape(block_list, weight.shape[0] // block_list, weight.shape[1])
    final_output = jnp.einsum(
        "eaq,awq->eaw",
        incoming_gradient.reshape(item_count, block_list, -1),
        reshaped_array,
        preferred_element_type=jnp.float32,
    )
    return final_output.reshape(item_count, -1)


def block_grad(value_array, incoming_gradient, block_list):
    item_count = value_array.shape[0]
    final_output = jnp.einsum(
        "wli,wld->lid",
        value_array.reshape(item_count, block_list, -1),
        incoming_gradient.reshape(item_count, block_list, -1),
        preferred_element_type=jnp.float32,
    )
    return final_output.reshape(-1, final_output.shape[2])


def shuffle(value_array, block_list):
    item_count = value_array.shape[0]
    return (
        value_array.reshape(item_count, block_list, block_list, -1)
        .transpose(0, 2, 1, 3)
        .reshape(item_count, -1)
    )


def mixer_front(wide, gain, first, row_count, col_count):
    scale = rms_scale(wide)
    normed = (wide * scale * gain).astype(jnp.bfloat16)
    folded = jnp.einsum(
        "iqj,ijc->iqc",
        first,
        normed.reshape(row_count, col_count, -1),
        preferred_element_type=jnp.float32,
    )
    return (scale, normed, folded.astype(jnp.bfloat16))


def mixer_middle(received, second, kernel_here, third):
    mixed = jnp.einsum("jpi,ijc->pjc", second, received, preferred_element_type=jnp.float32)
    filtered = (mixed * kernel_here).astype(jnp.bfloat16)
    returned = jnp.einsum("jpi,ijc->pjc", third, filtered, preferred_element_type=jnp.float32)
    return (mixed, returned.astype(jnp.bfloat16))


def layer_tail(
    wide,
    normed,
    collected,
    fourth_factor,
    gain,
    mixing_weight,
    up_weight,
    activation_weight,
    down_weight,
    block_list,
):
    item_count = wide.shape[0]
    back_mixed = jnp.einsum(
        "iqj,ijc->iqc", fourth_factor, collected, preferred_element_type=jnp.float32
    ).reshape(item_count, -1)
    gating = block_apply(normed, mixing_weight, block_list)
    middle = bround(wide + back_mixed * gating)
    middle_wide = middle.astype(jnp.float32)
    scale_two = rms_scale(middle_wide)
    normed_two = (middle_wide * scale_two * gain).astype(jnp.bfloat16)
    lifted = block_apply(normed_two, up_weight, block_list)
    gated = block_apply(normed_two, activation_weight, block_list)
    hidden = (jax.nn.silu(gated) * lifted).astype(jnp.bfloat16)
    shuffled = shuffle(hidden, block_list)
    output = (middle_wide + block_apply(shuffled, down_weight, block_list)).astype(jnp.bfloat16)
    return (
        output,
        (back_mixed, gating, middle_wide, scale_two, normed_two, lifted, gated, shuffled),
    )


def shards(
    section_input,
    stashed_input,
    output_grad,
    gain_mixer,
    gain_channel,
    factor_first,
    factor_second,
    spectrum,
    factor_third,
    factor_fourth,
    mixer_gate,
    channel_up,
    channel_gate,
    channel_down,
):
    first = factor_first[0]
    second = factor_second[0]
    kernel_here = spectrum[0]
    third = factor_third[0]
    fourth_factor = factor_fourth[0]
    mixing_weight = mixer_gate[0]
    up_weight = channel_up[0]
    activation_weight = channel_gate[0]
    down_weight = channel_down[0]
    gain_one = gain_mixer[0]
    second_gain = gain_channel[0]
    block_list = NB
    row_count = first.shape[0]
    col_count = first.shape[1]
    grad_factor = 1.0 / math.sqrt(NI * NJ)
    expanded_forward = section_input[0].astype(jnp.float32)
    expanded_backward = stashed_input[0].astype(jnp.float32)
    scale_fwd, normalized_forward, folded_fwd = mixer_front(
        expanded_forward, gain_one, first, row_count, col_count
    )
    scale_back, normalized_backward, folded_back = mixer_front(
        expanded_backward, gain_one, first, row_count, col_count
    )
    recv_fwd, recv_back = (
        lax.all_to_all(folded_fwd, "seq", split_axis=1, concat_axis=0, tiled=True),
        lax.all_to_all(folded_back, "seq", split_axis=1, concat_axis=0, tiled=True),
    )
    mixed_fwd, returned_fwd = mixer_middle(recv_fwd, second, kernel_here, third)
    mixed_back, returned_back = mixer_middle(recv_back, second, kernel_here, third)
    gathered_forward, gathered_backward = (
        lax.all_to_all(returned_fwd, "seq", split_axis=0, concat_axis=1, tiled=True),
        lax.all_to_all(returned_back, "seq", split_axis=0, concat_axis=1, tiled=True),
    )
    output_fwd, unused = layer_tail(
        expanded_forward,
        normalized_forward,
        gathered_forward,
        fourth_factor,
        second_gain,
        mixing_weight,
        up_weight,
        activation_weight,
        down_weight,
        block_list,
    )
    next_input = from_behind(output_fwd[None], "section", 1)
    output_back, saved = layer_tail(
        expanded_backward,
        normalized_backward,
        gathered_backward,
        fourth_factor,
        second_gain,
        mixing_weight,
        up_weight,
        activation_weight,
        down_weight,
        block_list,
    )
    back_mixed, gating, middle_wide, scale_two, normed_two, lifted, gated, shuffled = saved
    incoming_gradient = output_grad[0]
    up_wide = incoming_gradient.astype(jnp.float32)
    d_shuffled = bround(block_back(incoming_gradient, down_weight, block_list))
    d_hidden = shuffle(d_shuffled, block_list).astype(jnp.float32)
    sigma = jax.nn.sigmoid(gated)
    d_lift = (d_hidden * gated * sigma).astype(jnp.bfloat16)
    d_gated = (d_hidden * lifted * sigma * (1.0 + gated * (1.0 - sigma))).astype(jnp.bfloat16)
    d_norm_two = block_back(d_lift, up_weight, block_list) + block_back(
        d_gated, activation_weight, block_list
    )
    d_middle = bround(up_wide + norm_back(middle_wide, scale_two, second_gain, d_norm_two))
    d_mid_wide = d_middle.astype(jnp.float32)
    d_back = (d_mid_wide * gating).astype(jnp.bfloat16)
    d_gating = (d_mid_wide * back_mixed).astype(jnp.bfloat16)
    d_returned = jnp.einsum(
        "iqj,iqc->ijc",
        fourth_factor,
        d_back.reshape(row_count, col_count, -1),
        preferred_element_type=jnp.float32,
    ).astype(jnp.bfloat16)
    d_recv = lax.all_to_all(d_returned, "seq", split_axis=1, concat_axis=0, tiled=True)
    d_filtered = jnp.einsum("jpi,pjc->ijc", third, d_recv, preferred_element_type=jnp.float32)
    kernel_grad = (d_filtered * mixed_back).astype(jnp.bfloat16)
    d_mixed = (d_filtered * kernel_here).astype(jnp.bfloat16)
    d_folded = jnp.einsum(
        "jpi,pjc->ijc", second, d_mixed, preferred_element_type=jnp.float32
    ).astype(jnp.bfloat16)
    d_rows = lax.all_to_all(d_folded, "seq", split_axis=0, concat_axis=1, tiled=True)
    item_count = expanded_backward.shape[0]
    d_normed = jnp.einsum(
        "iqj,iqc->ijc", first, d_rows, preferred_element_type=jnp.float32
    ).reshape(item_count, -1)
    d_normed = d_normed + block_back(d_gating, mixing_weight, block_list)
    d_input = (d_mid_wide + norm_back(expanded_backward, scale_back, gain_one, d_normed)).astype(
        jnp.bfloat16
    )
    upstream_grad = from_behind(d_input[None], "section", -1)
    term_mix = block_grad(normalized_backward, d_gating, block_list) * grad_factor
    term_up = block_grad(normed_two, d_lift, block_list) * grad_factor
    term_act = block_grad(normed_two, d_gated, block_list) * grad_factor
    term_down = block_grad(shuffled, incoming_gradient, block_list) * grad_factor
    part_mix, part_up, part_act, part_down = (
        lax.psum_scatter(
            term_mix.astype(jnp.bfloat16), "seq", scatter_dimension=0, tiled=True
        ).astype(jnp.float32),
        lax.psum_scatter(
            term_up.astype(jnp.bfloat16), "seq", scatter_dimension=0, tiled=True
        ).astype(jnp.float32),
        lax.psum_scatter(
            term_act.astype(jnp.bfloat16), "seq", scatter_dimension=0, tiled=True
        ).astype(jnp.float32),
        lax.psum_scatter(
            term_down.astype(jnp.bfloat16), "seq", scatter_dimension=0, tiled=True
        ).astype(jnp.float32),
    )
    return (
        next_input,
        upstream_grad,
        kernel_grad[None],
        part_mix.astype(jnp.bfloat16)[None],
        part_up.astype(jnp.bfloat16)[None],
        part_act.astype(jnp.bfloat16)[None],
        part_down.astype(jnp.bfloat16)[None],
    )


def solution(mesh):
    in_specs = (
        P("section", "seq", None),
        P("section", "seq", None),
        P("section", "seq", None),
        P("section", None),
        P("section", None),
        P("section", "seq", None, None),
        P("section", "seq", None, None),
        P("section", None, "seq", None),
        P("section", "seq", None, None),
        P("section", "seq", None, None),
        P("section", None, None),
        P("section", None, None),
        P("section", None, None),
        P("section", None, None),
    )
    out_specs = (
        P("section", "seq", None),
        P("section", "seq", None),
        P("section", None, "seq", None),
        P("section", "seq", None),
        P("section", "seq", None),
        P("section", "seq", None),
        P("section", "seq", None),
    )
    return jax.shard_map(shards, mesh=mesh, in_specs=in_specs, out_specs=out_specs, check_vma=False)
```

profile of v0, /device:TPU:1, one launch (start us, length us, event | category | flops | bytes accessed | tf_op | source)
XLA Modules:
  0.0 489.8 jit_solution(8661578263723097282)
XLA Ops:
  11.3 8.6 %all-to-all-start = ((bf16[2,128,1024]{2,0,1:T(2,128)(2,1)}), bf16[2,128,1024]{2,0,1:T(2,128)(2,1)}, u32[]{:S(2)}, u32[]{:S(2)}) async-start(bf16[2,128,1024]{2,0,1:T(2,128)(2,1)} %copy.106), calls=%async_computation | async-start | bytes 1048576 | tf_op jit(solution)/shard_map/all_to_all | solution.py:172
  22.7 2.9 convolution_convert_fusion
  25.6 1.6 fusion.44
  28.7 3.0 copy.131
  31.7 3.1 reshape.271
  34.7 2.5 copy.115
  38.5 2.1 copy.122
  40.6 7.4 %all-to-all-start.2 = ((bf16[2,128,1024]{2,0,1:T(2,128)(2,1)}), bf16[2,128,1024]{2,0,1:T(2,128)(2,1)}, u32[]{:S(2)}, u32[]{:S(2)}) async-start(bf16[2,128,1024]{2,0,1:T(2,128)(2,1)} %copy.122), calls=%async_computation.2 | async-start | bytes 1048576 | tf_op jit(solution)/shard_map/all_to_all | solution.py:173
  48.0 2.6 fusion.74
  50.6 1.6 copy.129
  52.2 2.5 copy.107
  54.7 2.9 fusion.10
  57.6 2.3 copy.110
  59.9 7.4 %all-to-all-start.1 = ((bf16[64,4,1024]{2,1,0:T(4,128)(2,1)}), bf16[64,4,1024]{2,1,0:T(4,128)(2,1)}, u32[]{:S(2)}, u32[]{:S(2)}) async-start(bf16[64,4,1024]{2,1,0:T(4,128)(2,1)} %copy.110), calls=%async_computation.1 | async-start | bytes 1048576 | tf_op jit(solution)/shard_map/all_to_all | solution.py:178
  67.3 2.2 copy.123
  69.5 2.0 all_to_all.89
  73.9 1.6 fusion.11
  76.7 2.2 all-to-all-done.1
  79.0 5.2 %all-to-all-start.3 = ((bf16[64,4,1024]{2,1,0:T(4,128)(2,1)}), bf16[64,4,1024]{2,1,0:T(4,128)(2,1)}, u32[]{:S(2)}, u32[]{:S(2)}) async-start(bf16[64,4,1024]{2,1,0:T(4,128)(2,1)} %copy.124), calls=%async_computation.3 | async-start | bytes 1048576 | tf_op jit(solution)/shard_map/all_to_all | solution.py:179
  84.4 2.0 copy.210
  86.4 2.0 all_to_all.85
  91.1 4.7 all-to-all-done.3
  95.8 2.0 copy.209
  101.5 2.0 copy.167
  103.5 2.9 convolution_bitcast_fusion
  106.4 2.9 reshape.262
  109.3 5.5 %multiply_convert_fusion.3 = (bf16[256,4,512]{2,0,1:T(8,128)(2,1)}, bf16[256,4,512]{2,0,1:T(8,128)(2,1)}, f32[256,4,512]{2,0,1:T(8,128)}) fusion(f32[256,4,512]{2,0,1:T(8,128)} %reshape.271, f32[256,4,512]{2,0,1:T(8,128)} %convolution_bitcast_fusion, bf16[256,4,256]{0,2,1:T(8,128)(2,1)} %bitcast.280, bf16[4,256,512]{2,1,0:T(8,128)(2,1)S(1)} %bitcast.268), kind=kOutput, calls=%fused_computation.7 | convolution fusion | flops 275251200 | bytes 9961472 | tf_op jit(solution)/shard_map/ynq,nqd->ynd/dot_general | solution.py:40
  114.8 3.0 reshape.261
  117.8 1.8 fusion.94
  119.5 1.5 convolution_add_fusion
  121.0 2.5 copy.134
  123.6 1.5 fusion.28
  125.1 2.6 fusion.27
  130.6 4.3 fusion.43
  134.9 2.5 copy.150
  137.4 2.6 multiply_convert_fusion
  140.1 2.3 fusion.8
  142.3 2.0 copy.137
  144.3 4.4 all-to-all-start.4
  149.0 1.8 convolution_bitcast_fusion.2
  150.8 2.9 reshape.251
  153.7 1.8 convolution_bitcast_fusion.3
  155.6 3.0 reshape.250
  158.6 1.4 multiply_convert_fusion.1
  160.1 4.4 fusion.42
  164.8 1.5 reshape.273
  166.3 2.3 copy.166
  169.9 3.1 copy.118
  173.0 2.3 reshape_reshape.6
  175.3 2.7 fusion.93
  178.0 2.6 copy.120
  180.6 2.3 copy.138
  187.2 7.1 %all-to-all-start.5 = ((bf16[64,4,1024]{2,1,0:T(4,128)(2,1)}), bf16[64,4,1024]{2,1,0:T(4,128)(2,1)}, u32[]{:S(2)}, u32[]{:S(2)}) async-start(bf16[64,4,1024]{2,1,0:T(4,128)(2,1)} %copy.141), calls=%async_computation.5 | async-start | bytes 1048576 | tf_op jit(solution)/shard_map/all_to_all | solution.py:234
  194.3 2.7 multiply_convert_fusion.2
  197.1 2.3 fusion.48
  199.3 4.3 collective-permute-start
  203.7 2.3 all-to-all-done.5
  205.9 2.0 copy.208
  209.1 1.8 fusion.38
  214.2 13.3 %collective-permute-done.1 = bf16[1,256,1024]{2,1,0:T(8,128)(2,1)S(1)} collective-permute-done((bf16[1,256,1024]{2,1,0:T(8,128)(2,1)S(1)}, bf16[1,256,1024]{2,1,0:T(8,128)(2,1)S(1)}, u32[]{:S(2)}, u32[]{:S(2)}) %collective-permute-start.1) | collective-permute-done | bytes 524320 | tf_op jit(solution)/shard_map/ppermute | solution.py:19
  227.5 74.7 %reduce-scatter.11.cloned.1.call-done = bf16[64,256]{1,0:T(8,128)(2,1)} async-done(((bf16[2048,256]{1,0:T(8,128)(2,1)}), bf16[64,256]{1,0:T(8,128)(2,1)}) %reduce-scatter.11.cloned.1.call-update) | async-done | bytes 32784 | tf_op jit(solution)/shard_map/reduce_scatter | solution.py:258
  302.2 89.1 %reduce-scatter.9.cloned.1.call-done = bf16[32,512]{1,0:T(8,128)(2,1)} async-done(((bf16[1024,512]{1,0:T(8,128)(2,1)}), bf16[32,512]{1,0:T(8,128)(2,1)}) %reduce-scatter.9.cloned.1.call-update) | async-done | bytes 32784 | tf_op jit(solution)/shard_map/reduce_scatter | solution.py:255
  391.3 89.2 %reduce-scatter.7.cloned.1.call-done = bf16[32,512]{1,0:T(8,128)(2,1)} async-done(((bf16[1024,512]{1,0:T(8,128)(2,1)}), bf16[32,512]{1,0:T(8,128)(2,1)}) %reduce-scatter.7.cloned.1.call-update) | async-done | bytes 32784 | tf_op jit(solution)/shard_map/reduce_scatter | solution.py:252
  480.6 1.9 copy.213
  (141 shorter events, 33.9 us)
Async XLA Ops:
  7.2 102.2 %copy-start = (bf16[1,1024,512]{2,1,0:T(8,128)(2,1)S(1)}, bf16[1,1024,512]{2,1,0:T(8,128)(2,1)}, u32[]{:S(2)}) copy-start(bf16[1,1024,512]{2,1,0:T(8,128)(2,1)} %param.26) | copy-start | bytes 3145732
  7.2 2.5 copy-start.37
  7.2 2.5 copy-start.41
  9.7 10.2 %copy-start.17 = (bf16[1,256,1024]{2,1,0:T(8,128)(2,1)S(1)}, bf16[1,256,1024]{2,1,0:T(8,128)(2,1)}, u32[]{:S(2)}) copy-start(bf16[1,256,1024]{2,1,0:T(8,128)(2,1)} %param.14) | copy-start | bytes 1572868
  10.1 12.2 %copy-start.34 = (bf16[1,256,1024]{2,1,0:T(8,128)(2,1)S(1)}, bf16[1,256,1024]{2,1,0:T(8,128)(2,1)}, u32[]{:S(2)}) copy-start(bf16[1,256,1024]{2,1,0:T(8,128)(2,1)} %param.16) | copy-start | bytes 1572868
  11.3 29.3 %all-to-all-start = ((bf16[2,128,1024]{2,0,1:T(2,128)(2,1)}), bf16[2,128,1024]{2,0,1:T(2,128)(2,1)}, u32[]{:S(2)}, u32[]{:S(2)}) async-start(bf16[2,128,1024]{2,0,1:T(2,128)(2,1)} %copy.106), calls=%async_computation | async-start | bytes 1048576 | tf_op jit(solution)/shard_map/all_to_all | solution.py:172
  21.1 4.5 copy-start.21
  22.7 4.5 copy-start.35
  22.7 2.9 copy-start.31
  22.7 4.5 copy-start.1
  28.7 8.6 %copy-start.7 = (f32[1,256,1024]{2,1,0:T(8,128)}, f32[1,256,1024]{2,1,0:T(8,128)S(1)}, u32[]{:S(2)}) copy-start(f32[1,256,1024]{2,1,0:T(8,128)S(1)} %convert_element_type.292) | copy-start | bytes 3145732
  38.5 9.6 %copy-start.14 = (f32[1,256,1024]{1,2,0:T(8,128)S(1)}, f32[1,256,1024]{1,2,0:T(8,128)}, u32[]{:S(2)}) copy-start(f32[1,256,1024]{1,2,0:T(8,128)} %copy.165) | copy-start | bytes 3145732
  40.6 19.3 %all-to-all-start.2 = ((bf16[2,128,1024]{2,0,1:T(2,128)(2,1)}), bf16[2,128,1024]{2,0,1:T(2,128)(2,1)}, u32[]{:S(2)}, u32[]{:S(2)}) async-start(bf16[2,128,1024]{2,0,1:T(2,128)(2,1)} %copy.122), calls=%async_computation.2 | async-start | bytes 1048576 | tf_op jit(solution)/shard_map/all_to_all | solution.py:173
  50.6 4.1 copy-start.39
  50.6 4.1 copy-start.40
  52.2 47.1 %copy-start.3 = (f32[256,1024]{1,0:T(8,128)}, f32[256,1024]{1,0:T(8,128)S(1)}, u32[]{:S(2)}) copy-start(f32[256,1024]{1,0:T(8,128)S(1)} %copy.129) | copy-start | bytes 3145732
  59.9 19.1 %all-to-all-start.1 = ((bf16[64,4,1024]{2,1,0:T(4,128)(2,1)}), bf16[64,4,1024]{2,1,0:T(4,128)(2,1)}, u32[]{:S(2)}, u32[]{:S(2)}) async-start(bf16[64,4,1024]{2,1,0:T(4,128)(2,1)} %copy.110), calls=%async_computation.1 | async-start | bytes 1048576 | tf_op jit(solution)/shard_map/all_to_all | solution.py:178
  72.9 1.1 copy-start.10
  75.5 12.9 %copy-start.38 = (bf16[1,2,128,128]{3,2,1,0:T(8,128)(2,1)S(1)}, bf16[1,2,128,128]{3,2,1,0:T(8,128)(2,1)}, u32[]{:S(2)}) copy-start(bf16[1,2,128,128]{3,2,1,0:T(8,128)(2,1)} %param.23) | copy-start | bytes 196612
  79.0 16.9 %all-to-all-start.3 = ((bf16[64,4,1024]{2,1,0:T(4,128)(2,1)}), bf16[64,4,1024]{2,1,0:T(4,128)(2,1)}, u32[]{:S(2)}, u32[]{:S(2)}) async-start(bf16[64,4,1024]{2,1,0:T(4,128)(2,1)} %copy.124), calls=%async_computation.3 | async-start | bytes 1048576 | tf_op jit(solution)/shard_map/all_to_all | solution.py:179
  84.2 143.3 %reduce-scatter.5.cloned.1.call-start = ((), (), s32[]{:S(2)}) async-start(), calls=%async_computation.10 | async-start | bytes 540672 | tf_op jit(solution)/shard_map/reduce_scatter | solution.py:249
  88.4 1.4 copy-start.30
  90.1 0.8 copy-start.18
  99.3 1.0 copy-start.5
  99.3 1.2 copy-start.42
  100.3 3.2 copy-start.2
  117.8 1.8 copy-start.32
  123.6 1.6 copy-start.9
  125.1 2.7 copy-start.4
  125.1 2.7 copy-start.6
  127.8 2.8 copy-start.23
  127.8 1.6 copy-start.15
  128.9 1.7 copy-start.25
  130.6 171.6 %reduce-scatter.11.cloned.1.call-start = ((), (), s32[]{:S(2)}) async-start(), calls=%async_computation.13 | async-start | bytes 1081344 | tf_op jit(solution)/shard_map/reduce_scatter | solution.py:258
  134.9 2.5 copy-start.36
  140.0 9.0 %copy-start.20 = (bf16[256,1024]{1,0:T(8,128)(2,1)S(1)}, bf16[256,1024]{1,0:T(8,128)(2,1)}, u32[]{:S(2)}) copy-start(bf16[256,1024]{1,0:T(8,128)(2,1)} %get-tuple-element.33) | copy-start | bytes 1572868
  144.3 36.3 %all-to-all-start.4 = ((bf16[2,128,1024]{2,0,1:T(2,128)(2,1)}), bf16[2,128,1024]{2,0,1:T(2,128)(2,1)}, u32[]{:S(2)}, u32[]{:S(2)}) async-start(bf16[2,128,1024]{2,0,1:T(2,128)(2,1)} %copy.137), calls=%async_computation.4 | async-start | bytes 1048576 | tf_op jit(solution)/shard_map/all_to_all | solution.py:227
  148.8 242.6 %reduce-scatter.9.cloned.1.call-start = ((), (), s32[]{:S(2)}) async-start(), calls=%async_computation.12 | async-start | bytes 1081344 | tf_op jit(solution)/shard_map/reduce_scatter | solution.py:255
  155.6 3.0 copy-start.16
  155.6 3.0 copy-start.33
  160.1 4.4 copy-start.22
  160.1 4.4 copy-start.26
  169.9 5.4 %copy-start.28 = (bf16[1,2048,256]{2,1,0:T(8,128)(2,1)S(1)}, bf16[1,2048,256]{2,1,0:T(8,128)(2,1)}, u32[]{:S(2)}) copy-start(bf16[1,2048,256]{2,1,0:T(8,128)(2,1)} %param.27) | copy-start | bytes 3145732
  180.6 4.9 copy-start.27
  184.5 1.0 copy-start.12
  187.2 18.7 %all-to-all-start.5 = ((bf16[64,4,1024]{2,1,0:T(4,128)(2,1)}), bf16[64,4,1024]{2,1,0:T(4,128)(2,1)}, u32[]{:S(2)}, u32[]{:S(2)}) async-start(bf16[64,4,1024]{2,1,0:T(4,128)(2,1)} %copy.141), calls=%async_computation.5 | async-start | bytes 1048576 | tf_op jit(solution)/shard_map/all_to_all | solution.py:234
  194.3 2.8 copy-start.19
  194.3 286.3 %reduce-scatter.7.cloned.1.call-start = ((), (), s32[]{:S(2)}) async-start(), calls=%async_computation.11 | async-start | bytes 1081344 | tf_op jit(solution)/shard_map/reduce_scatter | solution.py:252
  197.1 12.0 %copy-start.8 = (f32[1,256,1024]{2,1,0:T(8,128)S(1)}, f32[1,256,1024]{2,1,0:T(8,128)}, u32[]{:S(2)}) copy-start(f32[1,256,1024]{2,1,0:T(8,128)} %copy-done.7) | copy-start | bytes 3145732
  199.3 14.9 %collective-permute-start = (bf16[1,256,1024]{2,1,0:T(8,128)(2,1)}, bf16[1,256,1024]{2,1,0:T(8,128)(2,1)}, u32[]{:S(2)}, u32[]{:S(2)}) collective-permute-start(bf16[1,256,1024]{2,1,0:T(8,128)(2,1)} %fusion.48), channel_id=1, source_target_pairs={{0,32},{32,64},{64,96},{96,128},{128,160},{160,192},{192,224},{1,3... | collective-permute-start | bytes 1572872 | tf_op jit(solution)/shard_map/ppermute | solution.py:19
  209.1 1.8 copy-start.24
  209.1 1.8 copy-start.29
  210.9 1.9 copy-start.11
  210.9 1.9 copy-start.13
  211.4 16.1 %collective-permute-start.1 = (bf16[1,256,1024]{2,1,0:T(8,128)(2,1)S(1)}, bf16[1,256,1024]{2,1,0:T(8,128)(2,1)S(1)}, u32[]{:S(2)}, u32[]{:S(2)}) collective-permute-start(bf16[1,256,1024]{2,1,0:T(8,128)(2,1)S(1)} %bitcast.310), channel_id=1, source_target_pairs={{32,0},{64,32},{96,64},{128,96},{160,128},{192,160},{224,192},{33,... | collective-permute-start | bytes 1572872 | tf_op jit(solution)/shard_map/ppermute | solution.py:19
Sparse Core Ops, SparseCore 0:
  130.7 81.9 reduce-scatter.4
  217.0 85.1 reduce-scatter.10
  306.6 84.7 reduce-scatter.8
  395.5 84.9 reduce-scatter.6
where the time goes:
time: 493 us; the launch traced here: 490 us
  waiting for transfers between devices  276 us (56%)
  local copies, waits for them, and re-layouts  83.8 us (17%)
  matrix products  47.3 us (10%)
  starting transfers between devices  46.5 us (9%)
  other arithmetic  22.1 us (4%)
  between operations  14.4 us (3%)
    reduce_scatter x1, waiting for transfers between devices, shards(): lax.psum_scatter(term_up.astype(jnp.bfloat16), 'seq', scatter_dimension=0...  89.2 us
    reduce_scatter x1, waiting for transfers between devices, shards(): lax.psum_scatter(term_act.astype(jnp.bfloat16), 'seq', scatter_dimension=...  89.1 us
    reduce_scatter x1, waiting for transfers between devices, shards(): lax.psum_scatter(term_down.astype(jnp.bfloat16), 'seq', scatter_dimension...  74.7 us
    dot_general x7, matrix products, block_apply(): jnp.einsum('ynq,nqd->ynd', value_array.reshape(item_count, block_list, -1...  18.9 us
    reshape x7, local copies, waits for them, and re-layouts, block_apply(): return final_output.reshape(item_count, -1)  18.5 us
    ppermute x2, waiting for transfers between devices, from_behind(): return lax.ppermute(array, axis, pairs)  13.3 us
  transfers between devices with their start and end apart: 12, of which 7 were waited for; matrix products, arithmetic and copies ran while one was open for 21% of the time, Pallas kernels for 0%

commit v1 on v0

v1 whole, which is shorter than its diff:
```python
import math

import jax
import jax.numpy as jnp
from jax import lax
from jax.experimental import pallas as pl
from jax.experimental.pallas import tpu as pltpu
from jax.sharding import PartitionSpec as P

NB = 4
NI = 64
NJ = 128
D = 1024
FF = 2048
T = 256
HB = FF // NB
DB = D // NB
EPS = 1e-06
KGRAD = 1.0 / math.sqrt(NI * NJ)
GR = 224

F32 = jnp.float32
BF = jnp.bfloat16


def mm(a, b):
    return lax.dot_general(a, b, (((1,), (0,)), ((), ())), preferred_element_type=F32)


def mm_nt(a, b):
    return lax.dot_general(a, b, (((1,), (1,)), ((), ())), preferred_element_type=F32)


def mm_tn(a, b):
    return lax.dot_general(a, b, (((0,), (0,)), ((), ())), preferred_element_type=F32)


def iota(shape, dim):
    return lax.broadcasted_iota(jnp.int32, shape, dim)


def onehot(cond):
    return jnp.where(cond, 1.0, 0.0).astype(BF)


def r_half(r):
    return (r >> 2) & 1


def r_col(r):
    return ((r >> 3) << 2) + (r & 3)


def call(kernel, outs, *args, **kwargs):
    return pl.pallas_call(
        kernel,
        out_shape=[jax.ShapeDtypeStruct(s, d) for s, d in outs],
        compiler_params=pltpu.CompilerParams(vmem_limit_bytes=56 << 20),
        **kwargs,
    )(*args)


def rms(v):
    return lax.rsqrt(jnp.mean(v * v, axis=-1, keepdims=True) + EPS)


def first_rows(first):
    w = first.reshape(T, NJ)
    r, t = iota((T, T), 0), iota((T, T), 1)
    pick = onehot(t == (r_half(r) << 7) + r_col(r))
    return mm(pick, w).astype(BF)


def k_front(x_ref, gain_ref, first_ref, a1_ref):
    rows = first_rows(first_ref[...])
    r, c = iota((T, T), 0), iota((T, T), 1)
    m1 = jnp.where((c >> 7) == r_half(r), jnp.concatenate([rows, rows], axis=1), 0).astype(BF)
    x = x_ref[...].astype(F32)
    n1 = (x * rms(x) * gain_ref[...]).astype(BF)
    a1_ref[...] = mm(m1, n1).astype(BF)


def k_prep(first_ref, second_ref, third_ref, fourth_ref, m1t, m2, m2t, m3, m3t, m4, m4t):
    r, c = iota((T, T), 0), iota((T, T), 1)

    rows = first_rows(first_ref[...])
    e1t = onehot((iota((T, NJ), 0) & 127) == iota((T, NJ), 1))
    m1t[...] = jnp.where((r >> 7) == r_half(c), mm_nt(e1t, rows), 0.0).astype(BF)

    q = onehot(c == ((r & 3) << 6) + (r >> 2))
    e2 = onehot(iota((NI, T), 0) == (iota((NI, T), 1) >> 2))
    e2t = onehot((iota((T, NI), 0) >> 2) == iota((T, NI), 1))
    same = (r & 3) == (c & 3)
    for src, out, out_t in ((second_ref, m2, m2t), (third_ref, m3, m3t)):
        w = mm(q, src[...].reshape(T, NI)).astype(BF)
        out[...] = jnp.where(same, mm(w, e2), 0.0).astype(BF)
        out_t[...] = jnp.where(same, mm_nt(e2t, w), 0.0).astype(BF)

    w4 = fourth_ref[...].reshape(T, NJ)
    e4 = onehot(iota((NJ, T), 0) == r_col(iota((NJ, T), 1)))
    e4t = onehot(r_col(iota((T, NJ), 0)) == iota((T, NJ), 1))
    m4[...] = jnp.where((r >> 7) == r_half(c), mm(w4, e4), 0.0).astype(BF)
    m4t[...] = jnp.where(r_half(r) == (c >> 7), mm_nt(e4t, w4), 0.0).astype(BF)


def k_mid(recv_ref, spec_ref, m2_ref, m3_ref, b1_ref):
    a2 = mm(m2_ref[...], recv_ref[...])
    filt = (a2 * spec_ref[...].astype(F32)).astype(BF)
    b1_ref[...] = mm(m3_ref[...], filt).astype(BF)


def k_mid_keep(recv_ref, spec_ref, m2_ref, m3_ref, b1_ref, a2_ref):
    a2 = mm(m2_ref[...], recv_ref[...])
    a2_ref[...] = a2
    filt = (a2 * spec_ref[...].astype(F32)).astype(BF)
    b1_ref[...] = mm(m3_ref[...], filt).astype(BF)


def k_mid_back(recv_ref, a2_ref, spec_ref, m3t_ref, m2t_ref, da1_ref, sg_ref):
    dfilt = mm(m3t_ref[...], recv_ref[...])
    da2 = (dfilt * spec_ref[...].astype(F32)).astype(BF)
    da1_ref[...] = mm(m2t_ref[...], da2).astype(BF)
    sg_ref[...] = (dfilt * a2_ref[...]).astype(BF)


def cols(b, n):
    return slice(b * n, (b + 1) * n)


def hcols(b, k):
    return slice(k * HB + b * NJ, k * HB + (b + 1) * NJ)


def k_ahead(x_ref, g_ref, gain_ref, mix_ref, down_ref, n1_ref, gate_ref, dhid_ref):
    x = x_ref[...].astype(F32)
    n1_ref[...] = (x * rms(x) * gain_ref[...]).astype(BF)
    for b in range(NB):
        gate_ref[:, cols(b, DB)] = mm(n1_ref[:, cols(b, DB)], mix_ref[cols(b, DB), :])
        dhs = mm_nt(g_ref[:, cols(b, DB)], down_ref[cols(b, HB), :]).astype(BF)
        for k in range(NB):
            dhid_ref[:, hcols(b, k)] = dhs[:, cols(k, NJ)]


def k_tail_back(
    x_ref, recv_ref, g_ref, gate_ref, dhid_ref, m4_ref, m4t_ref, gain_ref, up_ref, act_ref,
    db1_ref, dy1_ref, dgate_ref, n2_ref, hs_ref, dup_ref, dact_ref,
    y1_ref, dn2_ref,
):
    b2 = mm(m4_ref[...], recv_ref[...])
    y1_ref[...] = (x_ref[...].astype(F32) + b2 * gate_ref[...]).astype(BF).astype(F32)
    y1 = y1_ref[...]
    r2 = rms(y1)
    n2_ref[...] = (y1 * r2 * gain_ref[...]).astype(BF)
    for b in range(NB):
        n2 = n2_ref[:, cols(b, DB)]
        up = mm(n2, up_ref[cols(b, DB), :])
        act = mm(n2, act_ref[cols(b, DB), :])
        sg = jax.nn.sigmoid(act)
        silu = act * sg
        hid = (silu * up).astype(BF)
        for k in range(NB):
            hs_ref[:, hcols(b, k)] = hid[:, cols(k, NJ)]
        dhid = dhid_ref[:, cols(b, HB)].astype(F32)
        dup = (dhid * silu).astype(BF)
        dact = (dhid * up * sg * (1.0 + act * (1.0 - sg))).astype(BF)
        dup_ref[:, cols(b, HB)] = dup
        dact_ref[:, cols(b, HB)] = dact
        dn2_ref[:, cols(b, DB)] = mm_nt(dup, up_ref[cols(b, DB), :]) + mm_nt(
            dact, act_ref[cols(b, DB), :]
        )
    s = gain_ref[...] * dn2_ref[...]
    y1 = y1_ref[...]
    back = r2 * s - y1 * (r2 * r2 * r2) * jnp.mean(s * y1, axis=-1, keepdims=True)
    dy1 = (g_ref[...].astype(F32) + back).astype(BF)
    dy1_ref[...] = dy1
    dyw = dy1.astype(F32)
    db2 = (dyw * gate_ref[...]).astype(BF)
    db1_ref[...] = mm(m4t_ref[...], db2).astype(BF)
    dgate_ref[...] = (dyw * mm(m4_ref[...], recv_ref[...])).astype(BF)


def k_grads(n1_ref, dgate_ref, n2_ref, dup_ref, dact_ref, hs_ref, g_ref, mix_ref, o_ref, dn1_ref):
    for b in range(NB):
        d = slice(8 * b, 8 * b + 8)
        dgate = dgate_ref[:, cols(b, DB)]
        dn1_ref[:, cols(b, DB)] = mm_nt(dgate, mix_ref[cols(b, DB), :])
        mix = mm_tn(n1_ref[:, cols(b, DB)], dgate) * KGRAD
        o_ref[d, 0:32, :] = mix.astype(BF).reshape(8, 32, DB)
        n2 = n2_ref[:, cols(b, DB)]
        up = (mm_tn(n2, dup_ref[:, cols(b, HB)]) * KGRAD).astype(BF).reshape(8, 32, HB)
        o_ref[d, 32:64, :] = up[:, :, :DB]
        o_ref[d, 64:96, :] = up[:, :, DB:]
        act = (mm_tn(n2, dact_ref[:, cols(b, HB)]) * KGRAD).astype(BF).reshape(8, 32, HB)
        o_ref[d, 96:128, :] = act[:, :, :DB]
        o_ref[d, 128:160, :] = act[:, :, DB:]
        down = mm_tn(hs_ref[:, cols(b, HB)], g_ref[:, cols(b, DB)]) * KGRAD
        o_ref[d, 160:224, :] = down.astype(BF).reshape(8, 64, DB)


def k_tail(x_ref, recv_ref, m4_ref, gain1_ref, gain2_ref, mix_ref, up_ref, act_ref, down_ref,
           out_ref, y1_ref, n_ref, hs_ref):
    x = x_ref[...].astype(F32)
    n_ref[...] = (x * rms(x) * gain1_ref[...]).astype(BF)
    b2 = mm(m4_ref[...], recv_ref[...])
    for b in range(NB):
        gate = mm(n_ref[:, cols(b, DB)], mix_ref[cols(b, DB), :])
        y1_ref[:, cols(b, DB)] = (
            (x_ref[:, cols(b, DB)].astype(F32) + b2[:, cols(b, DB)] * gate).astype(BF).astype(F32)
        )
    y1 = y1_ref[...]
    n_ref[...] = (y1 * rms(y1) * gain2_ref[...]).astype(BF)
    for b in range(NB):
        n2 = n_ref[:, cols(b, DB)]
        up = mm(n2, up_ref[cols(b, DB), :])
        act = mm(n2, act_ref[cols(b, DB), :])
        hid = (act * jax.nn.sigmoid(act) * up).astype(BF)
        for k in range(NB):
            hs_ref[:, hcols(b, k)] = hid[:, cols(k, NJ)]
    for b in range(NB):
        out_ref[:, cols(b, DB)] = (
            y1_ref[:, cols(b, DB)] + mm(hs_ref[:, cols(b, HB)], down_ref[cols(b, HB), :])
        ).astype(BF)


def k_end(x_ref, recv_ref, m1t_ref, dn1_ref, dy1_ref, gain_ref, dx_ref):
    x = x_ref[...].astype(F32)
    r1 = rms(x)
    s = gain_ref[...] * (mm(m1t_ref[...], recv_ref[...]) + dn1_ref[...])
    back = r1 * s - x * (r1 * r1 * r1) * jnp.mean(s * x, axis=-1, keepdims=True)
    dx_ref[...] = (dy1_ref[...].astype(F32) + back).astype(BF)


def k_sum(recv_ref, mix_ref, up_ref, act_ref, down_ref):
    total = recv_ref[0].astype(F32)
    for s in range(1, recv_ref.shape[0]):
        total = total + recv_ref[s].astype(F32)
    total = total.astype(BF)
    mix_ref[...] = total[0:32]
    up_ref[:, :DB] = total[32:64]
    up_ref[:, DB:] = total[64:96]
    act_ref[:, :DB] = total[96:128]
    act_ref[:, DB:] = total[128:160]
    down_ref[...] = total[160:224]


def swap(v):
    return lax.all_to_all(v, "seq", split_axis=0, concat_axis=0, tiled=True)


def shift(v, by):
    n = lax.axis_size("section")
    return lax.ppermute(v, "section", [(i, i + by) for i in range(n) if 0 <= i + by < n])


def shards(xa, xb, g, gain1, gain2, first, second, spec, third, fourth, mix, up, act, down):
    xa, xb, g = xa[0], xb[0], g[0]
    first, second, third, fourth = first[0], second[0], third[0], fourth[0]
    mix, up, act, down = mix[0], up[0], act[0], down[0]
    spec = spec[0].reshape(T, D)
    td, tt = (T, D), (T, T)

    (a1b,) = call(k_front, [(td, BF)], xb, gain1, first)
    rb = swap(a1b)
    (a1a,) = call(k_front, [(td, BF)], xa, gain1, first)
    ra = swap(a1a)
    m1t, m2, m2t, m3, m3t, m4, m4t = call(k_prep, [(tt, BF)] * 7, first, second, third, fourth)
    n1b, gateb, dhid = call(
        k_ahead, [(td, BF), (td, F32), ((T, FF), BF)], xb, g, gain1, mix, down
    )
    b1b, a2b = call(k_mid_keep, [(td, BF), (td, F32)], rb, spec, m2, m3)
    qb = swap(b1b)
    (b1a,) = call(k_mid, [(td, BF)], ra, spec, m2, m3)
    qa = swap(b1a)
    db1, dy1, dgate, n2, hs, dup, dact = call(
        k_tail_back,
        [(td, BF)] * 4 + [((T, FF), BF)] * 3,
        xb, qb, g, gateb, dhid, m4, m4t, gain2, up, act,
        scratch_shapes=[pltpu.VMEM(td, F32), pltpu.VMEM(td, F32)],
    )
    rc = swap(db1)
    grads, dn1 = call(
        k_grads, [((32, GR, DB), BF), (td, F32)], n1b, dgate, n2, dup, dact, hs, g, mix
    )
    gr = swap(grads)
    (outa,) = call(
        k_tail, [(td, BF)], xa, qa, m4, gain1, gain2, mix, up, act, down,
        scratch_shapes=[pltpu.VMEM(td, F32), pltpu.VMEM(td, BF), pltpu.VMEM((T, FF), BF)],
    )
    next_input = shift(outa, 1)
    da1, sgrad = call(k_mid_back, [(td, BF), (td, BF)], rc, a2b, spec, m3t, m2t)
    rd = swap(da1)
    (dx,) = call(k_end, [(td, BF)], xb, rd, m1t, dn1, dy1, gain1)
    upstream = shift(dx, -1)
    gm, gu, ga, gd = call(
        k_sum,
        [((32, DB), BF), ((32, HB), BF), ((32, HB), BF), ((64, DB), BF)],
        gr,
    )
    return (
        next_input[None],
        upstream[None],
        sgrad.reshape(1, NI, 4, D),
        gm[None],
        gu[None],
        ga[None],
        gd[None],
    )


def solution(mesh):
    in_specs = (
        P("section", "seq", None),
        P("section", "seq", None),
        P("section", "seq", None),
        P("section", None),
        P("section", None),
        P("section", "seq", None, None),
        P("section", "seq", None, None),
        P("section", None, "seq", None),
        P("section", "seq", None, None),
        P("section", "seq", None, None),
        P("section", None, None),
        P("section", None, None),
        P("section", None, None),
        P("section", None, None),
    )
    out_specs = (
        P("section", "seq", None),
        P("section", "seq", None),
        P("section", None, "seq", None),
        P("section", "seq", None),
        P("section", "seq", None),
        P("section", "seq", None),
        P("section", "seq", None),
    )
    return jax.shard_map(shards, mesh=mesh, in_specs=in_specs, out_specs=out_specs, check_vma=False)
```

time: 493 us -> 163 us (0.33)
  waiting for transfers between devices: 276 us -> 72.1 us
  local copies, waits for them, and re-layouts: 83.8 us -> 6.13 us
  matrix products: 47.3 us -> 0 us
  Pallas kernels: 0 us -> 43.1 us
  other arithmetic: 22.1 us -> 0 us
  between operations: 14.4 us -> 0.75 us
  starting transfers between devices: 46.5 us -> 39.6 us
    reduce_scatter x4 -> x0, waiting for transfers between devices: 253 us -> none  [the longest x1 89.2 us: shards(): lax.psum_scatter(term_up.astype(jnp.bfloat16), 'seq', scatter_dimension=0...]
    all_to_all x6 -> x7, waiting for transfers between devices: 9.25 us -> 58.6 us  [swap(): return lax.all_to_all(v, 'seq', split_axis=0, concat_axis=0, tiled=True)]
    dot_general x26 -> x0, matrix products: 47.3 us -> none  [the longest x7 18.9 us: block_apply(): jnp.einsum('ynq,nqd->ynd', value_array.reshape(item_count, block_list, -1...]
    pallas_call x0 -> x12, Pallas kernels: none -> 43.1 us  [call(): pl.pallas_call(kernel, out_shape=[jax.ShapeDtypeStruct(s, d) for s, d in...]
    reshape x11 -> x1, local copies, waits for them, and re-layouts: 25.7 us -> 0.99 us  [shards(): sgrad.reshape(1, NI, 4, D)]
    all_to_all x11 -> x0, local copies, waits for them, and re-layouts: 20.5 us -> none  [the longest x2 4.23 us: shards(): lax.all_to_all(folded_back, 'seq', split_axis=1, concat_axis=0, tiled=True)]
    convert_element_type x10 -> x0, local copies, waits for them, and re-layouts: 18.3 us -> none  [the longest x2 6.01 us: shards(): d_hidden = shuffle(d_shuffled, block_list).astype(jnp.float32)]
    transpose x2 -> x0, other arithmetic: 8.68 us -> none  [shuffle(): return value_array.reshape(item_count, block_list, block_list, -1).transp...]
  transfers between devices with their start and end apart: 12 -> 9, of which waited for: 7 -> 9; matrix products, arithmetic and copies ran while one was open for 21% -> 2% of each run, Pallas kernels for 0% -> 22%
where the time goes in v1:
time: 163 us; the launch traced here: 162 us
  waiting for transfers between devices  72.1 us (44%)
  Pallas kernels  43.1 us (26%)
  starting transfers between devices  39.6 us (24%)
  local copies, waits for them, and re-layouts  6.13 us (4%)
    all_to_all x7, waiting for transfers between devices, swap(): return lax.all_to_all(v, 'seq', split_axis=0, concat_axis=0, tiled=True)  58.6 us
    pallas_call x12, Pallas kernels, call(): pl.pallas_call(kernel, out_shape=[jax.ShapeDtypeStruct(s, d) for s, d in...  43.1 us
    all_to_all x7, starting transfers between devices, swap(): return lax.all_to_all(v, 'seq', split_axis=0, concat_axis=0, tiled=True)  34.8 us
    ppermute x2, waiting for transfers between devices, shift(): lax.ppermute(v, 'section', [(i, i + by) for i in range(n) if 0 <= i + by...  13.5 us
    ppermute x2, starting transfers between devices, shift(): lax.ppermute(v, 'section', [(i, i + by) for i in range(n) if 0 <= i + by...  4.83 us
  transfers between devices with their start and end apart: 9, of which 9 were waited for; matrix products, arithmetic and copies ran while one was open for 2% of the time, Pallas kernels for 22%

profile of v1, /device:TPU:1, one launch (start us, length us, event | category | flops | bytes accessed | tf_op | source)
XLA Modules:
  0.0 161.6 jit_solution(11138015772829507470)
XLA Ops:
  0.6 2.4 %shard_map.193 = bf16[256,1024]{1,0:T(8,128)(2,1)} custom-call(bf16[256,1024]{1,0:T(8,128)(2,1)} %bitcast.29, f32[1,1024]{1,0:T(1,128)} %gain_ref.9, bf16[2,128,128]{2,1,0:T(8,128)(2,1)} %bitcast.56), custom_call_target="tpu_custom_call" | custom-call | tf_op jit(solution)/shard_map/pallas_call | solution.py:55
  3.0 8.6 %all-to-all-start.2 = ((bf16[32,8,1024]{2,1,0:T(8,128)(2,1)}), bf16[32,8,1024]{2,1,0:T(8,128)(2,1)S(1)}, u32[]{:S(2)}, u32[]{:S(2)}) async-start(bf16[32,8,1024]{2,1,0:T(8,128)(2,1)} %bitcast.51), calls=%async_computation.2 | async-start | bytes 1048576 | tf_op jit(solution)/shard_map/all_to_all | solution.py:247
  11.6 2.0 %reshape_squeeze.3.spec_ref = bf16[256,1024]{1,0:T(8,128)(2,1)} reshape(bf16[1,64,4,1024]{3,2,1,0:T(4,128)(2,1)} %param.21) | data formatting | bytes 1048576 | tf_op jit(solution)/shard_map/reshape;squeeze | solution.py:259
  13.5 2.4 %shard_map.190 = (bf16[256,256]{1,0:T(8,128)(2,1)}, bf16[256,256]{1,0:T(8,128)(2,1)}, bf16[256,256]{1,0:T(8,128)(2,1)}, bf16[256,256]{1,0:T(8,128)(2,1)}, bf16[2...) custom-call(bf16[2,128,128]{2,1,0:T(8,128)(2,1)} %bitcast.57, bf16[4,64,64]{2,1,0:T(8,128)(2,1)} %bitcast.64, ...), custom_call_target="tpu_custom_call" | custom-call | tf_op jit(solution)/shard_map/pallas_call | solution.py:55
  16.0 7.2 %all-to-all-done.2 = bf16[32,8,1024]{2,1,0:T(8,128)(2,1)S(1)} async-done(((bf16[32,8,1024]{2,1,0:T(8,128)(2,1)}), bf16[32,8,1024]{2,1,0:T(8,128)(2,1)S(1)}, u32[]{:S(2)}, u32[]{:S(2)}) %all-to-all-start.2) | async-done | bytes 524320 | tf_op jit(solution)/shard_map/all_to_all | solution.py:247
  23.2 0.0 copy-start.3
  23.2 0.8 copy-done.3
  24.0 2.7 %shard_map.194 = (bf16[256,1024]{1,0:T(8,128)(2,1)}, f32[256,1024]{1,0:T(8,128)}) custom-call(bf16[256,1024]{1,0:T(8,128)(2,1)} %bitcast.50, bf16[256,1024]{1,0:T(8,128)(2,1)} %reshape_squeeze.3.spec_ref, bf16[256,256]{1,0:T(8,128)(2,1)} %get-tuple-element.34.m2_ref, bf16[256,256]{1,0:T(8,128)(2,1)} %get-tuple-element.35.m3_ref), custom_call_target="tpu_custom_call" | custom-call | tf_op jit(solution)/shard_map/pallas_call | solution.py:55
  26.7 3.7 %all-to-all-start.3 = ((bf16[32,8,1024]{2,1,0:T(8,128)(2,1)}), bf16[32,8,1024]{2,1,0:T(8,128)(2,1)S(1)}, u32[]{:S(2)}, u32[]{:S(2)}) async-start(bf16[32,8,1024]{2,1,0:T(8,128)(2,1)} %bitcast.63), calls=%async_computation.3 | async-start | bytes 1048576 | tf_op jit(solution)/shard_map/all_to_all | solution.py:247
  30.4 2.4 %shard_map.189 = bf16[256,1024]{1,0:T(8,128)(2,1)} custom-call(bf16[256,1024]{1,0:T(8,128)(2,1)} %bitcast.53, f32[1,1024]{1,0:T(1,128)} %gain_ref.9, bf16[2,128,128]{2,1,0:T(8,128)(2,1)} %bitcast.58), custom_call_target="tpu_custom_call" | custom-call | tf_op jit(solution)/shard_map/pallas_call | solution.py:55
  32.7 9.2 %all-to-all-done.3 = bf16[32,8,1024]{2,1,0:T(8,128)(2,1)S(1)} async-done(((bf16[32,8,1024]{2,1,0:T(8,128)(2,1)}), bf16[32,8,1024]{2,1,0:T(8,128)(2,1)S(1)}, u32[]{:S(2)}, u32[]{:S(2)}) %all-to-all-start.3) | async-done | bytes 524320 | tf_op jit(solution)/shard_map/all_to_all | solution.py:247
  41.9 0.0 copy-start.2
  41.9 3.7 %all-to-all-start = ((bf16[32,8,1024]{2,1,0:T(8,128)(2,1)}), bf16[32,8,1024]{2,1,0:T(8,128)(2,1)S(1)}, u32[]{:S(2)}, u32[]{:S(2)}) async-start(bf16[32,8,1024]{2,1,0:T(8,128)(2,1)} %bitcast.49), calls=%async_computation | async-start | bytes 1048576 | tf_op jit(solution)/shard_map/all_to_all | solution.py:247
  45.6 3.6 %shard_map.195 = (bf16[256,1024]{1,0:T(8,128)(2,1)}, f32[256,1024]{1,0:T(8,128)}, bf16[256,2048]{1,0:T(8,128)(2,1)}) custom-call(bf16[256,1024]{1,0:T(8,128)(2,1)} %bitcast.30, bf16[256,1024]{1,0:T(8,128)(2,1)} %bitcast.33, f32[1,1024]{1,0:T(1,128)} %gain_ref.9, bf16[1024,256]{1,0:T(8,128)(2,1)} %bitcast.36, bf16[2048,256]{1,0:T(8,128)(2,1)} %bitcast.43), custom_call_target="tpu_custom_call" | custom-call | tf_op jit(solution)/shard_map/pallas_call | solution.py:55
  49.2 0.0 copy-done.2
  49.2 7.3 %shard_map.196 = (bf16[256,1024]{1,0:T(8,128)(2,1)}, bf16[256,1024]{1,0:T(8,128)(2,1)}, bf16[256,1024]{1,0:T(8,128)(2,1)}, bf16[256,1024]{1,0:T(8,128)(2,1)}, bf...) custom-call(bf16[256,1024]{1,0:T(8,128)(2,1)} %bitcast.31, ...), custom_call_target="tpu_custom_call" | custom-call | tf_op jit(solution)/shard_map/pallas_call | solution.py:55
  56.5 0.7 all-to-all-done
  57.1 0.0 copy-start.1
  57.1 6.7 %all-to-all-start.4 = ((bf16[32,8,1024]{2,1,0:T(8,128)(2,1)}), bf16[32,8,1024]{2,1,0:T(8,128)(2,1)S(1)}, u32[]{:S(2)}, u32[]{:S(2)}) async-start(bf16[32,8,1024]{2,1,0:T(8,128)(2,1)} %bitcast.62), calls=%async_computation.4 | async-start | bytes 1048576 | tf_op jit(solution)/shard_map/all_to_all | solution.py:247
  63.8 0.0 copy-done.1
  63.8 2.6 %shard_map.191 = bf16[256,1024]{1,0:T(8,128)(2,1)} custom-call(bf16[256,1024]{1,0:T(8,128)(2,1)} %bitcast.46, bf16[256,1024]{1,0:T(8,128)(2,1)} %reshape_squeeze.3.spec_ref, bf16[256,256]{1,0:T(8,128)(2,1)} %get-tuple-element.34.m2_ref, bf16[256,256]{1,0:T(8,128)(2,1)} %get-tuple-element.35.m3_ref), custom_call_target="tpu_custom_call" | custom-call | tf_op jit(solution)/shard_map/pallas_call | solution.py:55
  66.4 9.0 %all-to-all-done.4 = bf16[32,8,1024]{2,1,0:T(8,128)(2,1)S(1)} async-done(((bf16[32,8,1024]{2,1,0:T(8,128)(2,1)}), bf16[32,8,1024]{2,1,0:T(8,128)(2,1)S(1)}, u32[]{:S(2)}, u32[]{:S(2)}) %all-to-all-start.4) | async-done | bytes 524320 | tf_op jit(solution)/shard_map/all_to_all | solution.py:247
  75.4 0.0 copy-start.4
  75.4 3.7 %all-to-all-start.1 = ((bf16[32,8,1024]{2,1,0:T(8,128)(2,1)}), bf16[32,8,1024]{2,1,0:T(8,128)(2,1)S(1)}, u32[]{:S(2)}, u32[]{:S(2)}) async-start(bf16[32,8,1024]{2,1,0:T(8,128)(2,1)} %bitcast.48), calls=%async_computation.1 | async-start | bytes 1048576 | tf_op jit(solution)/shard_map/all_to_all | solution.py:247
  79.1 0.0 copy-done.4
  79.1 2.9 %shard_map.197 = (bf16[256,1024]{1,0:T(8,128)(2,1)}, bf16[256,1024]{1,0:T(8,128)(2,1)}) custom-call(bf16[256,1024]{1,0:T(8,128)(2,1)} %bitcast.52, f32[256,1024]{1,0:T(8,128)} %get-tuple-element.42.a2_ref, bf16[256,1024]{1,0:T(8,128)(2,1)} %reshape_squeeze.3.spec_ref, bf16[256,256]{1,0:T(8,128)(2,1)} %get-tuple-element.43.m3t_ref, ...), custom_call_target="tpu_custom_call" | custom-call | tf_op jit(solution)/shard_map/pallas_call | solution.py:55
  82.0 8.6 %all-to-all-done.1 = bf16[32,8,1024]{2,1,0:T(8,128)(2,1)S(1)} async-done(((bf16[32,8,1024]{2,1,0:T(8,128)(2,1)}), bf16[32,8,1024]{2,1,0:T(8,128)(2,1)S(1)}, u32[]{:S(2)}, u32[]{:S(2)}) %all-to-all-start.1) | async-done | bytes 524320 | tf_op jit(solution)/shard_map/all_to_all | solution.py:247
  90.6 0.0 copy-start.5
  90.6 3.7 %all-to-all-start.5 = ((bf16[32,8,1024]{2,1,0:T(8,128)(2,1)}), bf16[32,8,1024]{2,1,0:T(8,128)(2,1)S(1)}, u32[]{:S(2)}, u32[]{:S(2)}) async-start(bf16[32,8,1024]{2,1,0:T(8,128)(2,1)} %bitcast.60), calls=%async_computation.5 | async-start | bytes 1048576 | tf_op jit(solution)/shard_map/all_to_all | solution.py:247
  94.3 5.8 %shard_map.198 = (bf16[32,224,256]{2,1,0:T(8,128)(2,1)}, f32[256,1024]{1,0:T(8,128)}) custom-call(bf16[256,1024]{1,0:T(8,128)(2,1)} %get-tuple-element.47.n1_ref, bf16[256,1024]{1,0:T(8,128)(2,1)} %get-tuple-element.48.dgate_ref, bf16[256,1024]{1,0:T(8,128)(2,1)} %get-tuple-element.49.n2_ref, bf16[256,2048]{1,0:T(8,128)(2,1)} %get-tuple-element.50.dup_ref, ...), custom_call_target="tpu_custom_call" | custom-call | tf_op jit(solution)/shard_map/pallas_call | solution.py:55
  100.1 5.7 %all-to-all-done.5 = bf16[32,8,1024]{2,1,0:T(8,128)(2,1)S(1)} async-done(((bf16[32,8,1024]{2,1,0:T(8,128)(2,1)}), bf16[32,8,1024]{2,1,0:T(8,128)(2,1)S(1)}, u32[]{:S(2)}, u32[]{:S(2)}) %all-to-all-start.5) | async-done | bytes 524320 | tf_op jit(solution)/shard_map/all_to_all | solution.py:247
  105.9 0.0 copy-start
  105.9 0.0 copy-done.5
  105.9 0.8 copy-done
  106.7 4.8 %all-to-all-start.6 = ((bf16[32,224,256]{2,1,0:T(8,128)(2,1)}), bf16[32,224,256]{2,1,0:T(8,128)(2,1)}, u32[]{:S(2)}, u32[]{:S(2)}) async-start(bf16[32,224,256]{2,1,0:T(8,128)(2,1)} %get-tuple-element.56), calls=%async_computation.6 | async-start | bytes 7340032 | tf_op jit(solution)/shard_map/all_to_all | solution.py:247
  111.5 0.0 copy-start.6
  111.5 4.9 %shard_map.192 = bf16[256,1024]{1,0:T(8,128)(2,1)} custom-call(bf16[256,1024]{1,0:T(8,128)(2,1)} %bitcast.54, bf16[256,1024]{1,0:T(8,128)(2,1)} %bitcast.55, bf16[256,256]{1,0:T(8,128)(2,1)} %get-tuple-element.36.m4_ref, f32[1,1024]{1,0:T(1,128)} %gain_ref.9, f32[1,1024]{1,0:T(1,128)} %gain_ref.8, bf16[1024,256]{1,0:T(8,128)(2,1)} %bitcast.38, ...), custom_call_target="tpu_custom_call" | custom-call | tf_op jit(solution)/shard_map/pallas_call | solution.py:55
  116.4 3.5 %collective-permute-start = (bf16[256,1024]{1,0:T(8,128)(2,1)}, bf16[256,1024]{1,0:T(8,128)(2,1)S(1)}, u32[]{:S(2)}, u32[]{:S(2)}) collective-permute-start(bf16[256,1024]{1,0:T(8,128)(2,1)} %shard_map.192), channel_id=1, source_target_pairs={{0,32},{32,64},{64,96},{96,128},{128,160},{160,192},{192,224},{1,3... | collective-permute-start | bytes 1572872 | tf_op jit(solution)/shard_map/ppermute | solution.py:252
  119.9 3.1 %shard_map.199 = bf16[256,1024]{1,0:T(8,128)(2,1)} custom-call(bf16[256,1024]{1,0:T(8,128)(2,1)} %bitcast.32, bf16[256,1024]{1,0:T(8,128)(2,1)} %bitcast.45, bf16[256,256]{1,0:T(8,128)(2,1)} %get-tuple-element.46.m1t_ref, f32[256,1024]{1,0:T(8,128)} %get-tuple-element.53.dn1_ref, bf16[256,1024]{1,0:T(8,128)(2,1)} %get-tuple-element.54.dy1_ref, ...), custom_call_target="tpu_custom_call" | custom-call | tf_op jit(solution)/shard_map/pallas_call | solution.py:55
  123.0 1.3 collective-permute-start.1
  124.3 0.0 copy-done.6
  124.3 1.0 reshape.29
  125.3 6.2 %collective-permute-done = bf16[256,1024]{1,0:T(8,128)(2,1)S(1)} collective-permute-done((bf16[256,1024]{1,0:T(8,128)(2,1)}, bf16[256,1024]{1,0:T(8,128)(2,1)S(1)}, u32[]{:S(2)}, u32[]{:S(2)}) %collective-permute-start) | collective-permute-done | bytes 524320 | tf_op jit(solution)/shard_map/ppermute | solution.py:252
  131.5 7.2 %collective-permute-done.1 = bf16[256,1024]{1,0:T(8,128)(2,1)S(1)} collective-permute-done((bf16[256,1024]{1,0:T(8,128)(2,1)}, bf16[256,1024]{1,0:T(8,128)(2,1)S(1)}, u32[]{:S(2)}, u32[]{:S(2)}) %collective-permute-start.1) | collective-permute-done | bytes 524320 | tf_op jit(solution)/shard_map/ppermute | solution.py:252
  138.8 18.2 %all-to-all-done.6.recv_ref = bf16[32,224,256]{2,1,0:T(8,128)(2,1)} async-done(((bf16[32,224,256]{2,1,0:T(8,128)(2,1)}), bf16[32,224,256]{2,1,0:T(8,128)(2,1)}, u32[]{:S(2)}, u32[]{:S(2)}) %all-to-all-start.6) | async-done | bytes 3670048 | tf_op jit(solution)/shard_map/all_to_all | solution.py:247
  156.9 3.1 %shard_map.200 = (bf16[32,256]{1,0:T(8,128)(2,1)}, bf16[32,512]{1,0:T(8,128)(2,1)}, bf16[32,512]{1,0:T(8,128)(2,1)}, bf16[64,256]{1,0:T(8,128)(2,1)}) custom-call(bf16[32,224,256]{2,1,0:T(8,128)(2,1)} %all-to-all-done.6.recv_ref), custom_call_target="tpu_custom_call" | custom-call | tf_op jit(solution)/shard_map/pallas_call | solution.py:55
  160.0 0.8 copy.23
  160.8 0.8 copy.24
Async XLA Ops:
  3.0 20.2 %all-to-all-start.2 = ((bf16[32,8,1024]{2,1,0:T(8,128)(2,1)}), bf16[32,8,1024]{2,1,0:T(8,128)(2,1)S(1)}, u32[]{:S(2)}, u32[]{:S(2)}) async-start(bf16[32,8,1024]{2,1,0:T(8,128)(2,1)} %bitcast.51), calls=%async_computation.2 | async-start | bytes 1048576 | tf_op jit(solution)/shard_map/all_to_all | solution.py:247
  23.2 0.8 copy-start.3
  26.7 15.2 %all-to-all-start.3 = ((bf16[32,8,1024]{2,1,0:T(8,128)(2,1)}), bf16[32,8,1024]{2,1,0:T(8,128)(2,1)S(1)}, u32[]{:S(2)}, u32[]{:S(2)}) async-start(bf16[32,8,1024]{2,1,0:T(8,128)(2,1)} %bitcast.63), calls=%async_computation.3 | async-start | bytes 1048576 | tf_op jit(solution)/shard_map/all_to_all | solution.py:247
  41.9 7.3 %copy-start.2 = (bf16[32,8,1024]{2,1,0:T(8,128)(2,1)}, bf16[32,8,1024]{2,1,0:T(8,128)(2,1)S(1)}, u32[]{:S(2)}) copy-start(bf16[32,8,1024]{2,1,0:T(8,128)(2,1)S(1)} %all-to-all-done.3) | copy-start | bytes 1572868
  41.9 15.2 %all-to-all-start = ((bf16[32,8,1024]{2,1,0:T(8,128)(2,1)}), bf16[32,8,1024]{2,1,0:T(8,128)(2,1)S(1)}, u32[]{:S(2)}, u32[]{:S(2)}) async-start(bf16[32,8,1024]{2,1,0:T(8,128)(2,1)} %bitcast.49), calls=%async_computation | async-start | bytes 1048576 | tf_op jit(solution)/shard_map/all_to_all | solution.py:247
  57.1 6.7 %copy-start.1 = (bf16[32,8,1024]{2,1,0:T(8,128)(2,1)}, bf16[32,8,1024]{2,1,0:T(8,128)(2,1)S(1)}, u32[]{:S(2)}) copy-start(bf16[32,8,1024]{2,1,0:T(8,128)(2,1)S(1)} %all-to-all-done) | copy-start | bytes 1572868
  57.1 18.3 %all-to-all-start.4 = ((bf16[32,8,1024]{2,1,0:T(8,128)(2,1)}), bf16[32,8,1024]{2,1,0:T(8,128)(2,1)S(1)}, u32[]{:S(2)}, u32[]{:S(2)}) async-start(bf16[32,8,1024]{2,1,0:T(8,128)(2,1)} %bitcast.62), calls=%async_computation.4 | async-start | bytes 1048576 | tf_op jit(solution)/shard_map/all_to_all | solution.py:247
  75.4 3.7 %copy-start.4 = (bf16[32,8,1024]{2,1,0:T(8,128)(2,1)}, bf16[32,8,1024]{2,1,0:T(8,128)(2,1)S(1)}, u32[]{:S(2)}) copy-start(bf16[32,8,1024]{2,1,0:T(8,128)(2,1)S(1)} %all-to-all-done.4) | copy-start | bytes 1572868
  75.4 15.2 %all-to-all-start.1 = ((bf16[32,8,1024]{2,1,0:T(8,128)(2,1)}), bf16[32,8,1024]{2,1,0:T(8,128)(2,1)S(1)}, u32[]{:S(2)}, u32[]{:S(2)}) async-start(bf16[32,8,1024]{2,1,0:T(8,128)(2,1)} %bitcast.48), calls=%async_computation.1 | async-start | bytes 1048576 | tf_op jit(solution)/shard_map/all_to_all | solution.py:247
  90.6 15.2 %copy-start.5 = (bf16[32,8,1024]{2,1,0:T(8,128)(2,1)}, bf16[32,8,1024]{2,1,0:T(8,128)(2,1)S(1)}, u32[]{:S(2)}) copy-start(bf16[32,8,1024]{2,1,0:T(8,128)(2,1)S(1)} %all-to-all-done.1) | copy-start | bytes 1572868
  90.6 15.2 %all-to-all-start.5 = ((bf16[32,8,1024]{2,1,0:T(8,128)(2,1)}), bf16[32,8,1024]{2,1,0:T(8,128)(2,1)S(1)}, u32[]{:S(2)}, u32[]{:S(2)}) async-start(bf16[32,8,1024]{2,1,0:T(8,128)(2,1)} %bitcast.60), calls=%async_computation.5 | async-start | bytes 1048576 | tf_op jit(solution)/shard_map/all_to_all | solution.py:247
  105.9 0.8 copy-start
  106.7 50.2 %all-to-all-start.6 = ((bf16[32,224,256]{2,1,0:T(8,128)(2,1)}), bf16[32,224,256]{2,1,0:T(8,128)(2,1)}, u32[]{:S(2)}, u32[]{:S(2)}) async-start(bf16[32,224,256]{2,1,0:T(8,128)(2,1)} %get-tuple-element.56), calls=%async_computation.6 | async-start | bytes 7340032 | tf_op jit(solution)/shard_map/all_to_all | solution.py:247
  111.5 12.8 %copy-start.6 = (bf16[256,1024]{1,0:T(8,128)(2,1)S(1)}, bf16[256,1024]{1,0:T(8,128)(2,1)}, u32[]{:S(2)}) copy-start(bf16[256,1024]{1,0:T(8,128)(2,1)} %get-tuple-element.55) | copy-start | bytes 1572868
  116.4 15.2 %collective-permute-start = (bf16[256,1024]{1,0:T(8,128)(2,1)}, bf16[256,1024]{1,0:T(8,128)(2,1)S(1)}, u32[]{:S(2)}, u32[]{:S(2)}) collective-permute-start(bf16[256,1024]{1,0:T(8,128)(2,1)} %shard_map.192), channel_id=1, source_target_pairs={{0,32},{32,64},{64,96},{96,128},{128,160},{160,192},{192,224},{1,3... | collective-permute-start | bytes 1572872 | tf_op jit(solution)/shard_map/ppermute | solution.py:252
  123.0 15.8 %collective-permute-start.1 = (bf16[256,1024]{1,0:T(8,128)(2,1)}, bf16[256,1024]{1,0:T(8,128)(2,1)S(1)}, u32[]{:S(2)}, u32[]{:S(2)}) collective-permute-start(bf16[256,1024]{1,0:T(8,128)(2,1)} %shard_map.199), channel_id=1, source_target_pairs={{32,0},{64,32},{96,64},{128,96},{160,128},{192,160},{224,192},{33,... | collective-permute-start | bytes 1572872 | tf_op jit(solution)/shard_map/ppermute | solution.py:252

commit v2 on v1

--- a/solution.py
+++ b/solution.py
@@ -51,13 +51,76 @@
     return ((r >> 3) << 2) + (r & 3)
 
 
-def call(kernel, outs, *args, **kwargs):
+class Lazy:
+    def __init__(self, copy, ref):
+        self.copy, self.ref, self.waited = copy, ref, False
+
+    def get(self):
+        if not self.waited:
+            self.copy.wait()
+            self.waited = True
+        return self.ref
+
+    def __getitem__(self, index):
+        return self.get()[index]
+
+
+class Late:
+    def __init__(self, copy, ref):
+        self.copy, self.ref, self.flushed = copy, ref, False
+
+    def __getitem__(self, index):
+        return self.ref[index]
+
+    def __setitem__(self, index, value):
+        self.ref[index] = value
+
+    def flush(self):
+        self.copy.start()
+        self.flushed = True
+
+
+def call(kernel, outs, *args, scratch=(), mib=40):
+    arrays = [a for a, _ in args]
+    in_roles, out_roles = [r for _, r in args], [o[2] for o in outs]
+    n_in, n_out = len(args), len(outs)
+    ins_h = [i for i, r in enumerate(in_roles) if r == "h"]
+    outs_h = [i for i, r in enumerate(out_roles) if r == "h"]
+    spec = {"v": pl.BlockSpec(memory_space=pltpu.VMEM), "h": pl.BlockSpec(memory_space=pltpu.HBM)}
+    bufs = [pltpu.VMEM(arrays[i].shape, arrays[i].dtype) for i in ins_h]
+    bufs += [pltpu.VMEM(outs[i][0], outs[i][1]) for i in outs_h]
+    n_buf = len(bufs)
+
+    def body(*refs):
+        ins, results = list(refs[:n_in]), list(refs[n_in : n_in + n_out])
+        vmem = refs[n_in + n_out : n_in + n_out + n_buf]
+        sems = refs[n_in + n_out + n_buf]
+        rest = refs[n_in + n_out + n_buf + 1 :]
+        for k, i in enumerate(ins_h):
+            copy = pltpu.make_async_copy(ins[i], vmem[k], sems.at[k])
+            copy.start()
+            ins[i] = Lazy(copy, vmem[k])
+        for k, i in enumerate(outs_h, len(ins_h)):
+            results[i] = Late(pltpu.make_async_copy(vmem[k], results[i], sems.at[k]), vmem[k])
+        kernel(*ins, *results, *rest)
+        for i in ins_h:
+            ins[i].get()
+        for i in outs_h:
+            if not results[i].flushed:
+                results[i].flush()
+        for i in outs_h:
+            results[i].copy.wait()
+
     return pl.pallas_call(
-        kernel,
-        out_shape=[jax.ShapeDtypeStruct(s, d) for s, d in outs],
-        compiler_params=pltpu.CompilerParams(vmem_limit_bytes=56 << 20),
-        **kwargs,
-    )(*args)
+        body,
+        out_shape=[
+            (pltpu.HBM if o[2] == "h" else jax.ShapeDtypeStruct)(o[0], o[1]) for o in outs
+        ],
+        in_specs=[spec[r] for r in in_roles],
+        out_specs=[spec[r] for r in out_roles],
+        scratch_shapes=bufs + [pltpu.SemaphoreType.DMA((max(n_buf, 1),))] + list(scratch),
+        compiler_params=pltpu.CompilerParams(vmem_limit_bytes=mib << 20),
+    )(*(pltpu.with_memory_space_constraint(a, pltpu.HBM) if r == "h" else a for a, r in args))
 
 
 def rms(v):
@@ -71,7 +134,7 @@
     return mm(pick, w).astype(BF)
 
 
-def k_front(x_ref, gain_ref, first_ref, a1_ref):
+def k_front(first_ref, x_ref, gain_ref, a1_ref):
     rows = first_rows(first_ref[...])
     r, c = iota((T, T), 0), iota((T, T), 1)
     m1 = jnp.where((c >> 7) == r_half(r), jnp.concatenate([rows, rows], axis=1), 0).astype(BF)
@@ -103,24 +166,21 @@
     m4t[...] = jnp.where(r_half(r) == (c >> 7), mm_nt(e4t, w4), 0.0).astype(BF)
 
 
-def k_mid(recv_ref, spec_ref, m2_ref, m3_ref, b1_ref):
-    a2 = mm(m2_ref[...], recv_ref[...])
-    filt = (a2 * spec_ref[...].astype(F32)).astype(BF)
-    b1_ref[...] = mm(m3_ref[...], filt).astype(BF)
-
-
-def k_mid_keep(recv_ref, spec_ref, m2_ref, m3_ref, b1_ref, a2_ref):
+def k_mid(recv_ref, m2_ref, spec_ref, m3_ref, a1_ref, send_ref, a2_ref):
     a2 = mm(m2_ref[...], recv_ref[...])
     a2_ref[...] = a2
+    a2_ref.flush()
     filt = (a2 * spec_ref[...].astype(F32)).astype(BF)
-    b1_ref[...] = mm(m3_ref[...], filt).astype(BF)
-
-
-def k_mid_back(recv_ref, a2_ref, spec_ref, m3t_ref, m2t_ref, da1_ref, sg_ref):
-    dfilt = mm(m3t_ref[...], recv_ref[...])
+    send_ref[:, :D] = mm(m3_ref[...], filt).astype(BF)
+    send_ref[:, D:] = a1_ref[...]
+
+
+def k_mid_back(recv_ref, m3t_ref, a2_ref, spec_ref, m2t_ref, da1_ref, sg_ref):
+    dfilt = mm(m3t_ref[...], recv_ref[:, :D])
+    sg_ref[...] = (dfilt * a2_ref[...]).astype(BF)
+    sg_ref.flush()
     da2 = (dfilt * spec_ref[...].astype(F32)).astype(BF)
     da1_ref[...] = mm(m2t_ref[...], da2).astype(BF)
-    sg_ref[...] = (dfilt * a2_ref[...]).astype(BF)
 
 
 def cols(b, n):
@@ -131,7 +191,7 @@
     return slice(k * HB + b * NJ, k * HB + (b + 1) * NJ)
 
 
-def k_ahead(x_ref, g_ref, gain_ref, mix_ref, down_ref, n1_ref, gate_ref, dhid_ref):
+def k_ahead(x_ref, gain_ref, mix_ref, g_ref, down_ref, n1_ref, gate_ref, dhid_ref):
     x = x_ref[...].astype(F32)
     n1_ref[...] = (x * rms(x) * gain_ref[...]).astype(BF)
     for b in range(NB):
@@ -142,15 +202,17 @@
 
 
 def k_tail_back(
-    x_ref, recv_ref, g_ref, gate_ref, dhid_ref, m4_ref, m4t_ref, gain_ref, up_ref, act_ref,
-    db1_ref, dy1_ref, dgate_ref, n2_ref, hs_ref, dup_ref, dact_ref,
-    y1_ref, dn2_ref,
+    recv_ref, m4_ref, x_ref, gate_ref, gain_ref, up_ref, act_ref, dhid_ref, g_ref, m4t_ref,
+    m2_ref, spec_ref, m3_ref,
+    send_ref, dy1_ref, dgate_ref, n2_ref, hs_ref, dup_ref, dact_ref,
+    y1_ref, dn2_ref, b2_ref,
 ):
-    b2 = mm(m4_ref[...], recv_ref[...])
-    y1_ref[...] = (x_ref[...].astype(F32) + b2 * gate_ref[...]).astype(BF).astype(F32)
+    b2_ref[...] = mm(m4_ref[...], recv_ref[:, :D])
+    y1_ref[...] = (x_ref[...].astype(F32) + b2_ref[...] * gate_ref[...]).astype(BF).astype(F32)
     y1 = y1_ref[...]
     r2 = rms(y1)
     n2_ref[...] = (y1 * r2 * gain_ref[...]).astype(BF)
+    n2_ref.flush()
     for b in range(NB):
         n2 = n2_ref[:, cols(b, DB)]
         up = mm(n2, up_ref[cols(b, DB), :])
@@ -168,40 +230,89 @@
         dn2_ref[:, cols(b, DB)] = mm_nt(dup, up_ref[cols(b, DB), :]) + mm_nt(
             dact, act_ref[cols(b, DB), :]
         )
+    hs_ref.flush()
+    dup_ref.flush()
+    dact_ref.flush()
     s = gain_ref[...] * dn2_ref[...]
     y1 = y1_ref[...]
     back = r2 * s - y1 * (r2 * r2 * r2) * jnp.mean(s * y1, axis=-1, keepdims=True)
     dy1 = (g_ref[...].astype(F32) + back).astype(BF)
     dy1_ref[...] = dy1
+    dy1_ref.flush()
     dyw = dy1.astype(F32)
+    dgate_ref[...] = (dyw * b2_ref[...]).astype(BF)
+    dgate_ref.flush()
     db2 = (dyw * gate_ref[...]).astype(BF)
-    db1_ref[...] = mm(m4t_ref[...], db2).astype(BF)
-    dgate_ref[...] = (dyw * mm(m4_ref[...], recv_ref[...])).astype(BF)
-
-
-def k_grads(n1_ref, dgate_ref, n2_ref, dup_ref, dact_ref, hs_ref, g_ref, mix_ref, o_ref, dn1_ref):
-    for b in range(NB):
-        d = slice(8 * b, 8 * b + 8)
+    send_ref[:, :D] = mm(m4t_ref[...], db2).astype(BF)
+    filt = (mm(m2_ref[...], recv_ref[:, D:]) * spec_ref[...].astype(F32)).astype(BF)
+    send_ref[:, D:] = mm(m3_ref[...], filt).astype(BF)
+
+
+def k_grads(
+    n1_ref, dgate_ref, mix_ref, n2_ref, dup_ref, dact_ref, hs_ref, g_ref,
+    keep_ref, send_ref, dn1_ref,
+):
+    core = lax.axis_index("seq")
+
+    def put(b, rows, value):
+        v = (value * KGRAD).astype(BF).reshape(4, 2, rows.stop - rows.start, DB)
+
+        @pl.when((core & 1) == 0)
+        def _():
+            keep_ref[b, :, rows, :] = v[:, 0]
+            send_ref[b, :, rows, :] = v[:, 1]
+
+        @pl.when((core & 1) == 1)
+        def _():
+            keep_ref[b, :, rows, :] = v[:, 1]
+            send_ref[b, :, rows, :] = v[:, 0]
+
+    for b in range(NB):
         dgate = dgate_ref[:, cols(b, DB)]
         dn1_ref[:, cols(b, DB)] = mm_nt(dgate, mix_ref[cols(b, DB), :])
-        mix = mm_tn(n1_ref[:, cols(b, DB)], dgate) * KGRAD
-        o_ref[d, 0:32, :] = mix.astype(BF).reshape(8, 32, DB)
+        put(b, slice(0, 32), mm_tn(n1_ref[:, cols(b, DB)], dgate))
         n2 = n2_ref[:, cols(b, DB)]
-        up = (mm_tn(n2, dup_ref[:, cols(b, HB)]) * KGRAD).astype(BF).reshape(8, 32, HB)
-        o_ref[d, 32:64, :] = up[:, :, :DB]
-        o_ref[d, 64:96, :] = up[:, :, DB:]
-        act = (mm_tn(n2, dact_ref[:, cols(b, HB)]) * KGRAD).astype(BF).reshape(8, 32, HB)
-        o_ref[d, 96:128, :] = act[:, :, :DB]
-        o_ref[d, 128:160, :] = act[:, :, DB:]
-        down = mm_tn(hs_ref[:, cols(b, HB)], g_ref[:, cols(b, DB)]) * KGRAD
-        o_ref[d, 160:224, :] = down.astype(BF).reshape(8, 64, DB)
-
-
-def k_tail(x_ref, recv_ref, m4_ref, gain1_ref, gain2_ref, mix_ref, up_ref, act_ref, down_ref,
+        for h in range(2):
+            put(b, slice(32 + 32 * h, 64 + 32 * h), mm_tn(n2, dup_ref[:, cols(2 * b + h, DB)]))
+            put(b, slice(96 + 32 * h, 128 + 32 * h), mm_tn(n2, dact_ref[:, cols(2 * b + h, DB)]))
+        put(b, slice(160, 224), mm_tn(hs_ref[:, cols(b, HB)], g_ref[:, cols(b, DB)]))
+
+
+def k_sum_core(keep_ref, recv_ref, *outs):
+    for dy in range(4):
+        y = ((lax.axis_index("seq") >> 1) + dy) & 3
+        for x in range(4):
+            outs[dy][x] = (keep_ref[x, y].astype(F32) + recv_ref[x, y].astype(F32)).astype(BF)
+        outs[dy].flush()
+
+
+def k_sum_y(a_ref, b_ref, c_ref, d_ref, *outs):
+    for dx in range(4):
+        x = ((lax.axis_index("seq") >> 3) + dx) & 3
+        outs[dx][...] = (
+            a_ref[x].astype(F32) + b_ref[x].astype(F32) + c_ref[x].astype(F32) + d_ref[x].astype(F32)
+        ).astype(BF)
+
+
+def k_sum_x(a_ref, b_ref, c_ref, d_ref, mix_ref, up_ref, act_ref, down_ref):
+    def total(r):
+        return (
+            a_ref[r].astype(F32) + b_ref[r].astype(F32) + c_ref[r].astype(F32) + d_ref[r].astype(F32)
+        ).astype(BF)
+
+    mix_ref[...] = total(slice(0, 32))
+    up_ref[:, :DB] = total(slice(32, 64))
+    up_ref[:, DB:] = total(slice(64, 96))
+    act_ref[:, :DB] = total(slice(96, 128))
+    act_ref[:, DB:] = total(slice(128, 160))
+    down_ref[...] = total(slice(160, 224))
+
+
+def k_tail(recv_ref, m4_ref, x_ref, gain1_ref, mix_ref, gain2_ref, up_ref, act_ref, down_ref,
            out_ref, y1_ref, n_ref, hs_ref):
     x = x_ref[...].astype(F32)
     n_ref[...] = (x * rms(x) * gain1_ref[...]).astype(BF)
-    b2 = mm(m4_ref[...], recv_ref[...])
+    b2 = mm(m4_ref[...], recv_ref[:, D:])
     for b in range(NB):
         gate = mm(n_ref[:, cols(b, DB)], mix_ref[cols(b, DB), :])
         y1_ref[:, cols(b, DB)] = (
@@ -222,7 +333,7 @@
         ).astype(BF)
 
 
-def k_end(x_ref, recv_ref, m1t_ref, dn1_ref, dy1_ref, gain_ref, dx_ref):
+def k_end(recv_ref, m1t_ref, x_ref, gain_ref, dn1_ref, dy1_ref, dx_ref):
     x = x_ref[...].astype(F32)
     r1 = rms(x)
     s = gain_ref[...] * (mm(m1t_ref[...], recv_ref[...]) + dn1_ref[...])
@@ -230,21 +341,16 @@
     dx_ref[...] = (dy1_ref[...].astype(F32) + back).astype(BF)
 
 
-def k_sum(recv_ref, mix_ref, up_ref, act_ref, down_ref):
-    total = recv_ref[0].astype(F32)
-    for s in range(1, recv_ref.shape[0]):
-        total = total + recv_ref[s].astype(F32)
-    total = total.astype(BF)
-    mix_ref[...] = total[0:32]
-    up_ref[:, :DB] = total[32:64]
-    up_ref[:, DB:] = total[64:96]
-    act_ref[:, :DB] = total[96:128]
-    act_ref[:, DB:] = total[128:160]
-    down_ref[...] = total[160:224]
-
-
 def swap(v):
     return lax.all_to_all(v, "seq", split_axis=0, concat_axis=0, tiled=True)
+
+
+def ring_y(d):
+    return [(i, (i & 25) + ((((i >> 1) + d) & 3) << 1)) for i in range(32)]
+
+
+def ring_x(d):
+    return [(i, (i + 8 * d) & 31) for i in range(32)]
 
 
 def shift(v, by):
@@ -257,44 +363,64 @@
     first, second, third, fourth = first[0], second[0], third[0], fourth[0]
     mix, up, act, down = mix[0], up[0], act[0], down[0]
     spec = spec[0].reshape(T, D)
+
+    return body(xa, xb, g, gain1, gain2, first, second, spec, third, fourth, mix, up, act, down)
+
+
+def h(*arrays):
+    return [(a, "h") for a in arrays]
+
+
+def v(*arrays):
+    return [(a, "v") for a in arrays]
+
+
+def body(xa, xb, g, gain1, gain2, first, second, spec, third, fourth, mix, up, act, down):
     td, tt = (T, D), (T, T)
-
-    (a1b,) = call(k_front, [(td, BF)], xb, gain1, first)
-    rb = swap(a1b)
-    (a1a,) = call(k_front, [(td, BF)], xa, gain1, first)
-    ra = swap(a1a)
-    m1t, m2, m2t, m3, m3t, m4, m4t = call(k_prep, [(tt, BF)] * 7, first, second, third, fourth)
+    (a1b,) = call(k_front, [(td, BF, "v")], *h(first, xb, gain1))
+    r1 = swap(a1b)
+    (a1a,) = call(k_front, [(td, BF, "h")], *h(first, xa, gain1))
+    m1t, m2, m2t, m3, m3t, m4, m4t = call(
+        k_prep, [(tt, BF, "h")] * 7, *h(first, second, third, fourth)
+    )
+    send2, a2b = call(k_mid, [((T, 2 * D), BF, "v"), (td, F32, "h")], *v(r1), *h(m2, spec, m3, a1a))
+    r2 = swap(send2)
     n1b, gateb, dhid = call(
-        k_ahead, [(td, BF), (td, F32), ((T, FF), BF)], xb, g, gain1, mix, down
-    )
-    b1b, a2b = call(k_mid_keep, [(td, BF), (td, F32)], rb, spec, m2, m3)
-    qb = swap(b1b)
-    (b1a,) = call(k_mid, [(td, BF)], ra, spec, m2, m3)
-    qa = swap(b1a)
-    db1, dy1, dgate, n2, hs, dup, dact = call(
+        k_ahead,
+        [(td, BF, "h"), (td, F32, "h"), ((T, FF), BF, "h")],
+        *h(xb, gain1, mix, g, down),
+    )
+    send3, dy1, dgate, n2, hs, dup, dact = call(
         k_tail_back,
-        [(td, BF)] * 4 + [((T, FF), BF)] * 3,
-        xb, qb, g, gateb, dhid, m4, m4t, gain2, up, act,
-        scratch_shapes=[pltpu.VMEM(td, F32), pltpu.VMEM(td, F32)],
-    )
-    rc = swap(db1)
-    grads, dn1 = call(
-        k_grads, [((32, GR, DB), BF), (td, F32)], n1b, dgate, n2, dup, dact, hs, g, mix
-    )
-    gr = swap(grads)
+        [((T, 2 * D), BF, "v")] + [(td, BF, "h")] * 3 + [((T, FF), BF, "h")] * 3,
+        *v(r2),
+        *h(m4, xb, gateb, gain2, up, act, dhid, g, m4t, m2, spec, m3),
+        scratch=[pltpu.VMEM(td, F32)] * 3,
+    )
+    r3 = swap(send3)
+    keep, other, dn1 = call(
+        k_grads,
+        [((4, 4, GR, DB), BF, "h"), ((4, 4, GR, DB), BF, "h"), (td, F32, "h")],
+        *h(n1b, dgate, mix, n2, dup, dact, hs, g),
+    )
+    other = lax.ppermute(other, "seq", [(i, i ^ 1) for i in range(32)])
+    s0, *sy = call(k_sum_core, [((4, GR, DB), BF, "h")] * 4, *h(keep, other))
+    sy = [lax.ppermute(p, "seq", ring_y(d + 1)) for d, p in enumerate(sy)]
+    da1, sgrad = call(k_mid_back, [(td, BF, "v"), (td, BF, "h")], *v(r3), *h(m3t, a2b, spec, m2t))
+    r4 = swap(da1)
     (outa,) = call(
-        k_tail, [(td, BF)], xa, qa, m4, gain1, gain2, mix, up, act, down,
-        scratch_shapes=[pltpu.VMEM(td, F32), pltpu.VMEM(td, BF), pltpu.VMEM((T, FF), BF)],
+        k_tail, [(td, BF, "h")], *h(r3, m4, xa, gain1, mix, gain2, up, act, down),
+        scratch=[pltpu.VMEM(td, F32), pltpu.VMEM(td, BF), pltpu.VMEM((T, FF), BF)],
     )
     next_input = shift(outa, 1)
-    da1, sgrad = call(k_mid_back, [(td, BF), (td, BF)], rc, a2b, spec, m3t, m2t)
-    rd = swap(da1)
-    (dx,) = call(k_end, [(td, BF)], xb, rd, m1t, dn1, dy1, gain1)
+    (dx,) = call(k_end, [(td, BF, "h")], *v(r4), *h(m1t, xb, gain1, dn1, dy1))
     upstream = shift(dx, -1)
+    s0, *sx = call(k_sum_y, [((GR, DB), BF, "h")] * 4, *h(s0, *sy))
+    sx = [lax.ppermute(p, "seq", ring_x(d + 1)) for d, p in enumerate(sx)]
     gm, gu, ga, gd = call(
-        k_sum,
-        [((32, DB), BF), ((32, HB), BF), ((32, HB), BF), ((64, DB), BF)],
-        gr,
+        k_sum_x,
+        [((32, DB), BF, "h"), ((32, HB), BF, "h"), ((32, HB), BF, "h"), ((64, DB), BF, "h")],
+        *h(s0, *sx),
     )
     return (
         next_input[None],

time: 163 us -> 139 us (0.85)
  waiting for transfers between devices: 72.1 us -> 31 us
  blocking collectives: 0 us -> 20.7 us
  starting transfers between devices: 39.6 us -> 29.5 us
  Pallas kernels: 43.1 us -> 50.3 us
    all_to_all x7 -> x3, waiting for transfers between devices: 58.6 us -> 18.3 us  [swap(): return lax.all_to_all(v, 'seq', split_axis=0, concat_axis=0, tiled=True)]
    all_to_all x0 -> x1, blocking collectives: none -> 20.7 us  [swap(): return lax.all_to_all(v, 'seq', split_axis=0, concat_axis=0, tiled=True)]
    all_to_all x7 -> x3, starting transfers between devices: 34.8 us -> 16.3 us  [swap(): return lax.all_to_all(v, 'seq', split_axis=0, concat_axis=0, tiled=True)]
    ppermute x2, waiting for transfers between devices: 13.5 us -> 0.01 us  [shift(): lax.ppermute(v, 'section', [(i, i + by) for i in range(n) if 0 <= i + by...]
    ppermute x0 -> x7, waiting for transfers between devices: none -> 12.7 us  [the longest x3 8.36 us: body(): sy = [lax.ppermute(p, 'seq', ring_y(d + 1)) for d, p in enumerate(sy)]]
    ppermute x0 -> x7, starting transfers between devices: none -> 8.37 us  [the longest x3 5.01 us: body(): sy = [lax.ppermute(p, 'seq', ring_y(d + 1)) for d, p in enumerate(sy)]]
    pallas_call x12 -> x13, Pallas kernels: 43.1 us -> 50.3 us  [call(): pl.pallas_call(body, out_shape=[(pltpu.HBM if o[2] == 'h' else jax.ShapeD...]
    unnamed x16 -> x22, local copies, waits for them, and re-layouts: 3.19 us -> 4.44 us
  transfers between devices with their start and end apart: 9 -> 12, of which waited for: 9 -> 4; matrix products, arithmetic and copies ran while one was open for 2% -> 1% of each run, Pallas kernels for 22% -> 19%
where the time goes in v2:
time: 139 us
  Pallas kernels  50.3 us (36%)
  waiting for transfers between devices  31 us (22%)
  starting transfers between devices  29.5 us (21%)
  blocking collectives  20.7 us (15%)
  local copies, waits for them, and re-layouts  6.35 us (5%)
    pallas_call x13, Pallas kernels, call(): pl.pallas_call(body, out_shape=[(pltpu.HBM if o[2] == 'h' else jax.ShapeD...  50.3 us
    all_to_all x1, blocking collectives, swap(): return lax.all_to_all(v, 'seq', split_axis=0, concat_axis=0, tiled=True)  20.7 us
    all_to_all x3, waiting for transfers between devices, swap(): return lax.all_to_all(v, 'seq', split_axis=0, concat_axis=0, tiled=True)  18.3 us
    all_to_all x3, starting transfers between devices, swap(): return lax.all_to_all(v, 'seq', split_axis=0, concat_axis=0, tiled=True)  16.3 us
    ppermute x3, waiting for transfers between devices, body(): sy = [lax.ppermute(p, 'seq', ring_y(d + 1)) for d, p in enumerate(sy)]  8.36 us
    ppermute x3, starting transfers between devices, body(): sy = [lax.ppermute(p, 'seq', ring_y(d + 1)) for d, p in enumerate(sy)]  5.01 us
    ppermute x2, starting transfers between devices, shift(): lax.ppermute(v, 'section', [(i, i + by) for i in range(n) if 0 <= i + by...  4.86 us
    unnamed x22, local copies, waits for them, and re-layouts  4.44 us
  transfers between devices with their start and end apart: 12, of which 4 were waited for; matrix products, arithmetic and copies ran while one was open for 1% of the time, Pallas kernels for 19%

profile of v2, /device:TPU:1, one launch (start us, length us, event | category | flops | bytes accessed | tf_op | source)
XLA Modules:
  0.0 138.7 jit_solution(3907292098325813904)
XLA Ops:
  0.6 0.0 copy-start.2
  0.6 2.5 %shard_map.189 = bf16[256,1024]{1,0:T(8,128)(2,1)} custom-call(bf16[2,128,128]{2,1,0:T(8,128)(2,1)} %bitcast.49, bf16[256,1024]{1,0:T(8,128)(2,1)} %bitcast.31, f32[1,1024]{1,0:T(1,128)} %refs_3_.3), custom_call_target="tpu_custom_call" | custom-call | tf_op jit(solution)/shard_map/pallas_call | solution.py:114
  3.1 8.6 %all-to-all-start = ((bf16[32,8,1024]{2,1,0:T(8,128)(2,1)}), bf16[32,8,1024]{2,1,0:T(8,128)(2,1)S(1)}, u32[]{:S(2)}, u32[]{:S(2)}) async-start(bf16[32,8,1024]{2,1,0:T(8,128)(2,1)} %bitcast.2), calls=%async_computation | async-start | bytes 1048576 | tf_op jit(solution)/shard_map/all_to_all | solution.py:345
  11.7 0.0 copy-done.2
  11.7 0.9 reshape_squeeze.3.refs_2_.refs_11_.refs_3_
  12.6 2.4 %shard_map.191.refs_4_ = bf16[256,1024]{1,0:T(8,128)(2,1)} custom-call(bf16[2,128,128]{2,1,0:T(8,128)(2,1)} %bitcast.50, bf16[256,1024]{1,0:T(8,128)(2,1)} %bitcast.47, f32[1,1024]{1,0:T(1,128)} %refs_3_.3), custom_call_target="tpu_custom_call" | custom-call | tf_op jit(solution)/shard_map/pallas_call | solution.py:114
  15.0 3.1 %shard_map.190 = (bf16[256,256]{1,0:T(8,128)(2,1)}, bf16[256,256]{1,0:T(8,128)(2,1)}, bf16[256,256]{1,0:T(8,128)(2,1)}, bf16[256,256]{1,0:T(8,128)(2,1)}, bf16[2...) custom-call(bf16[2,128,128]{2,1,0:T(8,128)(2,1)} %bitcast.51, bf16[4,64,64]{2,1,0:T(8,128)(2,1)} %bitcast.54, ...), custom_call_target="tpu_custom_call" | custom-call | tf_op jit(solution)/shard_map/pallas_call | solution.py:114
  18.1 5.2 %all-to-all-done = bf16[32,8,1024]{2,1,0:T(8,128)(2,1)S(1)} async-done(((bf16[32,8,1024]{2,1,0:T(8,128)(2,1)}), bf16[32,8,1024]{2,1,0:T(8,128)(2,1)S(1)}, u32[]{:S(2)}, u32[]{:S(2)}) %all-to-all-start) | async-done | bytes 524320 | tf_op jit(solution)/shard_map/all_to_all | solution.py:345
  23.3 3.2 %shard_map.192 = (bf16[256,2048]{1,0:T(8,128)(2,1)}, f32[256,1024]{1,0:T(8,128)}) custom-call(bf16[256,1024]{1,0:T(8,128)(2,1)S(1)} %bitcast.29, bf16[256,256]{1,0:T(8,128)(2,1)} %get-tuple-element.43.refs_1_.refs_10_, bf16[256,1024]{1,0:T(8,128)(2,1)} %reshape_squeeze.3.refs_2_.refs_11_.refs_3_, bf16[256,256]{1,0:T(8,128)(2,1)} %get-tuple-element.44.refs_3_.refs_12_, ...), custom_call_target="tpu_custom_call" | custom-call | tf_op jit(solution)/shard_map/pallas_call | solution.py:114
  26.5 3.7 %all-to-all-start.1 = ((bf16[32,8,2048]{2,1,0:T(8,128)(2,1)}), bf16[32,8,2048]{2,1,0:T(8,128)(2,1)S(1)}, u32[]{:S(2)}, u32[]{:S(2)}) async-start(bf16[32,8,2048]{2,1,0:T(8,128)(2,1)} %bitcast.8), calls=%async_computation.1 | async-start | bytes 2097152 | tf_op jit(solution)/shard_map/all_to_all | solution.py:345
  30.2 3.6 %shard_map.193 = (bf16[256,1024]{1,0:T(8,128)(2,1)}, f32[256,1024]{1,0:T(8,128)}, bf16[256,2048]{1,0:T(8,128)(2,1)}) custom-call(bf16[256,1024]{1,0:T(8,128)(2,1)} %bitcast.32, f32[1,1024]{1,0:T(1,128)} %refs_3_.3, bf16[1024,256]{1,0:T(8,128)(2,1)} %bitcast.38, bf16[256,1024]{1,0:T(8,128)(2,1)} %bitcast.35, bf16[2048,256]{1,0:T(8,128)(2,1)} %bitcast.41), custom_call_target="tpu_custom_call" | custom-call | tf_op jit(solution)/shard_map/pallas_call | solution.py:114
  33.9 13.2 %all-to-all-done.1 = bf16[32,8,2048]{2,1,0:T(8,128)(2,1)S(1)} async-done(((bf16[32,8,2048]{2,1,0:T(8,128)(2,1)}), bf16[32,8,2048]{2,1,0:T(8,128)(2,1)S(1)}, u32[]{:S(2)}, u32[]{:S(2)}) %all-to-all-start.1) | async-done | bytes 1048608 | tf_op jit(solution)/shard_map/all_to_all | solution.py:345
  47.0 6.1 %shard_map.194 = (bf16[256,2048]{1,0:T(8,128)(2,1)S(1)}, bf16[256,1024]{1,0:T(8,128)(2,1)}, bf16[256,1024]{1,0:T(8,128)(2,1)}, bf16[256,1024]{1,0:T(8,128)(2,1)}...) custom-call(bf16[256,2048]{1,0:T(8,128)(2,1)S(1)} %bitcast.27, ...), custom_call_target="tpu_custom_call" | custom-call | tf_op jit(solution)/shard_map/pallas_call | solution.py:114
  53.1 10.5 %shard_map.197 = (bf16[4,4,224,256]{3,2,1,0:T(8,128)(2,1)}, bf16[4,4,224,256]{3,2,1,0:T(8,128)(2,1)}, f32[256,1024]{1,0:T(8,128)}) custom-call(bf16[256,1024]{1,0:T(8,128)(2,1)} %get-tuple-element.56.refs_0_, bf16[256,1024]{1,0:T(8,128)(2,1)} %get-tuple-element.57.refs_1_, bf16[1024,256]{1,0:T(8,128)(2,1)} %bitcast.39, ...), custom_call_target="tpu_custom_call" | custom-call | tf_op jit(solution)/shard_map/pallas_call | solution.py:114
  63.7 0.1 collective-permute-start.2
  63.8 20.7 %all_to_all.44 = bf16[32,8,2048]{2,1,0:T(8,128)(2,1)S(1)} all-to-all(bf16[32,8,2048]{2,1,0:T(8,128)(2,1)S(1)} %bitcast.30), channel_id=1, replica_groups=mesh['section'=8,'seq'=32] {'seq'}, dimensions={0} | all-to-all | bytes 2097152 | tf_op jit(solution)/shard_map/all_to_all | solution.py:345
  84.4 0.0 copy-start
  84.4 3.4 %shard_map.196 = (bf16[256,1024]{1,0:T(8,128)(2,1)}, bf16[256,1024]{1,0:T(8,128)(2,1)}) custom-call(bf16[256,2048]{1,0:T(8,128)(2,1)S(1)} %bitcast.25, bf16[256,256]{1,0:T(8,128)(2,1)} %get-tuple-element.51.refs_1_, f32[256,1024]{1,0:T(8,128)} %get-tuple-element.52.refs_2_, bf16[256,1024]{1,0:T(8,128)(2,1)} %reshape_squeeze.3.refs_2_.refs_11_.refs_3_, ...), custom_call_target="tpu_custom_call" | custom-call | tf_op jit(solution)/shard_map/pallas_call | solution.py:114
  87.8 0.0 copy-done
  87.8 3.9 %all-to-all-start.3 = ((bf16[32,8,1024]{2,1,0:T(8,128)(2,1)}), bf16[32,8,1024]{2,1,0:T(8,128)(2,1)S(1)}, u32[]{:S(2)}, u32[]{:S(2)}) async-start(bf16[32,8,1024]{2,1,0:T(8,128)(2,1)} %bitcast.18), calls=%async_computation.3 | async-start | bytes 1048576 | tf_op jit(solution)/shard_map/all_to_all | solution.py:345
  91.8 0.0 collective-permute-done.2.refs_1_
  91.8 0.0 copy-start.1
  91.8 1.2 copy-done.1
  93.0 3.6 %shard_map.199 = (bf16[4,224,256]{2,1,0:T(8,128)(2,1)}, bf16[4,224,256]{2,1,0:T(8,128)(2,1)}, bf16[4,224,256]{2,1,0:T(8,128)(2,1)}, bf16[4,224,256]{2,1,0:T(8,128)(2,1)}) custom-call(bf16[4,4,224,256]{3,2,1,0:T(8,128)(2,1)} %get-tuple-element.65.refs_0_, bf16[4,4,224,256]{3,2,1,0:T(8,128)(2,1)} %copy-done.1), custom_call_target="tpu_custom_call" | custom-call | tf_op jit(solution)/shard_map/pallas_call | solution.py:114
  96.5 1.4 %collective-permute-start.3 = (bf16[4,224,256]{2,1,0:T(8,128)(2,1)}, bf16[4,224,256]{2,1,0:T(8,128)(2,1)S(1)}, u32[]{:S(2)}, u32[]{:S(2)}) collective-permute-start(bf16[4,224,256]{2,1,0:T(8,128)(2,1)} %get-tuple-element.68), channel_id=1, source_target_pairs={{0,2},{1,3},{2,4},{3,5},{4,6},{5,7},{6,0},{7,1},{8,10},{9,11},{10,... | collective-permute-start | bytes 1376264 | tf_op jit(solution)/shard_map/ppermute | solution.py:408
  98.0 2.4 %collective-permute-start.4 = (bf16[4,224,256]{2,1,0:T(8,128)(2,1)}, bf16[4,224,256]{2,1,0:T(8,128)(2,1)S(1)}, u32[]{:S(2)}, u32[]{:S(2)}) collective-permute-start(bf16[4,224,256]{2,1,0:T(8,128)(2,1)} %get-tuple-element.69), channel_id=1, source_target_pairs={{0,4},{1,5},{2,6},{3,7},{4,0},{5,1},{6,2},{7,3},{8,12},{9,13},{10,... | collective-permute-start | bytes 1376264 | tf_op jit(solution)/shard_map/ppermute | solution.py:408
  100.4 1.2 collective-permute-start.5
  101.6 4.9 %shard_map.195 = bf16[256,1024]{1,0:T(8,128)(2,1)} custom-call(bf16[256,2048]{1,0:T(8,128)(2,1)} %bitcast.26, bf16[256,256]{1,0:T(8,128)(2,1)} %get-tuple-element.46.refs_1_, bf16[256,1024]{1,0:T(8,128)(2,1)} %bitcast.48, f32[1,1024]{1,0:T(1,128)} %refs_3_.3, bf16[1024,256]{1,0:T(8,128)(2,1)} %bitcast.40, f32[1,1024]{1,0:T(1,128)} %refs_5_.1, ...), custom_call_target="tpu_custom_call" | custom-call | tf_op jit(solution)/shard_map/pallas_call | solution.py:114
  106.4 3.6 %collective-permute-start = (bf16[256,1024]{1,0:T(8,128)(2,1)}, bf16[256,1024]{1,0:T(8,128)(2,1)S(1)}, u32[]{:S(2)}, u32[]{:S(2)}) collective-permute-start(bf16[256,1024]{1,0:T(8,128)(2,1)} %shard_map.195), channel_id=1, source_target_pairs={{0,32},{32,64},{64,96},{96,128},{128,160},{160,192},{192,224},{1,3... | collective-permute-start | bytes 1572872 | tf_op jit(solution)/shard_map/ppermute | solution.py:358
  110.0 0.0 all-to-all-done.3
  110.0 0.0 copy-start.3
  110.0 2.9 %shard_map.198 = bf16[256,1024]{1,0:T(8,128)(2,1)} custom-call(bf16[256,1024]{1,0:T(8,128)(2,1)S(1)} %bitcast.28, bf16[256,256]{1,0:T(8,128)(2,1)} %get-tuple-element.55.refs_1_, bf16[256,1024]{1,0:T(8,128)(2,1)} %bitcast.34, f32[1,1024]{1,0:T(1,128)} %refs_3_.3, f32[256,1024]{1,0:T(8,128)} %get-tuple-element.62.refs_4_, ...), custom_call_target="tpu_custom_call" | custom-call | tf_op jit(solution)/shard_map/pallas_call | solution.py:114
  113.0 1.3 collective-permute-start.1
  114.3 0.0 collective-permute-done.3.refs_1_
  114.3 0.0 copy-start.4
  114.3 8.4 %collective-permute-done.4.refs_2_ = bf16[4,224,256]{2,1,0:T(8,128)(2,1)S(1)} collective-permute-done((bf16[4,224,256]{2,1,0:T(8,128)(2,1)}, bf16[4,224,256]{2,1,0:T(8,128)(2,1)S(1)}, u32[]{:S(2)}, u32[]{:S(2)}) %collective-permute-start.4) | collective-permute-done | bytes 458784 | tf_op jit(solution)/shard_map/ppermute | solution.py:408
  122.7 0.0 copy-start.5
  122.7 0.0 collective-permute-done.5.refs_3_
  122.7 0.0 copy-start.6
  122.7 0.0 copy-done.4
  122.7 0.8 copy-done.5
  123.4 0.2 copy-done.6
  123.6 2.3 %shard_map.200 = (bf16[224,256]{1,0:T(8,128)(2,1)}, bf16[224,256]{1,0:T(8,128)(2,1)}, bf16[224,256]{1,0:T(8,128)(2,1)}, bf16[224,256]{1,0:T(8,128)(2,1)}) custom-call(bf16[4,224,256]{2,1,0:T(8,128)(2,1)} %get-tuple-element.67.refs_0_, bf16[4,224,256]{2,1,0:T(8,128)(2,1)} %copy-done.4, bf16[4,224,256]{2,1,0:T(8,128)(2,1)} %copy-done.5, ...), custom_call_target="tpu_custom_call" | custom-call | tf_op jit(solution)/shard_map/pallas_call | solution.py:114
  126.0 0.1 collective-permute-start.6
  126.0 1.7 %collective-permute-start.7 = (bf16[224,256]{1,0:T(8,128)(2,1)}, bf16[224,256]{1,0:T(8,128)(2,1)S(1)}, u32[]{:S(2)}, u32[]{:S(2)}) collective-permute-start(bf16[224,256]{1,0:T(8,128)(2,1)} %get-tuple-element.73), channel_id=1, source_target_pairs={{0,16},{1,17},{2,18},{3,19},{4,20},{5,21},{6,22},{7,23},{8,24},{9,... | collective-permute-start | bytes 344072 | tf_op jit(solution)/shard_map/ppermute | solution.py:419
  127.7 1.5 %collective-permute-start.8 = (bf16[224,256]{1,0:T(8,128)(2,1)}, bf16[224,256]{1,0:T(8,128)(2,1)S(1)}, u32[]{:S(2)}, u32[]{:S(2)}) collective-permute-start(bf16[224,256]{1,0:T(8,128)(2,1)} %get-tuple-element.74), channel_id=1, source_target_pairs={{0,24},{1,25},{2,26},{3,27},{4,28},{5,29},{6,30},{7,31},{8,0},{9,1... | collective-permute-start | bytes 344072 | tf_op jit(solution)/shard_map/ppermute | solution.py:419
  129.2 0.0 copy-done.3
  129.2 1.0 reshape.25
  130.2 0.0 collective-permute-done
  130.2 0.0 collective-permute-done.1
  130.2 4.3 %collective-permute-done.6.refs_1_ = bf16[224,256]{1,0:T(8,128)(2,1)S(1)} collective-permute-done((bf16[224,256]{1,0:T(8,128)(2,1)}, bf16[224,256]{1,0:T(8,128)(2,1)S(1)}, u32[]{:S(2)}, u32[]{:S(2)}) %collective-permute-start.6) | collective-permute-done | bytes 114720 | tf_op jit(solution)/shard_map/ppermute | solution.py:419
  134.5 0.0 copy-start.7
  134.5 0.0 collective-permute-done.7.refs_2_
  134.5 0.0 copy-start.8
  134.5 0.0 collective-permute-done.8.refs_3_
  134.5 0.0 copy-start.9
  134.6 0.6 copy-done.7
  135.2 0.0 copy-done.8
  135.2 0.0 copy-done.9
  135.3 1.8 %shard_map.201 = (bf16[32,256]{1,0:T(8,128)(2,1)}, bf16[32,512]{1,0:T(8,128)(2,1)}, bf16[32,512]{1,0:T(8,128)(2,1)}, bf16[64,256]{1,0:T(8,128)(2,1)}) custom-call(bf16[224,256]{1,0:T(8,128)(2,1)} %get-tuple-element.71.refs_0_, bf16[224,256]{1,0:T(8,128)(2,1)} %copy-done.7, bf16[224,256]{1,0:T(8,128)(2,1)} %copy-done.8, bf16[224,256]{1,0:T(8,128)(2,1)} %copy-done.9), custom_call_target="tpu_custom_call" | custom-call | tf_op jit(solution)/shard_map/pallas_call | solution.py:114
  137.1 0.8 copy.23
  137.9 0.8 copy.24
Async XLA Ops:
  0.6 11.1 %copy-start.2 = (bf16[1,64,4,1024]{3,2,1,0:T(4,128)(2,1)S(1)}, bf16[1,64,4,1024]{3,2,1,0:T(4,128)(2,1)}, u32[]{:S(2)}) copy-start(bf16[1,64,4,1024]{3,2,1,0:T(4,128)(2,1)} %param.21) | copy-start | bytes 1572868
  3.1 20.2 %all-to-all-start = ((bf16[32,8,1024]{2,1,0:T(8,128)(2,1)}), bf16[32,8,1024]{2,1,0:T(8,128)(2,1)S(1)}, u32[]{:S(2)}, u32[]{:S(2)}) async-start(bf16[32,8,1024]{2,1,0:T(8,128)(2,1)} %bitcast.2), calls=%async_computation | async-start | bytes 1048576 | tf_op jit(solution)/shard_map/all_to_all | solution.py:345
  26.5 20.6 %all-to-all-start.1 = ((bf16[32,8,2048]{2,1,0:T(8,128)(2,1)}), bf16[32,8,2048]{2,1,0:T(8,128)(2,1)S(1)}, u32[]{:S(2)}, u32[]{:S(2)}) async-start(bf16[32,8,2048]{2,1,0:T(8,128)(2,1)} %bitcast.8), calls=%async_computation.1 | async-start | bytes 2097152 | tf_op jit(solution)/shard_map/all_to_all | solution.py:345
  63.7 28.1 %collective-permute-start.2 = (bf16[4,4,224,256]{3,2,1,0:T(8,128)(2,1)}, bf16[4,4,224,256]{3,2,1,0:T(8,128)(2,1)S(1)}, u32[]{:S(2)}, u32[]{:S(2)}) collective-permute-start(bf16[4,4,224,256]{3,2,1,0:T(8,128)(2,1)} %get-tuple-element.66), channel_id=1, source_target_pairs={{0,1},{1,0},{2,3},{3,2},{4,5},{5,4},{6,7},{7,6},{8,9},{9,8},{10,11... | collective-permute-start | bytes 5505032 | tf_op jit(solution)/shard_map/ppermute | solution.py:406
  84.4 3.4 %copy-start = (bf16[32,8,2048]{2,1,0:T(8,128)(2,1)}, bf16[32,8,2048]{2,1,0:T(8,128)(2,1)S(1)}, u32[]{:S(2)}) copy-start(bf16[32,8,2048]{2,1,0:T(8,128)(2,1)S(1)} %all_to_all.44) | copy-start | bytes 3145732
  87.8 22.2 %all-to-all-start.3 = ((bf16[32,8,1024]{2,1,0:T(8,128)(2,1)}), bf16[32,8,1024]{2,1,0:T(8,128)(2,1)S(1)}, u32[]{:S(2)}, u32[]{:S(2)}) async-start(bf16[32,8,1024]{2,1,0:T(8,128)(2,1)} %bitcast.18), calls=%async_computation.3 | async-start | bytes 1048576 | tf_op jit(solution)/shard_map/all_to_all | solution.py:345
  91.8 1.2 copy-start.1
  96.5 17.8 %collective-permute-start.3 = (bf16[4,224,256]{2,1,0:T(8,128)(2,1)}, bf16[4,224,256]{2,1,0:T(8,128)(2,1)S(1)}, u32[]{:S(2)}, u32[]{:S(2)}) collective-permute-start(bf16[4,224,256]{2,1,0:T(8,128)(2,1)} %get-tuple-element.68), channel_id=1, source_target_pairs={{0,2},{1,3},{2,4},{3,5},{4,6},{5,7},{6,0},{7,1},{8,10},{9,11},{10,... | collective-permute-start | bytes 1376264 | tf_op jit(solution)/shard_map/ppermute | solution.py:408
  98.0 24.7 %collective-permute-start.4 = (bf16[4,224,256]{2,1,0:T(8,128)(2,1)}, bf16[4,224,256]{2,1,0:T(8,128)(2,1)S(1)}, u32[]{:S(2)}, u32[]{:S(2)}) collective-permute-start(bf16[4,224,256]{2,1,0:T(8,128)(2,1)} %get-tuple-element.69), channel_id=1, source_target_pairs={{0,4},{1,5},{2,6},{3,7},{4,0},{5,1},{6,2},{7,3},{8,12},{9,13},{10,... | collective-permute-start | bytes 1376264 | tf_op jit(solution)/shard_map/ppermute | solution.py:408
  100.4 22.3 %collective-permute-start.5 = (bf16[4,224,256]{2,1,0:T(8,128)(2,1)}, bf16[4,224,256]{2,1,0:T(8,128)(2,1)S(1)}, u32[]{:S(2)}, u32[]{:S(2)}) collective-permute-start(bf16[4,224,256]{2,1,0:T(8,128)(2,1)} %get-tuple-element.70), channel_id=1, source_target_pairs={{0,6},{1,7},{2,0},{3,1},{4,2},{5,3},{6,4},{7,5},{8,14},{9,15},{10,... | collective-permute-start | bytes 1376264 | tf_op jit(solution)/shard_map/ppermute | solution.py:408
  106.4 23.8 %collective-permute-start = (bf16[256,1024]{1,0:T(8,128)(2,1)}, bf16[256,1024]{1,0:T(8,128)(2,1)S(1)}, u32[]{:S(2)}, u32[]{:S(2)}) collective-permute-start(bf16[256,1024]{1,0:T(8,128)(2,1)} %shard_map.195), channel_id=1, source_target_pairs={{0,32},{32,64},{64,96},{96,128},{128,160},{160,192},{192,224},{1,3... | collective-permute-start | bytes 1572872 | tf_op jit(solution)/shard_map/ppermute | solution.py:358
  110.0 19.2 %copy-start.3 = (bf16[256,1024]{1,0:T(8,128)(2,1)S(1)}, bf16[256,1024]{1,0:T(8,128)(2,1)}, u32[]{:S(2)}) copy-start(bf16[256,1024]{1,0:T(8,128)(2,1)} %get-tuple-element.64) | copy-start | bytes 1572868
  113.0 17.2 %collective-permute-start.1 = (bf16[256,1024]{1,0:T(8,128)(2,1)}, bf16[256,1024]{1,0:T(8,128)(2,1)S(1)}, u32[]{:S(2)}, u32[]{:S(2)}) collective-permute-start(bf16[256,1024]{1,0:T(8,128)(2,1)} %shard_map.198), channel_id=1, source_target_pairs={{32,0},{64,32},{96,64},{128,96},{160,128},{192,160},{224,192},{33,... | collective-permute-start | bytes 1572872 | tf_op jit(solution)/shard_map/ppermute | solution.py:358
  114.3 8.4 %copy-start.4 = (bf16[4,224,256]{2,1,0:T(8,128)(2,1)}, bf16[4,224,256]{2,1,0:T(8,128)(2,1)S(1)}, u32[]{:S(2)}) copy-start(bf16[4,224,256]{2,1,0:T(8,128)(2,1)S(1)} %collective-permute-done.3.refs_1_) | copy-start | bytes 1376260
  122.7 0.8 copy-start.5
  122.7 0.9 copy-start.6
  126.0 8.6 %collective-permute-start.6 = (bf16[224,256]{1,0:T(8,128)(2,1)}, bf16[224,256]{1,0:T(8,128)(2,1)S(1)}, u32[]{:S(2)}, u32[]{:S(2)}) collective-permute-start(bf16[224,256]{1,0:T(8,128)(2,1)} %get-tuple-element.72), channel_id=1, source_target_pairs={{0,8},{1,9},{2,10},{3,11},{4,12},{5,13},{6,14},{7,15},{8,16},{9,17... | collective-permute-start | bytes 344072 | tf_op jit(solution)/shard_map/ppermute | solution.py:419
  126.0 8.5 %collective-permute-start.7 = (bf16[224,256]{1,0:T(8,128)(2,1)}, bf16[224,256]{1,0:T(8,128)(2,1)S(1)}, u32[]{:S(2)}, u32[]{:S(2)}) collective-permute-start(bf16[224,256]{1,0:T(8,128)(2,1)} %get-tuple-element.73), channel_id=1, source_target_pairs={{0,16},{1,17},{2,18},{3,19},{4,20},{5,21},{6,22},{7,23},{8,24},{9,... | collective-permute-start | bytes 344072 | tf_op jit(solution)/shard_map/ppermute | solution.py:419
  127.7 6.8 %collective-permute-start.8 = (bf16[224,256]{1,0:T(8,128)(2,1)}, bf16[224,256]{1,0:T(8,128)(2,1)S(1)}, u32[]{:S(2)}, u32[]{:S(2)}) collective-permute-start(bf16[224,256]{1,0:T(8,128)(2,1)} %get-tuple-element.74), channel_id=1, source_target_pairs={{0,24},{1,25},{2,26},{3,27},{4,28},{5,29},{6,30},{7,31},{8,0},{9,1... | collective-permute-start | bytes 344072 | tf_op jit(solution)/shard_map/ppermute | solution.py:419
  134.5 0.6 copy-start.7
  134.5 0.7 copy-start.8
  134.5 0.7 copy-start.9

commit v3 on v2

v3 whole, which is shorter than its diff:
```python
import math

import jax
import jax.numpy as jnp
from jax import lax
from jax.experimental import pallas as pl
from jax.experimental.pallas import tpu as pltpu
from jax.sharding import PartitionSpec as P

NB = 4
NI = 64
NJ = 128
D = 1024
FF = 2048
T = 256
HB = FF // NB
DB = D // NB
EPS = 1e-06
KGRAD = 1.0 / math.sqrt(NI * NJ)
GR = 224

F32 = jnp.float32
BF = jnp.bfloat16


def mm(a, b):
    return lax.dot_general(a, b, (((1,), (0,)), ((), ())), preferred_element_type=F32)


def mm_nt(a, b):
    return lax.dot_general(a, b, (((1,), (1,)), ((), ())), preferred_element_type=F32)


def iota(shape, dim):
    return lax.broadcasted_iota(jnp.int32, shape, dim)


def onehot(cond):
    return jnp.where(cond, 1.0, 0.0).astype(BF)


def r_half(r):
    return (r >> 2) & 1


def r_col(r):
    return ((r >> 3) << 2) + (r & 3)


class Lazy:
    def __init__(self, copies, ref):
        self.copies, self.ref, self.waited = copies, ref, set()

    def get(self, part=None):
        for k in range(len(self.copies)) if part is None else (part,):
            if k not in self.waited:
                self.copies[k].wait()
                self.waited.add(k)
        return self.ref

    def __getitem__(self, index):
        return self.get()[index]


class Late:
    def __init__(self, copies, ref):
        self.copies, self.ref, self.started = copies, ref, set()

    def __getitem__(self, index):
        return self.ref[index]

    def __setitem__(self, index, value):
        self.ref[index] = value

    def flush(self, part=None):
        for k in range(len(self.copies)) if part is None else (part,):
            if k not in self.started:
                self.copies[k].start()
                self.started.add(k)


PARTS = {"h": None, "x": 0, "c": 1}


def cuts(src, dst, sems, at, role, shape):
    if role == "h":
        return [pltpu.make_async_copy(src, dst, sems.at[at])]
    n = shape[PARTS[role]] // 4
    parts = [(slice(None),) * PARTS[role] + (pl.ds(k * n, n),) for k in range(4)]
    return [
        pltpu.make_async_copy(src.at[p], dst.at[p], sems.at[at + k]) for k, p in enumerate(parts)
    ]


def call(kernel, outs, *args, scratch=(), mib=40):
    arrays = [a for a, _ in args]
    in_roles, out_roles = [r for _, r in args], [o[2] for o in outs]
    n_in, n_out = len(args), len(outs)
    ins_h = [i for i, r in enumerate(in_roles) if r in PARTS]
    outs_h = [i for i, r in enumerate(out_roles) if r in PARTS]
    vm, hb = pl.BlockSpec(memory_space=pltpu.VMEM), pl.BlockSpec(memory_space=pltpu.HBM)
    bufs = [pltpu.VMEM(arrays[i].shape, arrays[i].dtype) for i in ins_h]
    bufs += [pltpu.VMEM(outs[i][0], outs[i][1]) for i in outs_h]
    n_buf = len(bufs)

    def body(*refs):
        ins, results = list(refs[:n_in]), list(refs[n_in : n_in + n_out])
        vmem = refs[n_in + n_out : n_in + n_out + n_buf]
        sems = refs[n_in + n_out + n_buf]
        rest = refs[n_in + n_out + n_buf + 1 :]
        at = 0
        for k, i in enumerate(ins_h):
            ins[i] = Lazy(cuts(ins[i], vmem[k], sems, at, in_roles[i], arrays[i].shape), vmem[k])
            for copy in ins[i].copies:
                copy.start()
            at += 4
        for k, i in enumerate(outs_h, len(ins_h)):
            copies = cuts(vmem[k], results[i], sems, at, out_roles[i], outs[i][0])
            results[i] = Late(copies, vmem[k])
            at += 4
        kernel(*ins, *results, *rest)
        for i in ins_h:
            ins[i].get()
        for i in outs_h:
            results[i].flush()
        for i in outs_h:
            for copy in results[i].copies:
                copy.wait()

    return pl.pallas_call(
        body,
        out_shape=[
            (jax.ShapeDtypeStruct if o[2] == "v" else pltpu.HBM)(o[0], o[1]) for o in outs
        ],
        in_specs=[vm if r == "v" else hb for r in in_roles],
        out_specs=[vm if r == "v" else hb for r in out_roles],
        scratch_shapes=bufs + [pltpu.SemaphoreType.DMA((4 * max(n_buf, 1),))] + list(scratch),
        compiler_params=pltpu.CompilerParams(vmem_limit_bytes=mib << 20),
    )(*(a if r == "v" else pltpu.with_memory_space_constraint(a, pltpu.HBM) for a, r in args))


def rows_of(n):
    return [slice(r, r + n) for r in range(0, T, n)]


def rms(v):
    return lax.rsqrt(jnp.mean(v * v, axis=-1, keepdims=True) + EPS)


def first_rows(first):
    w = first.reshape(T, NJ)
    r, t = iota((T, T), 0), iota((T, T), 1)
    pick = onehot(t == (r_half(r) << 7) + r_col(r))
    return mm(pick, w).astype(BF)


def k_front(first_ref, x_ref, gain_ref, a1_ref, n1_ref):
    rows = first_rows(first_ref[...])
    r, c = iota((T, T), 0), iota((T, T), 1)
    m1 = jnp.where((c >> 7) == r_half(r), jnp.concatenate([rows, rows], axis=1), 0).astype(BF)
    gain = gain_ref[...]
    for k in range(4):
        x_ref.get(k)
        for q in rows_of(16)[4 * k : 4 * k + 4]:
            x = x_ref.ref[q, :].astype(F32)
            n1_ref[q, :] = (x * rms(x) * gain).astype(BF)
    for k in range(4):
        a1_ref[:, cols(k, DB)] = mm(m1, n1_ref[:, cols(k, DB)]).astype(BF)
        a1_ref.flush(k)


def k_prep(first_ref, second_ref, third_ref, fourth_ref, m1t, m2, m2t, m3, m3t, m4, m4t):
    r, c = iota((T, T), 0), iota((T, T), 1)

    rows = first_rows(first_ref[...])
    e1t = onehot((iota((T, NJ), 0) & 127) == iota((T, NJ), 1))
    m1t[...] = jnp.where((r >> 7) == r_half(c), mm_nt(e1t, rows), 0.0).astype(BF)

    q = onehot(c == ((r & 3) << 6) + (r >> 2))
    e2 = onehot(iota((NI, T), 0) == (iota((NI, T), 1) >> 2))
    e2t = onehot((iota((T, NI), 0) >> 2) == iota((T, NI), 1))
    same = (r & 3) == (c & 3)
    for src, out, out_t in ((second_ref, m2, m2t), (third_ref, m3, m3t)):
        w = mm(q, src[...].reshape(T, NI)).astype(BF)
        out[...] = jnp.where(same, mm(w, e2), 0.0).astype(BF)
        out_t[...] = jnp.where(same, mm_nt(e2t, w), 0.0).astype(BF)

    w4 = fourth_ref[...].reshape(T, NJ)
    e4 = onehot(iota((NJ, T), 0) == r_col(iota((NJ, T), 1)))
    e4t = onehot(r_col(iota((T, NJ), 0)) == iota((T, NJ), 1))
    m4[...] = jnp.where((r >> 7) == r_half(c), mm(w4, e4), 0.0).astype(BF)
    m4t[...] = jnp.where(r_half(r) == (c >> 7), mm_nt(e4t, w4), 0.0).astype(BF)


def k_mid(recv_ref, m2_ref, spec_ref, m3_ref, a1_ref, send_ref, a2_ref):
    for k in range(4):
        q = cols(k, DB)
        a2 = mm(m2_ref[...], recv_ref[:, q])
        a2_ref[:, q] = a2
        filt = (a2 * spec_ref[:, q].astype(F32)).astype(BF)
        send_ref[:, q] = mm(m3_ref[...], filt).astype(BF)
        if k == 1:
            send_ref.flush(0)
    send_ref.flush(1)
    send_ref[:, D:] = a1_ref[...]
    send_ref.flush()


def k_mid_back(recv_ref, m3t_ref, a2_ref, spec_ref, m2t_ref, da1_ref, sg_ref):
    for k in range(4):
        q = cols(k, DB)
        dfilt = mm(m3t_ref[...], recv_ref[:, q])
        sg_ref[:, q] = (dfilt * a2_ref[:, q]).astype(BF)
        da2 = (dfilt * spec_ref[:, q].astype(F32)).astype(BF)
        da1_ref[:, q] = mm(m2t_ref[...], da2).astype(BF)
        da1_ref.flush(k)


def cols(b, n):
    return slice(b * n, (b + 1) * n)


def hcols(b, k):
    return slice(k * HB + b * NJ, k * HB + (b + 1) * NJ)


def k_ahead(x_ref, gain_ref, mix_ref, g_ref, down_ref, m4_ref, n1_ref, gate_ref, dhid_ref, x_out, m4_out):
    x = x_ref[...].astype(F32)
    n1_ref[...] = (x * rms(x) * gain_ref[...]).astype(BF)
    for b in range(NB):
        gate_ref[:, cols(b, DB)] = mm(n1_ref[:, cols(b, DB)], mix_ref[cols(b, DB), :])
        dhs = mm_nt(g_ref[:, cols(b, DB)], down_ref[cols(b, HB), :]).astype(BF)
        for k in range(NB):
            dhid_ref[:, hcols(b, k)] = dhs[:, cols(k, NJ)]
    x_out[...] = x_ref[...]
    m4_out[...] = m4_ref[...]


def k_tail_back(
    recv_ref, m4_ref, x_ref, gate_ref, gain_ref, m2_ref, spec_ref, m3_ref, up_ref, act_ref,
    dhid_ref, g_ref, m4t_ref,
    send_ref, dy1_ref, dgate_ref, n2_ref, hs_ref, dup_ref, dact_ref,
    y1_ref, dn2_ref, b2_ref, up2_ref, act2_ref, db2_ref, r2_ref,
):
    b2_ref[...] = mm(m4_ref[...], recv_ref[:, :D])
    gain = gain_ref[...]
    for q in rows_of(16):
        y1 = (x_ref[q, :].astype(F32) + b2_ref[q, :] * gate_ref[q, :]).astype(BF).astype(F32)
        y1_ref[q, :] = y1
        r2 = rms(y1)
        r2_ref[q, :] = r2
        n2_ref[q, :] = (y1 * r2 * gain).astype(BF)
    n2_ref.flush()

    def lift(b):
        n2 = n2_ref[:, cols(b, DB)]
        up2_ref[b % 2] = mm(n2, up_ref[cols(b, DB), :])
        act2_ref[b % 2] = mm(n2, act_ref[cols(b, DB), :])

    def lower(b):
        dn2_ref[:, cols(b, DB)] = mm_nt(dup_ref[:, cols(b, HB)], up_ref[cols(b, DB), :]) + mm_nt(
            dact_ref[:, cols(b, HB)], act_ref[cols(b, DB), :]
        )

    def follow(k):
        a2 = mm(m2_ref[...], recv_ref[:, cols(4 + k, DB)])
        filt = (a2 * spec_ref[:, cols(k, DB)].astype(F32)).astype(BF)
        send_ref[:, cols(4 + k, DB)] = mm(m3_ref[...], filt).astype(BF)

    for w in (m2_ref, spec_ref, m3_ref, up_ref, act_ref, dhid_ref):
        w.get()
    lift(0)
    for b in range(NB):
        if b + 1 < NB:
            lift(b + 1)
        if b > 0:
            lower(b - 1)
        follow(b)
        for q in rows_of(32):
            up, act = up2_ref[b % 2, q, :], act2_ref[b % 2, q, :]
            sg = jax.nn.sigmoid(act)
            silu = act * sg
            hid = (silu * up).astype(BF)
            for k in range(NB):
                hs_ref[q, hcols(b, k)] = hid[:, cols(k, NJ)]
            dhid = dhid_ref[q, cols(b, HB)].astype(F32)
            dup_ref[q, cols(b, HB)] = (dhid * silu).astype(BF)
            dact_ref[q, cols(b, HB)] = (dhid * up * (sg + silu * (1.0 - sg))).astype(BF)
        dup_ref.flush(b)
        dact_ref.flush(b)
    lower(NB - 1)
    send_ref.flush(2)
    send_ref.flush(3)
    hs_ref.flush()
    for q in rows_of(16):
        s = gain * dn2_ref[q, :]
        y1, r2 = y1_ref[q, :], r2_ref[q, :]
        back = r2 * s - y1 * (r2 * r2 * r2) * jnp.mean(s * y1, axis=-1, keepdims=True)
        dy1 = (g_ref[q, :].astype(F32) + back).astype(BF)
        dy1_ref[q, :] = dy1
        dyw = dy1.astype(F32)
        db2_ref[q, :] = (dyw * gate_ref[q, :]).astype(BF)
        dgate_ref[q, :] = (dyw * b2_ref[q, :]).astype(BF)
    dy1_ref.flush()
    dgate_ref.flush()
    for k in range(4):
        send_ref[:, cols(k, DB)] = mm(m4t_ref[...], db2_ref[:, cols(k, DB)]).astype(BF)
        if k % 2:
            send_ref.flush(k // 2)


def k_grads(
    n1_ref, dgate_ref, mix_ref, n2_ref, dup_ref, dact_ref, hs_ref, g_ref,
    keep_ref, send_ref, dn1_ref, buf_ref, sems,
):
    core = lax.axis_index("seq") & 1

    def put(b, rows, value):
        w = value.astype(BF).reshape(4, 2, rows.stop - rows.start, DB)
        buf_ref[core, b, :, rows, :] = w[:, 0]
        buf_ref[1 - core, b, :, rows, :] = w[:, 1]

    copies = []
    for b in range(NB):
        dgate = dgate_ref[:, cols(b, DB)]
        put(b, slice(0, 32), mm(n1_ref[:, cols(b, DB)].T, dgate))
        dn1_ref[:, cols(b, DB)] = mm_nt(dgate, mix_ref[cols(b, DB), :])
        n2 = n2_ref[:, cols(b, DB)].T
        for k in range(2):
            put(b, slice(32 + 32 * k, 64 + 32 * k), mm(n2, dup_ref[:, cols(2 * b + k, DB)]))
            put(b, slice(96 + 32 * k, 128 + 32 * k), mm(n2, dact_ref[:, cols(2 * b + k, DB)]))
        put(b, slice(160, 224), mm(hs_ref[:, cols(b, HB)].T, g_ref[:, cols(b, DB)]))
        for side, out in enumerate((keep_ref, send_ref)):
            copy = pltpu.make_async_copy(buf_ref.at[side, b], out.at[b], sems.at[2 * b + side])
            copy.start()
            copies.append(copy)
    for copy in copies:
        copy.wait()


def ring_slots():
    i = lax.axis_index("seq")
    return i & 1, i >> 3, (i >> 1) & 3


def k_sum_core(keep_ref, recv_ref, *outs):
    core, x, y = ring_slots()
    keep = keep_ref.get()
    for d in range(4):
        for k in range(4):
            ix = jnp.where(core == 0, k, (x + d) & 3)
            iy = jnp.where(core == 0, (y + d) & 3, k)
            outs[d][k] = (keep[ix, iy].astype(F32) + recv_ref[ix, iy].astype(F32)).astype(BF)
        outs[d].flush()


def k_sum_ring(a_ref, b_ref, c_ref, d_ref, *outs):
    core, x, y = ring_slots()
    for d in range(4):
        k = (jnp.where(core == 0, x, y) + d) & 3
        outs[d][...] = (
            a_ref[k].astype(F32) + b_ref[k].astype(F32) + c_ref[k].astype(F32) + d_ref[k].astype(F32)
        ).astype(BF)


def k_sum_x(a_ref, b_ref, c_ref, d_ref, mix_ref, up_ref, act_ref, down_ref):
    def total(r):
        w = a_ref[r].astype(F32) + b_ref[r].astype(F32) + c_ref[r].astype(F32) + d_ref[r].astype(F32)
        return (w * KGRAD).astype(BF)

    mix_ref[...] = total(slice(0, 32))
    up_ref[:, :DB] = total(slice(32, 64))
    up_ref[:, DB:] = total(slice(64, 96))
    act_ref[:, :DB] = total(slice(96, 128))
    act_ref[:, DB:] = total(slice(128, 160))
    down_ref[...] = total(slice(160, 224))


def k_place(a_ref, b_ref, a_out, b_out, sems):
    copies = [
        pltpu.make_async_copy(a_ref, a_out.at[0], sems.at[0]),
        pltpu.make_async_copy(b_ref, b_out.at[0], sems.at[1]),
    ]
    for copy in copies:
        copy.start()
    for copy in copies:
        copy.wait()


def k_tail(recv_ref, m4_ref, x_ref, gain1_ref, mix_ref, gain2_ref, up_ref, act_ref, down_ref,
           out_ref, y1_ref, n_ref, hs_ref, gate_ref, b2_ref, up2_ref, act2_ref):
    gain1 = gain1_ref[...]
    for q in rows_of(16):
        x = x_ref[q, :].astype(F32)
        n_ref[q, :] = (x * rms(x) * gain1).astype(BF)
    for b in range(NB):
        b2_ref[:, cols(b, DB)] = mm(m4_ref[...], recv_ref[:, cols(4 + b, DB)])
        gate_ref[:, cols(b, DB)] = mm(n_ref[:, cols(b, DB)], mix_ref[cols(b, DB), :])
    gain2 = gain2_ref[...]
    for q in rows_of(16):
        y1 = (x_ref[q, :].astype(F32) + b2_ref[q, :] * gate_ref[q, :]).astype(BF).astype(F32)
        y1_ref[q, :] = y1
        n_ref[q, :] = (y1 * rms(y1) * gain2).astype(BF)

    def lift(b):
        n2 = n_ref[:, cols(b, DB)]
        up2_ref[b % 2] = mm(n2, up_ref[cols(b, DB), :])
        act2_ref[b % 2] = mm(n2, act_ref[cols(b, DB), :])

    lift(0)
    for b in range(NB):
        if b + 1 < NB:
            lift(b + 1)
        for q in rows_of(32):
            up, act = up2_ref[b % 2, q, :], act2_ref[b % 2, q, :]
            hid = (act * jax.nn.sigmoid(act) * up).astype(BF)
            for k in range(NB):
                hs_ref[q, hcols(b, k)] = hid[:, cols(k, NJ)]
    for b in range(NB):
        out_ref[:, cols(b, DB)] = (
            y1_ref[:, cols(b, DB)] + mm(hs_ref[:, cols(b, HB)], down_ref[cols(b, HB), :])
        ).astype(BF)


def k_end(recv_ref, m1t_ref, x_ref, gain_ref, dn1_ref, dy1_ref, dx_ref, w_ref):
    gain = gain_ref[...]
    for k in range(4):
        q = cols(k, DB)
        w_ref[:, q] = mm(m1t_ref[...], recv_ref[:, q]) + dn1_ref[:, q]
    for q in rows_of(16):
        x = x_ref[q, :].astype(F32)
        r1 = rms(x)
        s = gain * w_ref[q, :]
        back = r1 * s - x * (r1 * r1 * r1) * jnp.mean(s * x, axis=-1, keepdims=True)
        dx_ref[q, :] = (dy1_ref[q, :].astype(F32) + back).astype(BF)


def swap(v):
    return lax.all_to_all(v, "seq", split_axis=0, concat_axis=0, tiled=True)


def ring_y(i, d):
    return (i & 25) + ((((i >> 1) + d) & 3) << 1)


def ring_x(i, d):
    return (i + 8 * d) & 31


def ring(value, even, odd, d):
    pairs = [(i, odd(i, d) if i & 1 else even(i, d)) for i in range(32)]
    return lax.ppermute(value, "seq", pairs)


def shift(v, by):
    n = lax.axis_size("section")
    return lax.ppermute(v, "section", [(i, i + by) for i in range(n) if 0 <= i + by < n])


def shards(xa, xb, g, gain1, gain2, first, second, spec, third, fourth, mix, up, act, down):
    xa, xb, g = xa[0], xb[0], g[0]
    first, second, third, fourth = first[0], second[0], third[0], fourth[0]
    mix, up, act, down = mix[0], up[0], act[0], down[0]
    spec = spec[0].reshape(T, D)

    return body(xa, xb, g, gain1, gain2, first, second, spec, third, fourth, mix, up, act, down)


def h(*arrays):
    return [(a, "h") for a in arrays]


def v(*arrays):
    return [(a, "v") for a in arrays]


def front(x, gain, first):
    return call(
        k_front, [((T, D), BF, "c")], (first, "h"), (x, "x"), (gain, "h"),
        scratch=[pltpu.VMEM((T, D), BF)],
    )


def body(xa, xb, g, gain1, gain2, first, second, spec, third, fourth, mix, up, act, down):
    td, tt = (T, D), (T, T)
    (a1b,) = front(xb, gain1, first)
    r1 = swap(a1b)
    (a1a,) = front(xa, gain1, first)
    m1t, m2, m2t, m3, m3t, m4, m4t = call(
        k_prep, [(tt, BF, r) for r in "hvhvhhh"], *h(first, second, third, fourth)
    )
    send2, a2b = call(k_mid, [((T, 2 * D), BF, "c"), (td, F32, "h")], *v(r1, m2, spec, m3), *h(a1a))
    r2 = swap(send2)
    n1b, gateb, dhid, xb_v, m4_v = call(
        k_ahead,
        [(td, BF, "h"), (td, F32, "v"), ((T, FF), BF, "h"), (td, BF, "v"), (tt, BF, "v")],
        *h(xb, gain1, mix, g, down, m4),
    )
    send3, dy1, dgate, n2, hs, dup, dact = call(
        k_tail_back,
        [((T, 2 * D), BF, "c")]
        + [(td, BF, "h")] * 3
        + [((T, FF), BF, "h")]
        + [((T, FF), BF, "c")] * 2,
        *v(r2, m4_v, xb_v, gateb),
        *h(gain2, m2, spec, m3, up, act, dhid, g, m4t),
        scratch=[pltpu.VMEM(td, F32)] * 3
        + [pltpu.VMEM((2, T, HB), F32)] * 2
        + [pltpu.VMEM(td, BF), pltpu.VMEM((T, 1), F32)],
    )
    r3 = swap(send3)
    keep, other, dn1 = call(
        k_grads,
        [((4, 4, GR, DB), BF, "r"), ((4, 4, GR, DB), BF, "r"), (td, F32, "h")],
        *h(n1b, dgate, mix, n2, dup, dact, hs, g),
        scratch=[pltpu.VMEM((2, 4, 4, GR, DB), BF), pltpu.SemaphoreType.DMA((8,))],
    )
    other = lax.ppermute(other, "seq", [(i, i ^ 1) for i in range(32)])
    s0, *sy = call(k_sum_core, [((4, GR, DB), BF, "h")] * 4, *h(keep), *v(other))
    for d in (1, 3, 2):
        sy[d - 1] = ring(sy[d - 1], ring_y, ring_x, d)
    da1, sgrad = call(
        k_mid_back, [(td, BF, "c"), (td, BF, "h")], *v(r3), *h(m3t, a2b), *v(spec), *h(m2t)
    )
    r4 = swap(da1)
    (outa,) = call(
        k_tail, [(td, BF, "v")], *h(r3, m4, xa, gain1, mix, gain2, up, act, down),
        scratch=[pltpu.VMEM(td, F32), pltpu.VMEM(td, BF), pltpu.VMEM((T, FF), BF)]
        + [pltpu.VMEM(td, F32)] * 2
        + [pltpu.VMEM((2, T, HB), F32)] * 2,
    )
    next_input = shift(outa, 1)
    (dx,) = call(
        k_end, [(td, BF, "v")], *v(r4), *h(m1t, xb, gain1, dn1, dy1),
        scratch=[pltpu.VMEM(td, F32)],
    )
    upstream = shift(dx, -1)
    s0, *sx = call(k_sum_ring, [((GR, DB), BF, "v")] * 4, *h(s0), *v(*sy))
    sx = [ring(p, ring_x, ring_y, d + 1) for d, p in enumerate(sx)]
    gm, gu, ga, gd = call(
        k_sum_x,
        [((32, DB), BF, "h"), ((32, HB), BF, "h"), ((32, HB), BF, "h"), ((64, DB), BF, "h")],
        *v(s0, *sx),
    )
    next_input, upstream = call(
        k_place, [((1, T, D), BF, "r")] * 2, *v(next_input, upstream),
        scratch=[pltpu.SemaphoreType.DMA((2,))],
    )
    return (
        next_input,
        upstream,
        sgrad.reshape(1, NI, 4, D),
        gm[None],
        gu[None],
        ga[None],
        gd[None],
    )


def solution(mesh):
    in_specs = (
        P("section", "seq", None),
        P("section", "seq", None),
        P("section", "seq", None),
        P("section", None),
        P("section", None),
        P("section", "seq", None, None),
        P("section", "seq", None, None),
        P("section", None, "seq", None),
        P("section", "seq", None, None),
        P("section", "seq", None, None),
        P("section", None, None),
        P("section", None, None),
        P("section", None, None),
        P("section", None, None),
    )
    out_specs = (
        P("section", "seq", None),
        P("section", "seq", None),
        P("section", None, "seq", None),
        P("section", "seq", None),
        P("section", "seq", None),
        P("section", "seq", None),
        P("section", "seq", None),
    )
    return jax.shard_map(shards, mesh=mesh, in_specs=in_specs, out_specs=out_specs, check_vma=False)
```

time: 139 us -> 126 us (0.906)
  the two profiles are of different devices: /device:TPU:1 before, /device:TPU:96 now
where the time goes in v3:
time: 126 us; the launch traced here: 125 us
  Pallas kernels  44.9 us (36%)
  starting transfers between devices  34.6 us (27%)
  waiting for transfers between devices  21.6 us (17%)
  blocking collectives  20.4 us (16%)
  local copies, waits for them, and re-layouts  2.83 us (2%)
    pallas_call x14, Pallas kernels, call(): pl.pallas_call(body, out_shape=[(jax.ShapeDtypeStruct if o[2] == 'v' else...  44.9 us
    all_to_all x1, blocking collectives, swap(): return lax.all_to_all(v, 'seq', split_axis=0, concat_axis=0, tiled=True)  20.4 us
    all_to_all x3, waiting for transfers between devices, swap(): return lax.all_to_all(v, 'seq', split_axis=0, concat_axis=0, tiled=True)  17.8 us
    all_to_all x3, starting transfers between devices, swap(): return lax.all_to_all(v, 'seq', split_axis=0, concat_axis=0, tiled=True)  15.5 us
    ppermute x6, starting transfers between devices, ring(): return lax.ppermute(value, 'seq', pairs)  11.6 us
    ppermute x2, starting transfers between devices, shift(): lax.ppermute(v, 'section', [(i, i + by) for i in range(n) if 0 <= i + by...  6.95 us
    ppermute x2, waiting for transfers between devices, shift(): lax.ppermute(v, 'section', [(i, i + by) for i in range(n) if 0 <= i + by...  3.77 us
  transfers between devices with their start and end apart: 12, of which 3 were waited for; matrix products, arithmetic and copies ran while one was open for 2% of the time, Pallas kernels for 21%

profile of v3, /device:TPU:96, one launch (start us, length us, event | category | flops | bytes accessed | tf_op | source)
XLA Modules:
  0.0 125.4 jit_solution(1698215713809766006)
XLA Ops:
  0.6 0.0 copy-start.8
  0.6 2.7 %shard_map.189 = bf16[256,1024]{1,0:T(8,128)(2,1)} custom-call(bf16[2,128,128]{2,1,0:T(8,128)(2,1)} %bitcast.48, bf16[256,1024]{1,0:T(8,128)(2,1)} %bitcast.28, f32[1,1024]{1,0:T(1,128)} %refs_3_.3), custom_call_target="tpu_custom_call" | custom-call | tf_op jit(solution)/shard_map/pallas_call | solution.py:130
  3.4 7.3 %all-to-all-start = ((bf16[32,8,1024]{2,1,0:T(8,128)(2,1)}), bf16[32,8,1024]{2,1,0:T(8,128)(2,1)S(1)}, u32[]{:S(2)}, u32[]{:S(2)}) async-start(bf16[32,8,1024]{2,1,0:T(8,128)(2,1)} %bitcast.45), calls=%async_computation | async-start | bytes 1048576 | tf_op jit(solution)/shard_map/all_to_all | solution.py:439
  10.7 0.0 copy-done.8
  10.7 0.1 reshape_squeeze.3.refs_2_.refs_6_.refs_3_
  10.8 0.0 copy-start.1
  10.8 2.8 %shard_map.191.refs_4_ = bf16[256,1024]{1,0:T(8,128)(2,1)} custom-call(bf16[2,128,128]{2,1,0:T(8,128)(2,1)} %bitcast.49, bf16[256,1024]{1,0:T(8,128)(2,1)} %bitcast.43, f32[1,1024]{1,0:T(1,128)} %refs_3_.3), custom_call_target="tpu_custom_call" | custom-call | tf_op jit(solution)/shard_map/pallas_call | solution.py:130
  13.6 3.2 %shard_map.190 = (bf16[256,256]{1,0:T(8,128)(2,1)}, bf16[256,256]{1,0:T(8,128)(2,1)S(1)}, bf16[256,256]{1,0:T(8,128)(2,1)}, bf16[256,256]{1,0:T(8,128)(2,1)S(1)}...) custom-call(bf16[2,128,128]{2,1,0:T(8,128)(2,1)} %bitcast.50, ...), custom_call_target="tpu_custom_call" | custom-call | tf_op jit(solution)/shard_map/pallas_call | solution.py:130
  16.9 0.0 copy-start.3
  16.9 0.0 copy-start.4
  16.9 4.9 %all-to-all-done = bf16[32,8,1024]{2,1,0:T(8,128)(2,1)S(1)} async-done(((bf16[32,8,1024]{2,1,0:T(8,128)(2,1)}), bf16[32,8,1024]{2,1,0:T(8,128)(2,1)S(1)}, u32[]{:S(2)}, u32[]{:S(2)}) %all-to-all-start) | async-done | bytes 524320 | tf_op jit(solution)/shard_map/all_to_all | solution.py:439
  21.8 2.4 %shard_map.192 = (bf16[256,2048]{1,0:T(8,128)(2,1)}, f32[256,1024]{1,0:T(8,128)}) custom-call(bf16[256,1024]{1,0:T(8,128)(2,1)S(1)} %bitcast.27, bf16[256,256]{1,0:T(8,128)(2,1)S(1)} %get-tuple-element.47.refs_1_.refs_5_, bf16[256,1024]{1,0:T(8,128)(2,1)S(1)} %reshape_squeeze.3.refs_2_.refs_6_.refs_3_, ...), custom_call_target="tpu_custom_call" | custom-call | tf_op jit(solution)/shard_map/pallas_call | solution.py:130
  24.1 0.0 copy-done.1
  24.1 0.0 copy-done.3
  24.1 0.0 copy-done.4
  24.2 4.2 %all-to-all-start.1 = ((bf16[32,8,2048]{2,1,0:T(8,128)(2,1)}), bf16[32,8,2048]{2,1,0:T(8,128)(2,1)S(1)}, u32[]{:S(2)}, u32[]{:S(2)}) async-start(bf16[32,8,2048]{2,1,0:T(8,128)(2,1)} %bitcast.47), calls=%async_computation.1 | async-start | bytes 2097152 | tf_op jit(solution)/shard_map/all_to_all | solution.py:439
  28.3 3.8 %shard_map.193 = (bf16[256,1024]{1,0:T(8,128)(2,1)}, f32[256,1024]{1,0:T(8,128)S(1)}, bf16[256,2048]{1,0:T(8,128)(2,1)}, bf16[256,1024]{1,0:T(8,128)(2,1)S(1)}, bf16[256,256]{1,0:T(8,128)(2,1)S(1)}) custom-call(bf16[256,1024]{1,0:T(8,128)(2,1)} %bitcast.29, f32[1,1024]{1,0:T(1,128)} %refs_3_.3, bf16[1024,256]{1,0:T(8,128)(2,1)} %bitcast.34, ...), custom_call_target="tpu_custom_call" | custom-call | tf_op jit(solution)/shard_map/pallas_call | solution.py:130
  32.1 13.0 %all-to-all-done.1 = bf16[32,8,2048]{2,1,0:T(8,128)(2,1)S(1)} async-done(((bf16[32,8,2048]{2,1,0:T(8,128)(2,1)}), bf16[32,8,2048]{2,1,0:T(8,128)(2,1)S(1)}, u32[]{:S(2)}, u32[]{:S(2)}) %all-to-all-start.1) | async-done | bytes 1048608 | tf_op jit(solution)/shard_map/all_to_all | solution.py:439
  45.1 7.0 %shard_map.194 = (bf16[256,2048]{1,0:T(8,128)(2,1)}, bf16[256,1024]{1,0:T(8,128)(2,1)}, bf16[256,1024]{1,0:T(8,128)(2,1)}, bf16[256,1024]{1,0:T(8,128)(2,1)}, bf...) custom-call(bf16[256,2048]{1,0:T(8,128)(2,1)S(1)} %bitcast.25, ...), custom_call_target="tpu_custom_call" | custom-call | tf_op jit(solution)/shard_map/pallas_call | solution.py:130
  52.1 0.0 copy-start.7
  52.1 6.2 %shard_map.197 = (bf16[4,4,224,256]{3,2,1,0:T(8,128)(2,1)}, bf16[4,4,224,256]{3,2,1,0:T(8,128)(2,1)}, f32[256,1024]{1,0:T(8,128)}) custom-call(bf16[256,1024]{1,0:T(8,128)(2,1)} %get-tuple-element.62.refs_0_, bf16[256,1024]{1,0:T(8,128)(2,1)} %get-tuple-element.63.refs_1_, bf16[1024,256]{1,0:T(8,128)(2,1)} %bitcast.35, ...), custom_call_target="tpu_custom_call" | custom-call | tf_op jit(solution)/shard_map/pallas_call | solution.py:130
  58.3 0.0 copy-start.2
  58.3 0.5 collective-permute-start.2
  58.8 0.0 copy-done.7
  58.8 20.4 %all_to_all.44 = bf16[32,8,2048]{2,1,0:T(8,128)(2,1)S(1)} all-to-all(bf16[32,8,2048]{2,1,0:T(8,128)(2,1)S(1)} %bitcast.46), channel_id=1, replica_groups=mesh['section'=8,'seq'=32] {'seq'}, dimensions={0} | all-to-all | bytes 2097152 | tf_op jit(solution)/shard_map/all_to_all | solution.py:439
  79.2 0.0 copy-start
  79.2 0.0 copy-done.2
  79.2 3.3 %shard_map.196 = (bf16[256,1024]{1,0:T(8,128)(2,1)}, bf16[256,1024]{1,0:T(8,128)(2,1)}) custom-call(bf16[256,2048]{1,0:T(8,128)(2,1)S(1)} %bitcast.23, bf16[256,256]{1,0:T(8,128)(2,1)} %get-tuple-element.57.refs_1_, f32[256,1024]{1,0:T(8,128)} %get-tuple-element.58.refs_2_, bf16[256,1024]{1,0:T(8,128)(2,1)S(1)} %copy-done.2, ...), custom_call_target="tpu_custom_call" | custom-call | tf_op jit(solution)/shard_map/pallas_call | solution.py:130
  82.5 0.0 copy-done
  82.5 4.1 %all-to-all-start.3 = ((bf16[32,8,1024]{2,1,0:T(8,128)(2,1)}), bf16[32,8,1024]{2,1,0:T(8,128)(2,1)S(1)}, u32[]{:S(2)}, u32[]{:S(2)}) async-start(bf16[32,8,1024]{2,1,0:T(8,128)(2,1)} %bitcast.51), calls=%async_computation.3 | async-start | bytes 1048576 | tf_op jit(solution)/shard_map/all_to_all | solution.py:439
  86.5 0.0 collective-permute-done.2.refs_1_
  86.5 3.0 %shard_map.200 = (bf16[4,224,256]{2,1,0:T(8,128)(2,1)}, bf16[4,224,256]{2,1,0:T(8,128)(2,1)}, bf16[4,224,256]{2,1,0:T(8,128)(2,1)}, bf16[4,224,256]{2,1,0:T(8,128)(2,1)}) custom-call(bf16[4,4,224,256]{3,2,1,0:T(8,128)(2,1)} %get-tuple-element.73.refs_0_, bf16[4,4,224,256]{3,2,1,0:T(8,128)(2,1)S(1)} %collective-permute-done.2.refs_1_), custom_call_target="tpu_custom_call" | custom-call | tf_op jit(solution)/shard_map/pallas_call | solution.py:130
  89.5 1.9 %collective-permute-start.3 = (bf16[4,224,256]{2,1,0:T(8,128)(2,1)}, bf16[4,224,256]{2,1,0:T(8,128)(2,1)S(1)}, u32[]{:S(2)}, u32[]{:S(2)}) collective-permute-start(bf16[4,224,256]{2,1,0:T(8,128)(2,1)} %get-tuple-element.76), channel_id=1, source_target_pairs={{0,2},{1,9},{2,4},{3,11},{4,6},{5,13},{6,0},{7,15},{8,10},{9,17},{... | collective-permute-start | bytes 1376264 | tf_op jit(solution)/shard_map/ppermute | solution.py:452
  91.4 2.7 %collective-permute-start.4 = (bf16[4,224,256]{2,1,0:T(8,128)(2,1)}, bf16[4,224,256]{2,1,0:T(8,128)(2,1)S(1)}, u32[]{:S(2)}, u32[]{:S(2)}) collective-permute-start(bf16[4,224,256]{2,1,0:T(8,128)(2,1)} %get-tuple-element.77), channel_id=1, source_target_pairs={{0,4},{1,17},{2,6},{3,19},{4,0},{5,21},{6,2},{7,23},{8,12},{9,25},... | collective-permute-start | bytes 1376264 | tf_op jit(solution)/shard_map/ppermute | solution.py:452
  94.1 1.5 %collective-permute-start.5 = (bf16[4,224,256]{2,1,0:T(8,128)(2,1)}, bf16[4,224,256]{2,1,0:T(8,128)(2,1)S(1)}, u32[]{:S(2)}, u32[]{:S(2)}) collective-permute-start(bf16[4,224,256]{2,1,0:T(8,128)(2,1)} %get-tuple-element.78), channel_id=1, source_target_pairs={{0,6},{1,25},{2,0},{3,27},{4,2},{5,29},{6,4},{7,31},{8,14},{9,1},{... | collective-permute-start | bytes 1376264 | tf_op jit(solution)/shard_map/ppermute | solution.py:452
  95.6 4.3 %shard_map.195 = bf16[256,1024]{1,0:T(8,128)(2,1)S(1)} custom-call(bf16[256,2048]{1,0:T(8,128)(2,1)} %bitcast.24, bf16[256,256]{1,0:T(8,128)(2,1)} %get-tuple-element.50.refs_5_.refs_1_, bf16[256,1024]{1,0:T(8,128)(2,1)} %bitcast.44, f32[1,1024]{1,0:T(1,128)} %refs_3_.3, bf16[1024,256]{1,0:T(8,128)(2,1)} %bitcast.36, f32[1,1024]{1,0:T(1,128)} %refs_5_.1, ...), custom_call_target="tpu_custom_call" | custom-call | tf_op jit(solution)/shard_map/pallas_call | solution.py:130
  99.9 5.0 %collective-permute-start = (bf16[256,1024]{1,0:T(8,128)(2,1)S(1)}, bf16[256,1024]{1,0:T(8,128)(2,1)S(1)}, u32[]{:S(2)}, u32[]{:S(2)}) collective-permute-start(bf16[256,1024]{1,0:T(8,128)(2,1)S(1)} %shard_map.195), channel_id=1, source_target_pairs={{0,32},{32,64},{64,96},{96,128},{128,160},{160,192},{192,224},{1,3... | collective-permute-start | bytes 1572872 | tf_op jit(solution)/shard_map/ppermute | solution.py:457
  104.9 0.0 all-to-all-done.3
  104.9 2.5 %shard_map.198 = bf16[256,1024]{1,0:T(8,128)(2,1)S(1)} custom-call(bf16[256,1024]{1,0:T(8,128)(2,1)S(1)} %bitcast.26, bf16[256,256]{1,0:T(8,128)(2,1)} %get-tuple-element.61.refs_1_, bf16[256,1024]{1,0:T(8,128)(2,1)} %bitcast.30, f32[1,1024]{1,0:T(1,128)} %refs_3_.3, f32[256,1024]{1,0:T(8,128)} %get-tuple-element.68.refs_4_, ...), custom_call_target="tpu_custom_call" | custom-call | tf_op jit(solution)/shard_map/pallas_call | solution.py:130
  107.4 1.9 %collective-permute-start.1 = (bf16[256,1024]{1,0:T(8,128)(2,1)S(1)}, bf16[256,1024]{1,0:T(8,128)(2,1)S(1)}, u32[]{:S(2)}, u32[]{:S(2)}) collective-permute-start(bf16[256,1024]{1,0:T(8,128)(2,1)S(1)} %shard_map.198), channel_id=1, source_target_pairs={{32,0},{64,32},{96,64},{128,96},{160,128},{192,160},{224,192},{33,... | collective-permute-start | bytes 1572872 | tf_op jit(solution)/shard_map/ppermute | solution.py:457
  109.4 0.0 collective-permute-done.3.refs_1_
  109.4 0.0 collective-permute-done.4.refs_2_
  109.4 0.0 collective-permute-done.5.refs_3_
  109.4 1.9 %shard_map.201 = (bf16[224,256]{1,0:T(8,128)(2,1)S(1)}, bf16[224,256]{1,0:T(8,128)(2,1)}, bf16[224,256]{1,0:T(8,128)(2,1)}, bf16[224,256]{1,0:T(8,128)(2,1)}) custom-call(bf16[4,224,256]{2,1,0:T(8,128)(2,1)} %get-tuple-element.75.refs_0_, bf16[4,224,256]{2,1,0:T(8,128)(2,1)S(1)} %collective-permute-done.3.refs_1_, ...), custom_call_target="tpu_custom_call" | custom-call | tf_op jit(solution)/shard_map/pallas_call | solution.py:130
  111.3 0.0 copy-start.5
  111.3 0.6 copy-done.5
  112.0 0.0 copy-start.6
  112.0 1.5 %collective-permute-start.6 = (bf16[224,256]{1,0:T(8,128)(2,1)}, bf16[224,256]{1,0:T(8,128)(2,1)S(1)}, u32[]{:S(2)}, u32[]{:S(2)}) collective-permute-start(bf16[224,256]{1,0:T(8,128)(2,1)} %get-tuple-element.80), channel_id=1, source_target_pairs={{0,8},{1,3},{2,10},{3,5},{4,12},{5,7},{6,14},{7,1},{8,16},{9,11},{... | collective-permute-start | bytes 344072 | tf_op jit(solution)/shard_map/ppermute | solution.py:452
  113.4 2.7 %collective-permute-start.7 = (bf16[224,256]{1,0:T(8,128)(2,1)}, bf16[224,256]{1,0:T(8,128)(2,1)S(1)}, u32[]{:S(2)}, u32[]{:S(2)}) collective-permute-start(bf16[224,256]{1,0:T(8,128)(2,1)} %get-tuple-element.81), channel_id=1, source_target_pairs={{0,16},{1,5},{2,18},{3,7},{4,20},{5,1},{6,22},{7,3},{8,24},{9,13},... | collective-permute-start | bytes 344072 | tf_op jit(solution)/shard_map/ppermute | solution.py:452
  116.2 1.4 %collective-permute-start.8 = (bf16[224,256]{1,0:T(8,128)(2,1)}, bf16[224,256]{1,0:T(8,128)(2,1)S(1)}, u32[]{:S(2)}, u32[]{:S(2)}) collective-permute-start(bf16[224,256]{1,0:T(8,128)(2,1)} %get-tuple-element.82), channel_id=1, source_target_pairs={{0,24},{1,7},{2,26},{3,1},{4,28},{5,3},{6,30},{7,5},{8,0},{9,15},{... | collective-permute-start | bytes 344072 | tf_op jit(solution)/shard_map/ppermute | solution.py:452
  117.6 2.0 %reshape.25 = bf16[1,64,4,1024]{3,2,1,0:T(4,128)(2,1)} reshape(bf16[256,1024]{1,0:T(8,128)(2,1)} %get-tuple-element.72) | data formatting | bytes 1048576 | tf_op jit(solution)/shard_map/reshape | solution.py:552
  119.6 0.0 collective-permute-done.refs_0_
  119.6 3.8 %collective-permute-done.1.refs_1_ = bf16[256,1024]{1,0:T(8,128)(2,1)S(1)} collective-permute-done((bf16[256,1024]{1,0:T(8,128)(2,1)S(1)}, bf16[256,1024]{1,0:T(8,128)(2,1)S(1)}, u32[]{:S(2)}, u32[]{:S(2)}) %collective-permute-start.1) | collective-permute-done | bytes 524320 | tf_op jit(solution)/shard_map/ppermute | solution.py:457
  123.4 1.0 shard_map.199
  124.4 0.0 collective-permute-done.6.refs_1_
  124.4 0.0 collective-permute-done.7.refs_2_
  124.4 0.0 collective-permute-done.8.refs_3_
  124.4 0.0 copy-done.6
  124.4 0.8 shard_map.202
Async XLA Ops:
  0.6 10.1 %copy-start.8 = (bf16[1,64,4,1024]{3,2,1,0:T(4,128)(2,1)S(1)}, bf16[1,64,4,1024]{3,2,1,0:T(4,128)(2,1)}, u32[]{:S(2)}) copy-start(bf16[1,64,4,1024]{3,2,1,0:T(4,128)(2,1)} %param.21) | copy-start | bytes 1572868
  3.4 18.4 %all-to-all-start = ((bf16[32,8,1024]{2,1,0:T(8,128)(2,1)}), bf16[32,8,1024]{2,1,0:T(8,128)(2,1)S(1)}, u32[]{:S(2)}, u32[]{:S(2)}) async-start(bf16[32,8,1024]{2,1,0:T(8,128)(2,1)} %bitcast.45), calls=%async_computation | async-start | bytes 1048576 | tf_op jit(solution)/shard_map/all_to_all | solution.py:439
  10.8 13.3 %copy-start.1 = (bf16[256,1024]{1,0:T(8,128)(2,1)}, bf16[256,1024]{1,0:T(8,128)(2,1)S(1)}, u32[]{:S(2)}) copy-start(bf16[256,1024]{1,0:T(8,128)(2,1)S(1)} %reshape_squeeze.3.refs_2_.refs_6_.refs_3_) | copy-start | bytes 1572868
  16.9 7.3 %copy-start.3 = (bf16[256,256]{1,0:T(8,128)(2,1)}, bf16[256,256]{1,0:T(8,128)(2,1)S(1)}, u32[]{:S(2)}) copy-start(bf16[256,256]{1,0:T(8,128)(2,1)S(1)} %get-tuple-element.47.refs_1_.refs_5_) | copy-start | bytes 393220
  16.9 7.3 %copy-start.4 = (bf16[256,256]{1,0:T(8,128)(2,1)}, bf16[256,256]{1,0:T(8,128)(2,1)S(1)}, u32[]{:S(2)}) copy-start(bf16[256,256]{1,0:T(8,128)(2,1)S(1)} %get-tuple-element.48.refs_3_.refs_7_) | copy-start | bytes 393220
  24.2 20.9 %all-to-all-start.1 = ((bf16[32,8,2048]{2,1,0:T(8,128)(2,1)}), bf16[32,8,2048]{2,1,0:T(8,128)(2,1)S(1)}, u32[]{:S(2)}, u32[]{:S(2)}) async-start(bf16[32,8,2048]{2,1,0:T(8,128)(2,1)} %bitcast.47), calls=%async_computation.1 | async-start | bytes 2097152 | tf_op jit(solution)/shard_map/all_to_all | solution.py:439
  52.1 6.7 %copy-start.7 = (bf16[256,2048]{1,0:T(8,128)(2,1)S(1)}, bf16[256,2048]{1,0:T(8,128)(2,1)}, u32[]{:S(2)}) copy-start(bf16[256,2048]{1,0:T(8,128)(2,1)} %get-tuple-element.56) | copy-start | bytes 3145732
  58.3 20.9 %copy-start.2 = (bf16[256,1024]{1,0:T(8,128)(2,1)S(1)}, bf16[256,1024]{1,0:T(8,128)(2,1)}, u32[]{:S(2)}) copy-start(bf16[256,1024]{1,0:T(8,128)(2,1)} %copy-done.1) | copy-start | bytes 1572868
  58.3 28.2 %collective-permute-start.2 = (bf16[4,4,224,256]{3,2,1,0:T(8,128)(2,1)}, bf16[4,4,224,256]{3,2,1,0:T(8,128)(2,1)S(1)}, u32[]{:S(2)}, u32[]{:S(2)}) collective-permute-start(bf16[4,4,224,256]{3,2,1,0:T(8,128)(2,1)} %get-tuple-element.74), channel_id=1, source_target_pairs={{0,1},{1,0},{2,3},{3,2},{4,5},{5,4},{6,7},{7,6},{8,9},{9,8},{10,11... | collective-permute-start | bytes 5505032 | tf_op jit(solution)/shard_map/ppermute | solution.py:518
  79.2 3.3 %copy-start = (bf16[32,8,2048]{2,1,0:T(8,128)(2,1)}, bf16[32,8,2048]{2,1,0:T(8,128)(2,1)S(1)}, u32[]{:S(2)}) copy-start(bf16[32,8,2048]{2,1,0:T(8,128)(2,1)S(1)} %all_to_all.44) | copy-start | bytes 3145732
  82.5 22.4 %all-to-all-start.3 = ((bf16[32,8,1024]{2,1,0:T(8,128)(2,1)}), bf16[32,8,1024]{2,1,0:T(8,128)(2,1)S(1)}, u32[]{:S(2)}, u32[]{:S(2)}) async-start(bf16[32,8,1024]{2,1,0:T(8,128)(2,1)} %bitcast.51), calls=%async_computation.3 | async-start | bytes 1048576 | tf_op jit(solution)/shard_map/all_to_all | solution.py:439
  89.5 19.8 %collective-permute-start.3 = (bf16[4,224,256]{2,1,0:T(8,128)(2,1)}, bf16[4,224,256]{2,1,0:T(8,128)(2,1)S(1)}, u32[]{:S(2)}, u32[]{:S(2)}) collective-permute-start(bf16[4,224,256]{2,1,0:T(8,128)(2,1)} %get-tuple-element.76), channel_id=1, source_target_pairs={{0,2},{1,9},{2,4},{3,11},{4,6},{5,13},{6,0},{7,15},{8,10},{9,17},{... | collective-permute-start | bytes 1376264 | tf_op jit(solution)/shard_map/ppermute | solution.py:452
  91.4 18.0 %collective-permute-start.4 = (bf16[4,224,256]{2,1,0:T(8,128)(2,1)}, bf16[4,224,256]{2,1,0:T(8,128)(2,1)S(1)}, u32[]{:S(2)}, u32[]{:S(2)}) collective-permute-start(bf16[4,224,256]{2,1,0:T(8,128)(2,1)} %get-tuple-element.77), channel_id=1, source_target_pairs={{0,4},{1,17},{2,6},{3,19},{4,0},{5,21},{6,2},{7,23},{8,12},{9,25},... | collective-permute-start | bytes 1376264 | tf_op jit(solution)/shard_map/ppermute | solution.py:452
  94.1 15.3 %collective-permute-start.5 = (bf16[4,224,256]{2,1,0:T(8,128)(2,1)}, bf16[4,224,256]{2,1,0:T(8,128)(2,1)S(1)}, u32[]{:S(2)}, u32[]{:S(2)}) collective-permute-start(bf16[4,224,256]{2,1,0:T(8,128)(2,1)} %get-tuple-element.78), channel_id=1, source_target_pairs={{0,6},{1,25},{2,0},{3,27},{4,2},{5,29},{6,4},{7,31},{8,14},{9,1},{... | collective-permute-start | bytes 1376264 | tf_op jit(solution)/shard_map/ppermute | solution.py:452
  99.9 19.8 %collective-permute-start = (bf16[256,1024]{1,0:T(8,128)(2,1)S(1)}, bf16[256,1024]{1,0:T(8,128)(2,1)S(1)}, u32[]{:S(2)}, u32[]{:S(2)}) collective-permute-start(bf16[256,1024]{1,0:T(8,128)(2,1)S(1)} %shard_map.195), channel_id=1, source_target_pairs={{0,32},{32,64},{64,96},{96,128},{128,160},{160,192},{192,224},{1,3... | collective-permute-start | bytes 1572872 | tf_op jit(solution)/shard_map/ppermute | solution.py:457
  107.4 15.9 %collective-permute-start.1 = (bf16[256,1024]{1,0:T(8,128)(2,1)S(1)}, bf16[256,1024]{1,0:T(8,128)(2,1)S(1)}, u32[]{:S(2)}, u32[]{:S(2)}) collective-permute-start(bf16[256,1024]{1,0:T(8,128)(2,1)S(1)} %shard_map.198), channel_id=1, source_target_pairs={{32,0},{64,32},{96,64},{128,96},{160,128},{192,160},{224,192},{33,... | collective-permute-start | bytes 1572872 | tf_op jit(solution)/shard_map/ppermute | solution.py:457
  111.3 0.6 copy-start.5
  112.0 12.5 %copy-start.6 = (bf16[224,256]{1,0:T(8,128)(2,1)S(1)}, bf16[224,256]{1,0:T(8,128)(2,1)}, u32[]{:S(2)}) copy-start(bf16[224,256]{1,0:T(8,128)(2,1)} %copy-done.5) | copy-start | bytes 344068
  112.0 12.4 %collective-permute-start.6 = (bf16[224,256]{1,0:T(8,128)(2,1)}, bf16[224,256]{1,0:T(8,128)(2,1)S(1)}, u32[]{:S(2)}, u32[]{:S(2)}) collective-permute-start(bf16[224,256]{1,0:T(8,128)(2,1)} %get-tuple-element.80), channel_id=1, source_target_pairs={{0,8},{1,3},{2,10},{3,5},{4,12},{5,7},{6,14},{7,1},{8,16},{9,11},{... | collective-permute-start | bytes 344072 | tf_op jit(solution)/shard_map/ppermute | solution.py:452
  113.4 11.0 %collective-permute-start.7 = (bf16[224,256]{1,0:T(8,128)(2,1)}, bf16[224,256]{1,0:T(8,128)(2,1)S(1)}, u32[]{:S(2)}, u32[]{:S(2)}) collective-permute-start(bf16[224,256]{1,0:T(8,128)(2,1)} %get-tuple-element.81), channel_id=1, source_target_pairs={{0,16},{1,5},{2,18},{3,7},{4,20},{5,1},{6,22},{7,3},{8,24},{9,13},... | collective-permute-start | bytes 344072 | tf_op jit(solution)/shard_map/ppermute | solution.py:452
  116.2 8.2 %collective-permute-start.8 = (bf16[224,256]{1,0:T(8,128)(2,1)}, bf16[224,256]{1,0:T(8,128)(2,1)S(1)}, u32[]{:S(2)}, u32[]{:S(2)}) collective-permute-start(bf16[224,256]{1,0:T(8,128)(2,1)} %get-tuple-element.82), channel_id=1, source_target_pairs={{0,24},{1,7},{2,26},{3,1},{4,28},{5,3},{6,30},{7,5},{8,0},{9,15},{... | collective-permute-start | bytes 344072 | tf_op jit(solution)/shard_map/ppermute | solution.py:452

commit v4 on v3

--- a/solution.py
+++ b/solution.py
@@ -111,9 +111,11 @@
         at = 0
         for k, i in enumerate(ins_h):
             ins[i] = Lazy(cuts(ins[i], vmem[k], sems, at, in_roles[i], arrays[i].shape), vmem[k])
-            for copy in ins[i].copies:
-                copy.start()
             at += 4
+        for part in range(4):
+            for i in ins_h:
+                for copy in ins[i].copies[part : part + 1]:
+                    copy.start()
         for k, i in enumerate(outs_h, len(ins_h)):
             copies = cuts(vmem[k], results[i], sems, at, out_roles[i], outs[i][0])
             results[i] = Late(copies, vmem[k])
@@ -206,14 +208,18 @@
     send_ref.flush()
 
 
-def k_mid_back(recv_ref, m3t_ref, a2_ref, spec_ref, m2t_ref, da1_ref, sg_ref):
+def k_mid_back(recv_ref, m3t_ref, a2_ref, spec_ref, m2t_ref, da1_ref, sg_ref, df_ref):
     for k in range(4):
         q = cols(k, DB)
-        dfilt = mm(m3t_ref[...], recv_ref[:, q])
-        sg_ref[:, q] = (dfilt * a2_ref[:, q]).astype(BF)
-        da2 = (dfilt * spec_ref[:, q].astype(F32)).astype(BF)
+        df_ref[:, q] = mm(m3t_ref[...], recv_ref[:, q])
+        da2 = (df_ref[:, q] * spec_ref[:, q].astype(F32)).astype(BF)
         da1_ref[:, q] = mm(m2t_ref[...], da2).astype(BF)
         da1_ref.flush(k)
+    for k in range(4):
+        q = cols(k, DB)
+        a2_ref.get(k)
+        sg_ref[:, q] = (df_ref[:, q] * a2_ref.ref[:, q]).astype(BF)
+        sg_ref.flush(k)
 
 
 def cols(b, n):
@@ -322,14 +328,17 @@
 
     copies = []
     for b in range(NB):
-        dgate = dgate_ref[:, cols(b, DB)]
-        put(b, slice(0, 32), mm(n1_ref[:, cols(b, DB)].T, dgate))
-        dn1_ref[:, cols(b, DB)] = mm_nt(dgate, mix_ref[cols(b, DB), :])
-        n2 = n2_ref[:, cols(b, DB)].T
+        for w in (n1_ref, dgate_ref, mix_ref, n2_ref, dup_ref, dact_ref, hs_ref, g_ref):
+            w.get(b)
+        dgate = dgate_ref.ref[:, cols(b, DB)]
+        put(b, slice(0, 32), mm(n1_ref.ref[:, cols(b, DB)].T, dgate))
+        dn1_ref[:, cols(b, DB)] = mm_nt(dgate, mix_ref.ref[cols(b, DB), :])
+        dn1_ref.flush(b)
+        n2 = n2_ref.ref[:, cols(b, DB)].T
         for k in range(2):
-            put(b, slice(32 + 32 * k, 64 + 32 * k), mm(n2, dup_ref[:, cols(2 * b + k, DB)]))
-            put(b, slice(96 + 32 * k, 128 + 32 * k), mm(n2, dact_ref[:, cols(2 * b + k, DB)]))
-        put(b, slice(160, 224), mm(hs_ref[:, cols(b, HB)].T, g_ref[:, cols(b, DB)]))
+            put(b, slice(32 + 32 * k, 64 + 32 * k), mm(n2, dup_ref.ref[:, cols(2 * b + k, DB)]))
+            put(b, slice(96 + 32 * k, 128 + 32 * k), mm(n2, dact_ref.ref[:, cols(2 * b + k, DB)]))
+        put(b, slice(160, 224), mm(hs_ref.ref[:, cols(b, HB)].T, g_ref.ref[:, cols(b, DB)]))
         for side, out in enumerate((keep_ref, send_ref)):
             copy = pltpu.make_async_copy(buf_ref.at[side, b], out.at[b], sems.at[2 * b + side])
             copy.start()
@@ -343,7 +352,7 @@
     return i & 1, i >> 3, (i >> 1) & 3
 
 
-def k_sum_core(keep_ref, recv_ref, *outs):
+def k_sum_core(keep_ref, recv_ref, m3t_ref, m2t_ref, *outs):
     core, x, y = ring_slots()
     keep = keep_ref.get()
     for d in range(4):
@@ -352,6 +361,8 @@
             iy = jnp.where(core == 0, (y + d) & 3, k)
             outs[d][k] = (keep[ix, iy].astype(F32) + recv_ref[ix, iy].astype(F32)).astype(BF)
         outs[d].flush()
+    outs[4][...] = m3t_ref[...]
+    outs[5][...] = m2t_ref[...]
 
 
 def k_sum_ring(a_ref, b_ref, c_ref, d_ref, *outs):
@@ -361,6 +372,7 @@
         outs[d][...] = (
             a_ref[k].astype(F32) + b_ref[k].astype(F32) + c_ref[k].astype(F32) + d_ref[k].astype(F32)
         ).astype(BF)
+    outs[0].flush()
 
 
 def k_sum_x(a_ref, b_ref, c_ref, d_ref, mix_ref, up_ref, act_ref, down_ref):
@@ -376,15 +388,22 @@
     down_ref[...] = total(slice(160, 224))
 
 
-def k_place(a_ref, b_ref, a_out, b_out, sems):
-    copies = [
-        pltpu.make_async_copy(a_ref, a_out.at[0], sems.at[0]),
-        pltpu.make_async_copy(b_ref, b_out.at[0], sems.at[1]),
-    ]
-    for copy in copies:
-        copy.start()
-    for copy in copies:
-        copy.wait()
+def k_place(a_ref, b_ref, a_out, b_out, zero_ref, sems):
+    section = lax.axis_index("section")
+    ends = ((a_ref, a_out, 0), (b_ref, b_out, lax.axis_size("section") - 1))
+    for k, (src, out, end) in enumerate(ends):
+
+        @pl.when(section != end)
+        def _():
+            pltpu.make_async_copy(src, out.at[0], sems.at[k]).start()
+
+        @pl.when(section == end)
+        def _():
+            zero_ref[...] = jnp.zeros_like(zero_ref)
+            pltpu.make_async_copy(zero_ref, out.at[0], sems.at[k]).start()
+
+    for k, (src, out, end) in enumerate(ends):
+        pltpu.make_async_copy(src, out.at[0], sems.at[k]).wait()
 
 
 def k_tail(recv_ref, m4_ref, x_ref, gain1_ref, mix_ref, gain2_ref, up_ref, act_ref, down_ref,
@@ -454,7 +473,8 @@
 
 def shift(v, by):
     n = lax.axis_size("section")
-    return lax.ppermute(v, "section", [(i, i + by) for i in range(n) if 0 <= i + by < n])
+    pairs = [(i, (i + by) % n) for i in range(n) if by > 0 or i + by >= 0]
+    return lax.ppermute(v, "section", pairs)
 
 
 def shards(xa, xb, g, gain1, gain2, first, second, spec, third, fourth, mix, up, act, down):
@@ -511,16 +531,20 @@
     r3 = swap(send3)
     keep, other, dn1 = call(
         k_grads,
-        [((4, 4, GR, DB), BF, "r"), ((4, 4, GR, DB), BF, "r"), (td, F32, "h")],
-        *h(n1b, dgate, mix, n2, dup, dact, hs, g),
+        [((4, 4, GR, DB), BF, "r"), ((4, 4, GR, DB), BF, "r"), (td, F32, "c")],
+        *((w, "x" if w is mix else "c") for w in (n1b, dgate, mix, n2, dup, dact, hs, g)),
         scratch=[pltpu.VMEM((2, 4, 4, GR, DB), BF), pltpu.SemaphoreType.DMA((8,))],
     )
     other = lax.ppermute(other, "seq", [(i, i ^ 1) for i in range(32)])
-    s0, *sy = call(k_sum_core, [((4, GR, DB), BF, "h")] * 4, *h(keep), *v(other))
+    s0, *sy, m3t, m2t = call(
+        k_sum_core, [((4, GR, DB), BF, "h")] * 4 + [(tt, BF, "v")] * 2,
+        *h(keep), *v(other), *h(m3t, m2t),
+    )
     for d in (1, 3, 2):
         sy[d - 1] = ring(sy[d - 1], ring_y, ring_x, d)
     da1, sgrad = call(
-        k_mid_back, [(td, BF, "c"), (td, BF, "h")], *v(r3), *h(m3t, a2b), *v(spec), *h(m2t)
+        k_mid_back, [(td, BF, "c")] * 2, *v(r3, m3t), (a2b, "c"), *v(spec, m2t),
+        scratch=[pltpu.VMEM(td, F32)],
     )
     r4 = swap(da1)
     (outa,) = call(
@@ -535,16 +559,16 @@
         scratch=[pltpu.VMEM(td, F32)],
     )
     upstream = shift(dx, -1)
-    s0, *sx = call(k_sum_ring, [((GR, DB), BF, "v")] * 4, *h(s0), *v(*sy))
+    s0, *sx = call(k_sum_ring, [((GR, DB), BF, r) for r in "hvvv"], *h(s0), *v(*sy))
     sx = [ring(p, ring_x, ring_y, d + 1) for d, p in enumerate(sx)]
     gm, gu, ga, gd = call(
         k_sum_x,
         [((32, DB), BF, "h"), ((32, HB), BF, "h"), ((32, HB), BF, "h"), ((64, DB), BF, "h")],
-        *v(s0, *sx),
+        *h(s0), *v(*sx),
     )
     next_input, upstream = call(
         k_place, [((1, T, D), BF, "r")] * 2, *v(next_input, upstream),
-        scratch=[pltpu.SemaphoreType.DMA((2,))],
+        scratch=[pltpu.VMEM(td, BF), pltpu.SemaphoreType.DMA((2,))],
     )
     return (
         next_input,

time: 126 us -> 121 us (0.960)
  the two profiles are of different devices: /device:TPU:96 before, /device:TPU:1 now
where the time goes in v4:
time: 121 us; the launch traced here: 120 us
  Pallas kernels  44.3 us (37%)
  waiting for transfers between devices  37.4 us (31%)
  starting transfers between devices  33 us (27%)
  local copies, waits for them, and re-layouts  3.85 us (3%)
    pallas_call x14, Pallas kernels, call(): pl.pallas_call(body, out_shape=[(jax.ShapeDtypeStruct if o[2] == 'v' else...  44.3 us
    all_to_all x4, waiting for transfers between devices, swap(): return lax.all_to_all(v, 'seq', split_axis=0, concat_axis=0, tiled=True)  32.4 us
    all_to_all x4, starting transfers between devices, swap(): return lax.all_to_all(v, 'seq', split_axis=0, concat_axis=0, tiled=True)  20.2 us
    ppermute x6, starting transfers between devices, ring(): return lax.ppermute(value, 'seq', pairs)  9.57 us
    ppermute x6, waiting for transfers between devices, ring(): return lax.ppermute(value, 'seq', pairs)  4.96 us
    ppermute x2, starting transfers between devices, shift(): return lax.ppermute(v, 'section', pairs)  3 us
  transfers between devices with their start and end apart: 13, of which 7 were waited for; matrix products, arithmetic and copies ran while one was open for 2% of the time, Pallas kernels for 20%

profile of v4, /device:TPU:1, one launch (start us, length us, event | category | flops | bytes accessed | tf_op | source)
XLA Modules:
  0.0 119.6 jit_solution(18111537639833585593)
XLA Ops:
  0.6 0.0 copy-start.7
  0.6 2.7 %shard_map.189 = bf16[256,1024]{1,0:T(8,128)(2,1)} custom-call(bf16[2,128,128]{2,1,0:T(8,128)(2,1)} %bitcast.48, bf16[256,1024]{1,0:T(8,128)(2,1)} %bitcast.28, f32[1,1024]{1,0:T(1,128)} %refs_3_.3), custom_call_target="tpu_custom_call" | custom-call | tf_op jit(solution)/shard_map/pallas_call | solution.py:132
  3.3 8.6 %all-to-all-start = ((bf16[32,8,1024]{2,1,0:T(8,128)(2,1)}), bf16[32,8,1024]{2,1,0:T(8,128)(2,1)S(1)}, u32[]{:S(2)}, u32[]{:S(2)}) async-start(bf16[32,8,1024]{2,1,0:T(8,128)(2,1)} %bitcast.45), calls=%async_computation | async-start | bytes 1048576 | tf_op jit(solution)/shard_map/all_to_all | solution.py:458
  11.9 2.6 %shard_map.191.refs_4_ = bf16[256,1024]{1,0:T(8,128)(2,1)} custom-call(bf16[2,128,128]{2,1,0:T(8,128)(2,1)} %bitcast.49, bf16[256,1024]{1,0:T(8,128)(2,1)} %bitcast.43, f32[1,1024]{1,0:T(1,128)} %refs_3_.3), custom_call_target="tpu_custom_call" | custom-call | tf_op jit(solution)/shard_map/pallas_call | solution.py:132
  14.6 0.0 copy-done.7
  14.6 0.1 reshape_squeeze.3.refs_2_.refs_6_.refs_3_
  14.7 0.0 copy-start.1
  14.7 3.3 %shard_map.190 = (bf16[256,256]{1,0:T(8,128)(2,1)}, bf16[256,256]{1,0:T(8,128)(2,1)S(1)}, bf16[256,256]{1,0:T(8,128)(2,1)}, bf16[256,256]{1,0:T(8,128)(2,1)S(1)}...) custom-call(bf16[2,128,128]{2,1,0:T(8,128)(2,1)} %bitcast.50, ...), custom_call_target="tpu_custom_call" | custom-call | tf_op jit(solution)/shard_map/pallas_call | solution.py:132
  18.1 0.0 copy-start.3
  18.1 0.0 copy-start.4
  18.1 5.5 %all-to-all-done = bf16[32,8,1024]{2,1,0:T(8,128)(2,1)S(1)} async-done(((bf16[32,8,1024]{2,1,0:T(8,128)(2,1)}), bf16[32,8,1024]{2,1,0:T(8,128)(2,1)S(1)}, u32[]{:S(2)}, u32[]{:S(2)}) %all-to-all-start) | async-done | bytes 524320 | tf_op jit(solution)/shard_map/all_to_all | solution.py:458
  23.5 2.4 %shard_map.192 = (bf16[256,2048]{1,0:T(8,128)(2,1)}, f32[256,1024]{1,0:T(8,128)}) custom-call(bf16[256,1024]{1,0:T(8,128)(2,1)S(1)} %bitcast.27, bf16[256,256]{1,0:T(8,128)(2,1)S(1)} %get-tuple-element.49.refs_1_.refs_5_, bf16[256,1024]{1,0:T(8,128)(2,1)S(1)} %reshape_squeeze.3.refs_2_.refs_6_.refs_3_, ...), custom_call_target="tpu_custom_call" | custom-call | tf_op jit(solution)/shard_map/pallas_call | solution.py:132
  25.9 0.0 copy-done.1
  25.9 0.0 copy-done.3
  25.9 0.0 copy-done.4
  25.9 3.7 %all-to-all-start.1 = ((bf16[32,8,2048]{2,1,0:T(8,128)(2,1)}), bf16[32,8,2048]{2,1,0:T(8,128)(2,1)S(1)}, u32[]{:S(2)}, u32[]{:S(2)}) async-start(bf16[32,8,2048]{2,1,0:T(8,128)(2,1)} %bitcast.47), calls=%async_computation.1 | async-start | bytes 2097152 | tf_op jit(solution)/shard_map/all_to_all | solution.py:458
  29.7 3.8 %shard_map.193 = (bf16[256,1024]{1,0:T(8,128)(2,1)}, f32[256,1024]{1,0:T(8,128)S(1)}, bf16[256,2048]{1,0:T(8,128)(2,1)}, bf16[256,1024]{1,0:T(8,128)(2,1)S(1)}, bf16[256,256]{1,0:T(8,128)(2,1)S(1)}) custom-call(bf16[256,1024]{1,0:T(8,128)(2,1)} %bitcast.29, f32[1,1024]{1,0:T(1,128)} %refs_3_.3, bf16[1024,256]{1,0:T(8,128)(2,1)} %bitcast.34, ...), custom_call_target="tpu_custom_call" | custom-call | tf_op jit(solution)/shard_map/pallas_call | solution.py:132
  33.5 13.0 %all-to-all-done.1 = bf16[32,8,2048]{2,1,0:T(8,128)(2,1)S(1)} async-done(((bf16[32,8,2048]{2,1,0:T(8,128)(2,1)}), bf16[32,8,2048]{2,1,0:T(8,128)(2,1)S(1)}, u32[]{:S(2)}, u32[]{:S(2)}) %all-to-all-start.1) | async-done | bytes 1048608 | tf_op jit(solution)/shard_map/all_to_all | solution.py:458
  46.5 7.0 %shard_map.194 = (bf16[256,2048]{1,0:T(8,128)(2,1)}, bf16[256,1024]{1,0:T(8,128)(2,1)}, bf16[256,1024]{1,0:T(8,128)(2,1)}, bf16[256,1024]{1,0:T(8,128)(2,1)}, bf...) custom-call(bf16[256,2048]{1,0:T(8,128)(2,1)S(1)} %bitcast.25, ...), custom_call_target="tpu_custom_call" | custom-call | tf_op jit(solution)/shard_map/pallas_call | solution.py:132
  53.5 4.9 %shard_map.196 = (bf16[4,4,224,256]{3,2,1,0:T(8,128)(2,1)}, bf16[4,4,224,256]{3,2,1,0:T(8,128)(2,1)}, f32[256,1024]{1,0:T(8,128)}) custom-call(bf16[256,1024]{1,0:T(8,128)(2,1)} %get-tuple-element.59.refs_0_, bf16[256,1024]{1,0:T(8,128)(2,1)} %get-tuple-element.60.refs_1_, bf16[1024,256]{1,0:T(8,128)(2,1)} %bitcast.35, ...), custom_call_target="tpu_custom_call" | custom-call | tf_op jit(solution)/shard_map/pallas_call | solution.py:132
  58.3 0.2 collective-permute-start.1
  58.5 4.0 %all-to-all-start.2 = ((bf16[32,8,2048]{2,1,0:T(8,128)(2,1)}), bf16[32,8,2048]{2,1,0:T(8,128)(2,1)S(1)}, u32[]{:S(2)}, u32[]{:S(2)}) async-start(bf16[32,8,2048]{2,1,0:T(8,128)(2,1)} %bitcast.46), calls=%async_computation.2 | async-start | bytes 2097152 | tf_op jit(solution)/shard_map/all_to_all | solution.py:458
  62.5 0.0 collective-permute-done.1.refs_1_
  62.6 0.0 copy-start.2
  62.6 3.1 %shard_map.197 = (bf16[4,224,256]{2,1,0:T(8,128)(2,1)}, bf16[4,224,256]{2,1,0:T(8,128)(2,1)}, bf16[4,224,256]{2,1,0:T(8,128)(2,1)}, bf16[4,224,256]{2,1,0:T(8,12...) custom-call(bf16[4,4,224,256]{3,2,1,0:T(8,128)(2,1)} %get-tuple-element.65.refs_0_, ...), custom_call_target="tpu_custom_call" | custom-call | tf_op jit(solution)/shard_map/pallas_call | solution.py:132
  65.7 0.0 copy-start.5
  65.7 0.6 copy-done.5
  66.4 13.2 %all-to-all-done.2 = bf16[32,8,2048]{2,1,0:T(8,128)(2,1)S(1)} async-done(((bf16[32,8,2048]{2,1,0:T(8,128)(2,1)}), bf16[32,8,2048]{2,1,0:T(8,128)(2,1)S(1)}, u32[]{:S(2)}, u32[]{:S(2)}) %all-to-all-start.2) | async-done | bytes 1048608 | tf_op jit(solution)/shard_map/all_to_all | solution.py:458
  79.5 0.0 copy-start
  79.5 0.0 copy-done.2
  79.5 0.0 copy-start.6
  79.5 1.0 copy-done.6
  80.6 2.4 %shard_map.198 = (bf16[256,1024]{1,0:T(8,128)(2,1)}, bf16[256,1024]{1,0:T(8,128)(2,1)}) custom-call(bf16[256,2048]{1,0:T(8,128)(2,1)S(1)} %bitcast.23, bf16[256,256]{1,0:T(8,128)(2,1)S(1)} %get-tuple-element.69.refs_1_, f32[256,1024]{1,0:T(8,128)} %get-tuple-element.70.refs_2_, bf16[256,1024]{1,0:T(8,128)(2,1)S(1)} %copy-done.2, bf16[256,256]{1,0:T(8,128)(2,1)S(1)} %copy-done.6), custom_call_target="tpu_custom_call" | custom-call | tf_op jit(solution)/shard_map/pallas_call | solution.py:132
  82.9 0.0 copy-done
  83.0 3.9 %all-to-all-start.3 = ((bf16[32,8,1024]{2,1,0:T(8,128)(2,1)}), bf16[32,8,1024]{2,1,0:T(8,128)(2,1)S(1)}, u32[]{:S(2)}, u32[]{:S(2)}) async-start(bf16[32,8,1024]{2,1,0:T(8,128)(2,1)} %bitcast.51), calls=%async_computation.3 | async-start | bytes 1048576 | tf_op jit(solution)/shard_map/all_to_all | solution.py:458
  86.9 1.4 %collective-permute-start.3 = (bf16[4,224,256]{2,1,0:T(8,128)(2,1)}, bf16[4,224,256]{2,1,0:T(8,128)(2,1)S(1)}, u32[]{:S(2)}, u32[]{:S(2)}) collective-permute-start(bf16[4,224,256]{2,1,0:T(8,128)(2,1)} %get-tuple-element.80), channel_id=1, source_target_pairs={{0,2},{1,9},{2,4},{3,11},{4,6},{5,13},{6,0},{7,15},{8,10},{9,17},{... | collective-permute-start | bytes 1376264 | tf_op jit(solution)/shard_map/ppermute | solution.py:471
  88.3 2.4 %collective-permute-start.4 = (bf16[4,224,256]{2,1,0:T(8,128)(2,1)}, bf16[4,224,256]{2,1,0:T(8,128)(2,1)S(1)}, u32[]{:S(2)}, u32[]{:S(2)}) collective-permute-start(bf16[4,224,256]{2,1,0:T(8,128)(2,1)} %get-tuple-element.81), channel_id=1, source_target_pairs={{0,4},{1,17},{2,6},{3,19},{4,0},{5,21},{6,2},{7,23},{8,12},{9,25},... | collective-permute-start | bytes 1376264 | tf_op jit(solution)/shard_map/ppermute | solution.py:471
  90.8 1.1 collective-permute-start.5
  91.9 4.3 %shard_map.195 = bf16[256,1024]{1,0:T(8,128)(2,1)S(1)} custom-call(bf16[256,2048]{1,0:T(8,128)(2,1)} %bitcast.24, bf16[256,256]{1,0:T(8,128)(2,1)} %get-tuple-element.52.refs_5_.refs_1_, bf16[256,1024]{1,0:T(8,128)(2,1)} %bitcast.44, f32[1,1024]{1,0:T(1,128)} %refs_3_.3, bf16[1024,256]{1,0:T(8,128)(2,1)} %bitcast.36, f32[1,1024]{1,0:T(1,128)} %refs_5_.1, ...), custom_call_target="tpu_custom_call" | custom-call | tf_op jit(solution)/shard_map/pallas_call | solution.py:132
  96.2 1.7 %collective-permute-start = (bf16[256,1024]{1,0:T(8,128)(2,1)S(1)}, bf16[256,1024]{1,0:T(8,128)(2,1)S(1)}, u32[]{:S(2)}, u32[]{:S(2)}) collective-permute-start(bf16[256,1024]{1,0:T(8,128)(2,1)S(1)} %shard_map.195), channel_id=1, source_target_pairs={{0,32},{32,64},{64,96},{96,128},{128,160},{160,192},{192,224},{224... | collective-permute-start | bytes 1572872 | tf_op jit(solution)/shard_map/ppermute | solution.py:477
  97.9 0.8 all-to-all-done.3
  98.7 2.5 %shard_map.199 = bf16[256,1024]{1,0:T(8,128)(2,1)S(1)} custom-call(bf16[256,1024]{1,0:T(8,128)(2,1)S(1)} %bitcast.26, bf16[256,256]{1,0:T(8,128)(2,1)} %get-tuple-element.73.refs_1_, bf16[256,1024]{1,0:T(8,128)(2,1)} %bitcast.30, f32[1,1024]{1,0:T(1,128)} %refs_3_.3, f32[256,1024]{1,0:T(8,128)} %get-tuple-element.74.refs_4_, ...), custom_call_target="tpu_custom_call" | custom-call | tf_op jit(solution)/shard_map/pallas_call | solution.py:132
  101.2 1.3 %collective-permute-start.2 = (bf16[256,1024]{1,0:T(8,128)(2,1)S(1)}, bf16[256,1024]{1,0:T(8,128)(2,1)S(1)}, u32[]{:S(2)}, u32[]{:S(2)}) collective-permute-start(bf16[256,1024]{1,0:T(8,128)(2,1)S(1)} %shard_map.199), channel_id=1, source_target_pairs={{32,0},{64,32},{96,64},{128,96},{160,128},{192,160},{224,192},{33,... | collective-permute-start | bytes 1572872 | tf_op jit(solution)/shard_map/ppermute | solution.py:477
  102.5 0.0 collective-permute-done.3.refs_1_
  102.5 4.0 %collective-permute-done.4.refs_2_ = bf16[4,224,256]{2,1,0:T(8,128)(2,1)S(1)} collective-permute-done((bf16[4,224,256]{2,1,0:T(8,128)(2,1)}, bf16[4,224,256]{2,1,0:T(8,128)(2,1)S(1)}, u32[]{:S(2)}, u32[]{:S(2)}) %collective-permute-start.4) | collective-permute-done | bytes 458784 | tf_op jit(solution)/shard_map/ppermute | solution.py:471
  106.5 0.0 collective-permute-done.5.refs_3_
  106.5 2.5 %shard_map.201 = (bf16[224,256]{1,0:T(8,128)(2,1)}, bf16[224,256]{1,0:T(8,128)(2,1)}, bf16[224,256]{1,0:T(8,128)(2,1)}, bf16[224,256]{1,0:T(8,128)(2,1)}) custom-call(bf16[4,224,256]{2,1,0:T(8,128)(2,1)} %get-tuple-element.79.refs_0_, bf16[4,224,256]{2,1,0:T(8,128)(2,1)S(1)} %collective-permute-done.3.refs_1_, ...), custom_call_target="tpu_custom_call" | custom-call | tf_op jit(solution)/shard_map/pallas_call | solution.py:132
  109.1 1.0 collective-permute-start.6
  110.0 2.4 %collective-permute-start.7 = (bf16[224,256]{1,0:T(8,128)(2,1)}, bf16[224,256]{1,0:T(8,128)(2,1)S(1)}, u32[]{:S(2)}, u32[]{:S(2)}) collective-permute-start(bf16[224,256]{1,0:T(8,128)(2,1)} %get-tuple-element.85), channel_id=1, source_target_pairs={{0,16},{1,5},{2,18},{3,7},{4,20},{5,1},{6,22},{7,3},{8,24},{9,13},... | collective-permute-start | bytes 344072 | tf_op jit(solution)/shard_map/ppermute | solution.py:471
  112.5 1.2 collective-permute-start.8
  113.6 2.0 %reshape.25 = bf16[1,64,4,1024]{3,2,1,0:T(4,128)(2,1)} reshape(bf16[256,1024]{1,0:T(8,128)(2,1)} %get-tuple-element.78) | data formatting | bytes 1048576 | tf_op jit(solution)/shard_map/reshape | solution.py:576
  115.7 0.0 collective-permute-done.6.refs_1_
  115.7 0.7 collective-permute-done.7.refs_2_
  116.4 0.2 collective-permute-done.8.refs_3_
  116.6 1.8 %shard_map.202 = (bf16[32,256]{1,0:T(8,128)(2,1)}, bf16[32,512]{1,0:T(8,128)(2,1)}, bf16[32,512]{1,0:T(8,128)(2,1)}, bf16[64,256]{1,0:T(8,128)(2,1)}) custom-call(bf16[224,256]{1,0:T(8,128)(2,1)} %get-tuple-element.83.refs_0_, bf16[224,256]{1,0:T(8,128)(2,1)S(1)} %collective-permute-done.6.refs_1_, bf16[224,256]{1,0:T(8,128)(2,1)S(1)} %collective-permute-done.7.refs_2_, ...), custom_call_target="tpu_custom_call" | custom-call | tf_op jit(solution)/shard_map/pallas_call | solution.py:132
  118.4 0.0 collective-permute-done.refs_0_
  118.4 0.0 collective-permute-done.2.refs_1_
  118.4 1.1 shard_map.200
Async XLA Ops:
  0.6 14.0 %copy-start.7 = (bf16[1,64,4,1024]{3,2,1,0:T(4,128)(2,1)S(1)}, bf16[1,64,4,1024]{3,2,1,0:T(4,128)(2,1)}, u32[]{:S(2)}) copy-start(bf16[1,64,4,1024]{3,2,1,0:T(4,128)(2,1)} %param.21) | copy-start | bytes 1572868
  3.3 20.2 %all-to-all-start = ((bf16[32,8,1024]{2,1,0:T(8,128)(2,1)}), bf16[32,8,1024]{2,1,0:T(8,128)(2,1)S(1)}, u32[]{:S(2)}, u32[]{:S(2)}) async-start(bf16[32,8,1024]{2,1,0:T(8,128)(2,1)} %bitcast.45), calls=%async_computation | async-start | bytes 1048576 | tf_op jit(solution)/shard_map/all_to_all | solution.py:458
  14.7 11.2 %copy-start.1 = (bf16[256,1024]{1,0:T(8,128)(2,1)}, bf16[256,1024]{1,0:T(8,128)(2,1)S(1)}, u32[]{:S(2)}) copy-start(bf16[256,1024]{1,0:T(8,128)(2,1)S(1)} %reshape_squeeze.3.refs_2_.refs_6_.refs_3_) | copy-start | bytes 1572868
  18.1 7.9 %copy-start.3 = (bf16[256,256]{1,0:T(8,128)(2,1)}, bf16[256,256]{1,0:T(8,128)(2,1)S(1)}, u32[]{:S(2)}) copy-start(bf16[256,256]{1,0:T(8,128)(2,1)S(1)} %get-tuple-element.49.refs_1_.refs_5_) | copy-start | bytes 393220
  18.1 7.9 %copy-start.4 = (bf16[256,256]{1,0:T(8,128)(2,1)}, bf16[256,256]{1,0:T(8,128)(2,1)S(1)}, u32[]{:S(2)}) copy-start(bf16[256,256]{1,0:T(8,128)(2,1)S(1)} %get-tuple-element.50.refs_3_.refs_7_) | copy-start | bytes 393220
  25.9 20.5 %all-to-all-start.1 = ((bf16[32,8,2048]{2,1,0:T(8,128)(2,1)}), bf16[32,8,2048]{2,1,0:T(8,128)(2,1)S(1)}, u32[]{:S(2)}, u32[]{:S(2)}) async-start(bf16[32,8,2048]{2,1,0:T(8,128)(2,1)} %bitcast.47), calls=%async_computation.1 | async-start | bytes 2097152 | tf_op jit(solution)/shard_map/all_to_all | solution.py:458
  58.3 4.2 %collective-permute-start.1 = (bf16[4,4,224,256]{3,2,1,0:T(8,128)(2,1)}, bf16[4,4,224,256]{3,2,1,0:T(8,128)(2,1)S(1)}, u32[]{:S(2)}, u32[]{:S(2)}) collective-permute-start(bf16[4,4,224,256]{3,2,1,0:T(8,128)(2,1)} %get-tuple-element.66), channel_id=1, source_target_pairs={{0,1},{1,0},{2,3},{3,2},{4,5},{5,4},{6,7},{7,6},{8,9},{9,8},{10,11... | collective-permute-start | bytes 5505032 | tf_op jit(solution)/shard_map/ppermute | solution.py:538
  58.5 21.0 %all-to-all-start.2 = ((bf16[32,8,2048]{2,1,0:T(8,128)(2,1)}), bf16[32,8,2048]{2,1,0:T(8,128)(2,1)S(1)}, u32[]{:S(2)}, u32[]{:S(2)}) async-start(bf16[32,8,2048]{2,1,0:T(8,128)(2,1)} %bitcast.46), calls=%async_computation.2 | async-start | bytes 2097152 | tf_op jit(solution)/shard_map/all_to_all | solution.py:458
  62.6 17.0 %copy-start.2 = (bf16[256,1024]{1,0:T(8,128)(2,1)S(1)}, bf16[256,1024]{1,0:T(8,128)(2,1)}, u32[]{:S(2)}) copy-start(bf16[256,1024]{1,0:T(8,128)(2,1)} %copy-done.1) | copy-start | bytes 1572868
  65.7 0.7 copy-start.5
  79.5 3.4 %copy-start = (bf16[32,8,2048]{2,1,0:T(8,128)(2,1)}, bf16[32,8,2048]{2,1,0:T(8,128)(2,1)S(1)}, u32[]{:S(2)}) copy-start(bf16[32,8,2048]{2,1,0:T(8,128)(2,1)S(1)} %all-to-all-done.2) | copy-start | bytes 3145732
  79.5 1.0 copy-start.6
  83.0 15.7 %all-to-all-start.3 = ((bf16[32,8,1024]{2,1,0:T(8,128)(2,1)}), bf16[32,8,1024]{2,1,0:T(8,128)(2,1)S(1)}, u32[]{:S(2)}, u32[]{:S(2)}) async-start(bf16[32,8,1024]{2,1,0:T(8,128)(2,1)} %bitcast.51), calls=%async_computation.3 | async-start | bytes 1048576 | tf_op jit(solution)/shard_map/all_to_all | solution.py:458
  86.9 15.6 %collective-permute-start.3 = (bf16[4,224,256]{2,1,0:T(8,128)(2,1)}, bf16[4,224,256]{2,1,0:T(8,128)(2,1)S(1)}, u32[]{:S(2)}, u32[]{:S(2)}) collective-permute-start(bf16[4,224,256]{2,1,0:T(8,128)(2,1)} %get-tuple-element.80), channel_id=1, source_target_pairs={{0,2},{1,9},{2,4},{3,11},{4,6},{5,13},{6,0},{7,15},{8,10},{9,17},{... | collective-permute-start | bytes 1376264 | tf_op jit(solution)/shard_map/ppermute | solution.py:471
  88.3 18.2 %collective-permute-start.4 = (bf16[4,224,256]{2,1,0:T(8,128)(2,1)}, bf16[4,224,256]{2,1,0:T(8,128)(2,1)S(1)}, u32[]{:S(2)}, u32[]{:S(2)}) collective-permute-start(bf16[4,224,256]{2,1,0:T(8,128)(2,1)} %get-tuple-element.81), channel_id=1, source_target_pairs={{0,4},{1,17},{2,6},{3,19},{4,0},{5,21},{6,2},{7,23},{8,12},{9,25},... | collective-permute-start | bytes 1376264 | tf_op jit(solution)/shard_map/ppermute | solution.py:471
  90.8 15.8 %collective-permute-start.5 = (bf16[4,224,256]{2,1,0:T(8,128)(2,1)}, bf16[4,224,256]{2,1,0:T(8,128)(2,1)S(1)}, u32[]{:S(2)}, u32[]{:S(2)}) collective-permute-start(bf16[4,224,256]{2,1,0:T(8,128)(2,1)} %get-tuple-element.82), channel_id=1, source_target_pairs={{0,6},{1,25},{2,0},{3,27},{4,2},{5,29},{6,4},{7,31},{8,14},{9,1},{... | collective-permute-start | bytes 1376264 | tf_op jit(solution)/shard_map/ppermute | solution.py:471
  96.2 22.2 %collective-permute-start = (bf16[256,1024]{1,0:T(8,128)(2,1)S(1)}, bf16[256,1024]{1,0:T(8,128)(2,1)S(1)}, u32[]{:S(2)}, u32[]{:S(2)}) collective-permute-start(bf16[256,1024]{1,0:T(8,128)(2,1)S(1)} %shard_map.195), channel_id=1, source_target_pairs={{0,32},{32,64},{64,96},{96,128},{128,160},{160,192},{192,224},{224... | collective-permute-start | bytes 1572872 | tf_op jit(solution)/shard_map/ppermute | solution.py:477
  101.2 17.2 %collective-permute-start.2 = (bf16[256,1024]{1,0:T(8,128)(2,1)S(1)}, bf16[256,1024]{1,0:T(8,128)(2,1)S(1)}, u32[]{:S(2)}, u32[]{:S(2)}) collective-permute-start(bf16[256,1024]{1,0:T(8,128)(2,1)S(1)} %shard_map.199), channel_id=1, source_target_pairs={{32,0},{64,32},{96,64},{128,96},{160,128},{192,160},{224,192},{33,... | collective-permute-start | bytes 1572872 | tf_op jit(solution)/shard_map/ppermute | solution.py:477
  109.1 6.6 %collective-permute-start.6 = (bf16[224,256]{1,0:T(8,128)(2,1)}, bf16[224,256]{1,0:T(8,128)(2,1)S(1)}, u32[]{:S(2)}, u32[]{:S(2)}) collective-permute-start(bf16[224,256]{1,0:T(8,128)(2,1)} %get-tuple-element.84), channel_id=1, source_target_pairs={{0,8},{1,3},{2,10},{3,5},{4,12},{5,7},{6,14},{7,1},{8,16},{9,11},{... | collective-permute-start | bytes 344072 | tf_op jit(solution)/shard_map/ppermute | solution.py:471
  110.0 6.3 %collective-permute-start.7 = (bf16[224,256]{1,0:T(8,128)(2,1)}, bf16[224,256]{1,0:T(8,128)(2,1)S(1)}, u32[]{:S(2)}, u32[]{:S(2)}) collective-permute-start(bf16[224,256]{1,0:T(8,128)(2,1)} %get-tuple-element.85), channel_id=1, source_target_pairs={{0,16},{1,5},{2,18},{3,7},{4,20},{5,1},{6,22},{7,3},{8,24},{9,13},... | collective-permute-start | bytes 344072 | tf_op jit(solution)/shard_map/ppermute | solution.py:471
  112.5 4.1 %collective-permute-start.8 = (bf16[224,256]{1,0:T(8,128)(2,1)}, bf16[224,256]{1,0:T(8,128)(2,1)S(1)}, u32[]{:S(2)}, u32[]{:S(2)}) collective-permute-start(bf16[224,256]{1,0:T(8,128)(2,1)} %get-tuple-element.86), channel_id=1, source_target_pairs={{0,24},{1,7},{2,26},{3,1},{4,28},{5,3},{6,30},{7,5},{8,0},{9,15},{... | collective-permute-start | bytes 344072 | tf_op jit(solution)/shard_map/ppermute | solution.py:471

commit v5 on v4

--- a/solution.py
+++ b/solution.py
@@ -273,15 +273,22 @@
         filt = (a2 * spec_ref[:, cols(k, DB)].astype(F32)).astype(BF)
         send_ref[:, cols(4 + k, DB)] = mm(m3_ref[...], filt).astype(BF)
 
-    for w in (m2_ref, spec_ref, m3_ref, up_ref, act_ref, dhid_ref):
+    for w in (m2_ref, spec_ref, m3_ref):
+        w.get()
+    for b in range(NB):
+        follow(b)
+    send_ref.flush(2)
+    send_ref.flush(3)
+    for w in (up_ref, act_ref):
         w.get()
     lift(0)
+    lift(1)
+    dhid_ref.get()
     for b in range(NB):
-        if b + 1 < NB:
+        if 0 < b < NB - 1:
             lift(b + 1)
         if b > 0:
             lower(b - 1)
-        follow(b)
         for q in rows_of(32):
             up, act = up2_ref[b % 2, q, :], act2_ref[b % 2, q, :]
             sg = jax.nn.sigmoid(act)
@@ -372,7 +379,8 @@
         outs[d][...] = (
             a_ref[k].astype(F32) + b_ref[k].astype(F32) + c_ref[k].astype(F32) + d_ref[k].astype(F32)
         ).astype(BF)
-    outs[0].flush()
+        if d == 0:
+            outs[0].flush()
 
 
 def k_sum_x(a_ref, b_ref, c_ref, d_ref, mix_ref, up_ref, act_ref, down_ref):

time: 121 us -> 121 us (level)
  no operation moved by 1% of the time
where the time goes in v5:
time: 121 us; the launch traced here: 119 us
  Pallas kernels  43.9 us (36%)
  waiting for transfers between devices  37.4 us (31%)
  starting transfers between devices  33.2 us (27%)
  local copies, waits for them, and re-layouts  3.85 us (3%)
    pallas_call x14, Pallas kernels, call(): pl.pallas_call(body, out_shape=[(jax.ShapeDtypeStruct if o[2] == 'v' else...  43.9 us
    all_to_all x4, waiting for transfers between devices, swap(): return lax.all_to_all(v, 'seq', split_axis=0, concat_axis=0, tiled=True)  32.4 us
    all_to_all x4, starting transfers between devices, swap(): return lax.all_to_all(v, 'seq', split_axis=0, concat_axis=0, tiled=True)  20.4 us
    ppermute x6, starting transfers between devices, ring(): return lax.ppermute(value, 'seq', pairs)  9.57 us
    ppermute x6, waiting for transfers between devices, ring(): return lax.ppermute(value, 'seq', pairs)  4.96 us
    ppermute x2, starting transfers between devices, shift(): return lax.ppermute(v, 'section', pairs)  3 us
  transfers between devices with their start and end apart: 13, of which 7 were waited for; matrix products, arithmetic and copies ran while one was open for 2% of the time, Pallas kernels for 20%

profile of v5, /device:TPU:1, one launch (start us, length us, event | category | flops | bytes accessed | tf_op | source)
XLA Modules:
  0.0 119.3 jit_solution(17887754498896290124)
XLA Ops:
  0.6 0.0 copy-start.7
  0.6 2.7 %shard_map.189 = bf16[256,1024]{1,0:T(8,128)(2,1)} custom-call(bf16[2,128,128]{2,1,0:T(8,128)(2,1)} %bitcast.48, bf16[256,1024]{1,0:T(8,128)(2,1)} %bitcast.28, f32[1,1024]{1,0:T(1,128)} %refs_3_.3), custom_call_target="tpu_custom_call" | custom-call | tf_op jit(solution)/shard_map/pallas_call | solution.py:132
  3.3 8.6 %all-to-all-start = ((bf16[32,8,1024]{2,1,0:T(8,128)(2,1)}), bf16[32,8,1024]{2,1,0:T(8,128)(2,1)S(1)}, u32[]{:S(2)}, u32[]{:S(2)}) async-start(bf16[32,8,1024]{2,1,0:T(8,128)(2,1)} %bitcast.45), calls=%async_computation | async-start | bytes 1048576 | tf_op jit(solution)/shard_map/all_to_all | solution.py:466
  11.9 2.6 %shard_map.191.refs_4_ = bf16[256,1024]{1,0:T(8,128)(2,1)} custom-call(bf16[2,128,128]{2,1,0:T(8,128)(2,1)} %bitcast.49, bf16[256,1024]{1,0:T(8,128)(2,1)} %bitcast.43, f32[1,1024]{1,0:T(1,128)} %refs_3_.3), custom_call_target="tpu_custom_call" | custom-call | tf_op jit(solution)/shard_map/pallas_call | solution.py:132
  14.6 0.0 copy-done.7
  14.6 0.1 reshape_squeeze.3.refs_2_.refs_6_.refs_3_
  14.7 0.0 copy-start.1
  14.7 3.3 %shard_map.190 = (bf16[256,256]{1,0:T(8,128)(2,1)}, bf16[256,256]{1,0:T(8,128)(2,1)S(1)}, bf16[256,256]{1,0:T(8,128)(2,1)}, bf16[256,256]{1,0:T(8,128)(2,1)S(1)}...) custom-call(bf16[2,128,128]{2,1,0:T(8,128)(2,1)} %bitcast.50, ...), custom_call_target="tpu_custom_call" | custom-call | tf_op jit(solution)/shard_map/pallas_call | solution.py:132
  18.1 0.0 copy-start.3
  18.1 0.0 copy-start.4
  18.1 5.5 %all-to-all-done = bf16[32,8,1024]{2,1,0:T(8,128)(2,1)S(1)} async-done(((bf16[32,8,1024]{2,1,0:T(8,128)(2,1)}), bf16[32,8,1024]{2,1,0:T(8,128)(2,1)S(1)}, u32[]{:S(2)}, u32[]{:S(2)}) %all-to-all-start) | async-done | bytes 524320 | tf_op jit(solution)/shard_map/all_to_all | solution.py:466
  23.5 2.4 %shard_map.192 = (bf16[256,2048]{1,0:T(8,128)(2,1)}, f32[256,1024]{1,0:T(8,128)}) custom-call(bf16[256,1024]{1,0:T(8,128)(2,1)S(1)} %bitcast.27, bf16[256,256]{1,0:T(8,128)(2,1)S(1)} %get-tuple-element.49.refs_1_.refs_5_, bf16[256,1024]{1,0:T(8,128)(2,1)S(1)} %reshape_squeeze.3.refs_2_.refs_6_.refs_3_, ...), custom_call_target="tpu_custom_call" | custom-call | tf_op jit(solution)/shard_map/pallas_call | solution.py:132
  25.9 0.0 copy-done.1
  25.9 0.0 copy-done.3
  25.9 0.0 copy-done.4
  25.9 3.7 %all-to-all-start.1 = ((bf16[32,8,2048]{2,1,0:T(8,128)(2,1)}), bf16[32,8,2048]{2,1,0:T(8,128)(2,1)S(1)}, u32[]{:S(2)}, u32[]{:S(2)}) async-start(bf16[32,8,2048]{2,1,0:T(8,128)(2,1)} %bitcast.47), calls=%async_computation.1 | async-start | bytes 2097152 | tf_op jit(solution)/shard_map/all_to_all | solution.py:466
  29.7 3.8 %shard_map.193 = (bf16[256,1024]{1,0:T(8,128)(2,1)}, f32[256,1024]{1,0:T(8,128)S(1)}, bf16[256,2048]{1,0:T(8,128)(2,1)}, bf16[256,1024]{1,0:T(8,128)(2,1)S(1)}, bf16[256,256]{1,0:T(8,128)(2,1)S(1)}) custom-call(bf16[256,1024]{1,0:T(8,128)(2,1)} %bitcast.29, f32[1,1024]{1,0:T(1,128)} %refs_3_.3, bf16[1024,256]{1,0:T(8,128)(2,1)} %bitcast.34, ...), custom_call_target="tpu_custom_call" | custom-call | tf_op jit(solution)/shard_map/pallas_call | solution.py:132
  33.5 13.0 %all-to-all-done.1 = bf16[32,8,2048]{2,1,0:T(8,128)(2,1)S(1)} async-done(((bf16[32,8,2048]{2,1,0:T(8,128)(2,1)}), bf16[32,8,2048]{2,1,0:T(8,128)(2,1)S(1)}, u32[]{:S(2)}, u32[]{:S(2)}) %all-to-all-start.1) | async-done | bytes 1048608 | tf_op jit(solution)/shard_map/all_to_all | solution.py:466
  46.5 6.5 %shard_map.194 = (bf16[256,2048]{1,0:T(8,128)(2,1)}, bf16[256,1024]{1,0:T(8,128)(2,1)}, bf16[256,1024]{1,0:T(8,128)(2,1)}, bf16[256,1024]{1,0:T(8,128)(2,1)}, bf...) custom-call(bf16[256,2048]{1,0:T(8,128)(2,1)S(1)} %bitcast.25, ...), custom_call_target="tpu_custom_call" | custom-call | tf_op jit(solution)/shard_map/pallas_call | solution.py:132
  53.0 4.9 %shard_map.196 = (bf16[4,4,224,256]{3,2,1,0:T(8,128)(2,1)}, bf16[4,4,224,256]{3,2,1,0:T(8,128)(2,1)}, f32[256,1024]{1,0:T(8,128)}) custom-call(bf16[256,1024]{1,0:T(8,128)(2,1)} %get-tuple-element.59.refs_0_, bf16[256,1024]{1,0:T(8,128)(2,1)} %get-tuple-element.60.refs_1_, bf16[1024,256]{1,0:T(8,128)(2,1)} %bitcast.35, ...), custom_call_target="tpu_custom_call" | custom-call | tf_op jit(solution)/shard_map/pallas_call | solution.py:132
  57.9 0.2 collective-permute-start.1
  58.1 4.2 %all-to-all-start.2 = ((bf16[32,8,2048]{2,1,0:T(8,128)(2,1)}), bf16[32,8,2048]{2,1,0:T(8,128)(2,1)S(1)}, u32[]{:S(2)}, u32[]{:S(2)}) async-start(bf16[32,8,2048]{2,1,0:T(8,128)(2,1)} %bitcast.46), calls=%async_computation.2 | async-start | bytes 2097152 | tf_op jit(solution)/shard_map/all_to_all | solution.py:466
  62.2 0.0 collective-permute-done.1.refs_1_
  62.3 0.0 copy-start.2
  62.3 3.1 %shard_map.197 = (bf16[4,224,256]{2,1,0:T(8,128)(2,1)}, bf16[4,224,256]{2,1,0:T(8,128)(2,1)}, bf16[4,224,256]{2,1,0:T(8,128)(2,1)}, bf16[4,224,256]{2,1,0:T(8,12...) custom-call(bf16[4,4,224,256]{3,2,1,0:T(8,128)(2,1)} %get-tuple-element.65.refs_0_, ...), custom_call_target="tpu_custom_call" | custom-call | tf_op jit(solution)/shard_map/pallas_call | solution.py:132
  65.4 0.0 copy-start.5
  65.4 0.6 copy-done.5
  66.1 13.2 %all-to-all-done.2 = bf16[32,8,2048]{2,1,0:T(8,128)(2,1)S(1)} async-done(((bf16[32,8,2048]{2,1,0:T(8,128)(2,1)}), bf16[32,8,2048]{2,1,0:T(8,128)(2,1)S(1)}, u32[]{:S(2)}, u32[]{:S(2)}) %all-to-all-start.2) | async-done | bytes 1048608 | tf_op jit(solution)/shard_map/all_to_all | solution.py:466
  79.2 0.0 copy-start
  79.2 0.0 copy-done.2
  79.2 0.0 copy-start.6
  79.3 1.0 copy-done.6
  80.3 2.4 %shard_map.198 = (bf16[256,1024]{1,0:T(8,128)(2,1)}, bf16[256,1024]{1,0:T(8,128)(2,1)}) custom-call(bf16[256,2048]{1,0:T(8,128)(2,1)S(1)} %bitcast.23, bf16[256,256]{1,0:T(8,128)(2,1)S(1)} %get-tuple-element.69.refs_1_, f32[256,1024]{1,0:T(8,128)} %get-tuple-element.70.refs_2_, bf16[256,1024]{1,0:T(8,128)(2,1)S(1)} %copy-done.2, bf16[256,256]{1,0:T(8,128)(2,1)S(1)} %copy-done.6), custom_call_target="tpu_custom_call" | custom-call | tf_op jit(solution)/shard_map/pallas_call | solution.py:132
  82.7 0.0 copy-done
  82.7 3.9 %all-to-all-start.3 = ((bf16[32,8,1024]{2,1,0:T(8,128)(2,1)}), bf16[32,8,1024]{2,1,0:T(8,128)(2,1)S(1)}, u32[]{:S(2)}, u32[]{:S(2)}) async-start(bf16[32,8,1024]{2,1,0:T(8,128)(2,1)} %bitcast.51), calls=%async_computation.3 | async-start | bytes 1048576 | tf_op jit(solution)/shard_map/all_to_all | solution.py:466
  86.6 1.4 %collective-permute-start.3 = (bf16[4,224,256]{2,1,0:T(8,128)(2,1)}, bf16[4,224,256]{2,1,0:T(8,128)(2,1)S(1)}, u32[]{:S(2)}, u32[]{:S(2)}) collective-permute-start(bf16[4,224,256]{2,1,0:T(8,128)(2,1)} %get-tuple-element.80), channel_id=1, source_target_pairs={{0,2},{1,9},{2,4},{3,11},{4,6},{5,13},{6,0},{7,15},{8,10},{9,17},{... | collective-permute-start | bytes 1376264 | tf_op jit(solution)/shard_map/ppermute | solution.py:479
  88.0 2.4 %collective-permute-start.4 = (bf16[4,224,256]{2,1,0:T(8,128)(2,1)}, bf16[4,224,256]{2,1,0:T(8,128)(2,1)S(1)}, u32[]{:S(2)}, u32[]{:S(2)}) collective-permute-start(bf16[4,224,256]{2,1,0:T(8,128)(2,1)} %get-tuple-element.81), channel_id=1, source_target_pairs={{0,4},{1,17},{2,6},{3,19},{4,0},{5,21},{6,2},{7,23},{8,12},{9,25},... | collective-permute-start | bytes 1376264 | tf_op jit(solution)/shard_map/ppermute | solution.py:479
  90.5 1.1 collective-permute-start.5
  91.6 4.3 %shard_map.195 = bf16[256,1024]{1,0:T(8,128)(2,1)S(1)} custom-call(bf16[256,2048]{1,0:T(8,128)(2,1)} %bitcast.24, bf16[256,256]{1,0:T(8,128)(2,1)} %get-tuple-element.52.refs_5_.refs_1_, bf16[256,1024]{1,0:T(8,128)(2,1)} %bitcast.44, f32[1,1024]{1,0:T(1,128)} %refs_3_.3, bf16[1024,256]{1,0:T(8,128)(2,1)} %bitcast.36, f32[1,1024]{1,0:T(1,128)} %refs_5_.1, ...), custom_call_target="tpu_custom_call" | custom-call | tf_op jit(solution)/shard_map/pallas_call | solution.py:132
  95.9 1.7 %collective-permute-start = (bf16[256,1024]{1,0:T(8,128)(2,1)S(1)}, bf16[256,1024]{1,0:T(8,128)(2,1)S(1)}, u32[]{:S(2)}, u32[]{:S(2)}) collective-permute-start(bf16[256,1024]{1,0:T(8,128)(2,1)S(1)} %shard_map.195), channel_id=1, source_target_pairs={{0,32},{32,64},{64,96},{96,128},{128,160},{160,192},{192,224},{224... | collective-permute-start | bytes 1572872 | tf_op jit(solution)/shard_map/ppermute | solution.py:485
  97.6 0.8 all-to-all-done.3
  98.4 2.5 %shard_map.199 = bf16[256,1024]{1,0:T(8,128)(2,1)S(1)} custom-call(bf16[256,1024]{1,0:T(8,128)(2,1)S(1)} %bitcast.26, bf16[256,256]{1,0:T(8,128)(2,1)} %get-tuple-element.73.refs_1_, bf16[256,1024]{1,0:T(8,128)(2,1)} %bitcast.30, f32[1,1024]{1,0:T(1,128)} %refs_3_.3, f32[256,1024]{1,0:T(8,128)} %get-tuple-element.74.refs_4_, ...), custom_call_target="tpu_custom_call" | custom-call | tf_op jit(solution)/shard_map/pallas_call | solution.py:132
  100.9 1.3 %collective-permute-start.2 = (bf16[256,1024]{1,0:T(8,128)(2,1)S(1)}, bf16[256,1024]{1,0:T(8,128)(2,1)S(1)}, u32[]{:S(2)}, u32[]{:S(2)}) collective-permute-start(bf16[256,1024]{1,0:T(8,128)(2,1)S(1)} %shard_map.199), channel_id=1, source_target_pairs={{32,0},{64,32},{96,64},{128,96},{160,128},{192,160},{224,192},{33,... | collective-permute-start | bytes 1572872 | tf_op jit(solution)/shard_map/ppermute | solution.py:485
  102.2 0.0 collective-permute-done.3.refs_1_
  102.2 4.0 %collective-permute-done.4.refs_2_ = bf16[4,224,256]{2,1,0:T(8,128)(2,1)S(1)} collective-permute-done((bf16[4,224,256]{2,1,0:T(8,128)(2,1)}, bf16[4,224,256]{2,1,0:T(8,128)(2,1)S(1)}, u32[]{:S(2)}, u32[]{:S(2)}) %collective-permute-start.4) | collective-permute-done | bytes 458784 | tf_op jit(solution)/shard_map/ppermute | solution.py:479
  106.2 0.0 collective-permute-done.5.refs_3_
  106.2 2.5 %shard_map.201 = (bf16[224,256]{1,0:T(8,128)(2,1)}, bf16[224,256]{1,0:T(8,128)(2,1)}, bf16[224,256]{1,0:T(8,128)(2,1)}, bf16[224,256]{1,0:T(8,128)(2,1)}) custom-call(bf16[4,224,256]{2,1,0:T(8,128)(2,1)} %get-tuple-element.79.refs_0_, bf16[4,224,256]{2,1,0:T(8,128)(2,1)S(1)} %collective-permute-done.3.refs_1_, ...), custom_call_target="tpu_custom_call" | custom-call | tf_op jit(solution)/shard_map/pallas_call | solution.py:132
  108.8 1.0 collective-permute-start.6
  109.7 2.4 %collective-permute-start.7 = (bf16[224,256]{1,0:T(8,128)(2,1)}, bf16[224,256]{1,0:T(8,128)(2,1)S(1)}, u32[]{:S(2)}, u32[]{:S(2)}) collective-permute-start(bf16[224,256]{1,0:T(8,128)(2,1)} %get-tuple-element.85), channel_id=1, source_target_pairs={{0,16},{1,5},{2,18},{3,7},{4,20},{5,1},{6,22},{7,3},{8,24},{9,13},... | collective-permute-start | bytes 344072 | tf_op jit(solution)/shard_map/ppermute | solution.py:479
  112.2 1.2 collective-permute-start.8
  113.3 2.0 %reshape.25 = bf16[1,64,4,1024]{3,2,1,0:T(4,128)(2,1)} reshape(bf16[256,1024]{1,0:T(8,128)(2,1)} %get-tuple-element.78) | data formatting | bytes 1048576 | tf_op jit(solution)/shard_map/reshape | solution.py:584
  115.4 0.0 collective-permute-done.6.refs_1_
  115.4 0.7 collective-permute-done.7.refs_2_
  116.1 0.2 collective-permute-done.8.refs_3_
  116.3 1.8 %shard_map.202 = (bf16[32,256]{1,0:T(8,128)(2,1)}, bf16[32,512]{1,0:T(8,128)(2,1)}, bf16[32,512]{1,0:T(8,128)(2,1)}, bf16[64,256]{1,0:T(8,128)(2,1)}) custom-call(bf16[224,256]{1,0:T(8,128)(2,1)} %get-tuple-element.83.refs_0_, bf16[224,256]{1,0:T(8,128)(2,1)S(1)} %collective-permute-done.6.refs_1_, bf16[224,256]{1,0:T(8,128)(2,1)S(1)} %collective-permute-done.7.refs_2_, ...), custom_call_target="tpu_custom_call" | custom-call | tf_op jit(solution)/shard_map/pallas_call | solution.py:132
  118.1 0.0 collective-permute-done.refs_0_
  118.1 0.0 collective-permute-done.2.refs_1_
  118.1 1.1 shard_map.200
Async XLA Ops:
  0.6 14.0 %copy-start.7 = (bf16[1,64,4,1024]{3,2,1,0:T(4,128)(2,1)S(1)}, bf16[1,64,4,1024]{3,2,1,0:T(4,128)(2,1)}, u32[]{:S(2)}) copy-start(bf16[1,64,4,1024]{3,2,1,0:T(4,128)(2,1)} %param.21) | copy-start | bytes 1572868
  3.3 20.2 %all-to-all-start = ((bf16[32,8,1024]{2,1,0:T(8,128)(2,1)}), bf16[32,8,1024]{2,1,0:T(8,128)(2,1)S(1)}, u32[]{:S(2)}, u32[]{:S(2)}) async-start(bf16[32,8,1024]{2,1,0:T(8,128)(2,1)} %bitcast.45), calls=%async_computation | async-start | bytes 1048576 | tf_op jit(solution)/shard_map/all_to_all | solution.py:466
  14.7 11.2 %copy-start.1 = (bf16[256,1024]{1,0:T(8,128)(2,1)}, bf16[256,1024]{1,0:T(8,128)(2,1)S(1)}, u32[]{:S(2)}) copy-start(bf16[256,1024]{1,0:T(8,128)(2,1)S(1)} %reshape_squeeze.3.refs_2_.refs_6_.refs_3_) | copy-start | bytes 1572868
  18.1 7.9 %copy-start.3 = (bf16[256,256]{1,0:T(8,128)(2,1)}, bf16[256,256]{1,0:T(8,128)(2,1)S(1)}, u32[]{:S(2)}) copy-start(bf16[256,256]{1,0:T(8,128)(2,1)S(1)} %get-tuple-element.49.refs_1_.refs_5_) | copy-start | bytes 393220
  18.1 7.9 %copy-start.4 = (bf16[256,256]{1,0:T(8,128)(2,1)}, bf16[256,256]{1,0:T(8,128)(2,1)S(1)}, u32[]{:S(2)}) copy-start(bf16[256,256]{1,0:T(8,128)(2,1)S(1)} %get-tuple-element.50.refs_3_.refs_7_) | copy-start | bytes 393220
  25.9 20.5 %all-to-all-start.1 = ((bf16[32,8,2048]{2,1,0:T(8,128)(2,1)}), bf16[32,8,2048]{2,1,0:T(8,128)(2,1)S(1)}, u32[]{:S(2)}, u32[]{:S(2)}) async-start(bf16[32,8,2048]{2,1,0:T(8,128)(2,1)} %bitcast.47), calls=%async_computation.1 | async-start | bytes 2097152 | tf_op jit(solution)/shard_map/all_to_all | solution.py:466
  57.9 4.4 %collective-permute-start.1 = (bf16[4,4,224,256]{3,2,1,0:T(8,128)(2,1)}, bf16[4,4,224,256]{3,2,1,0:T(8,128)(2,1)S(1)}, u32[]{:S(2)}, u32[]{:S(2)}) collective-permute-start(bf16[4,4,224,256]{3,2,1,0:T(8,128)(2,1)} %get-tuple-element.66), channel_id=1, source_target_pairs={{0,1},{1,0},{2,3},{3,2},{4,5},{5,4},{6,7},{7,6},{8,9},{9,8},{10,11... | collective-permute-start | bytes 5505032 | tf_op jit(solution)/shard_map/ppermute | solution.py:546
  58.1 21.2 %all-to-all-start.2 = ((bf16[32,8,2048]{2,1,0:T(8,128)(2,1)}), bf16[32,8,2048]{2,1,0:T(8,128)(2,1)S(1)}, u32[]{:S(2)}, u32[]{:S(2)}) async-start(bf16[32,8,2048]{2,1,0:T(8,128)(2,1)} %bitcast.46), calls=%async_computation.2 | async-start | bytes 2097152 | tf_op jit(solution)/shard_map/all_to_all | solution.py:466
  62.3 17.0 %copy-start.2 = (bf16[256,1024]{1,0:T(8,128)(2,1)S(1)}, bf16[256,1024]{1,0:T(8,128)(2,1)}, u32[]{:S(2)}) copy-start(bf16[256,1024]{1,0:T(8,128)(2,1)} %copy-done.1) | copy-start | bytes 1572868
  65.4 0.7 copy-start.5
  79.2 3.4 %copy-start = (bf16[32,8,2048]{2,1,0:T(8,128)(2,1)}, bf16[32,8,2048]{2,1,0:T(8,128)(2,1)S(1)}, u32[]{:S(2)}) copy-start(bf16[32,8,2048]{2,1,0:T(8,128)(2,1)S(1)} %all-to-all-done.2) | copy-start | bytes 3145732
  79.2 1.0 copy-start.6
  82.7 15.7 %all-to-all-start.3 = ((bf16[32,8,1024]{2,1,0:T(8,128)(2,1)}), bf16[32,8,1024]{2,1,0:T(8,128)(2,1)S(1)}, u32[]{:S(2)}, u32[]{:S(2)}) async-start(bf16[32,8,1024]{2,1,0:T(8,128)(2,1)} %bitcast.51), calls=%async_computation.3 | async-start | bytes 1048576 | tf_op jit(solution)/shard_map/all_to_all | solution.py:466
  86.6 15.6 %collective-permute-start.3 = (bf16[4,224,256]{2,1,0:T(8,128)(2,1)}, bf16[4,224,256]{2,1,0:T(8,128)(2,1)S(1)}, u32[]{:S(2)}, u32[]{:S(2)}) collective-permute-start(bf16[4,224,256]{2,1,0:T(8,128)(2,1)} %get-tuple-element.80), channel_id=1, source_target_pairs={{0,2},{1,9},{2,4},{3,11},{4,6},{5,13},{6,0},{7,15},{8,10},{9,17},{... | collective-permute-start | bytes 1376264 | tf_op jit(solution)/shard_map/ppermute | solution.py:479
  88.0 18.2 %collective-permute-start.4 = (bf16[4,224,256]{2,1,0:T(8,128)(2,1)}, bf16[4,224,256]{2,1,0:T(8,128)(2,1)S(1)}, u32[]{:S(2)}, u32[]{:S(2)}) collective-permute-start(bf16[4,224,256]{2,1,0:T(8,128)(2,1)} %get-tuple-element.81), channel_id=1, source_target_pairs={{0,4},{1,17},{2,6},{3,19},{4,0},{5,21},{6,2},{7,23},{8,12},{9,25},... | collective-permute-start | bytes 1376264 | tf_op jit(solution)/shard_map/ppermute | solution.py:479
  90.5 15.8 %collective-permute-start.5 = (bf16[4,224,256]{2,1,0:T(8,128)(2,1)}, bf16[4,224,256]{2,1,0:T(8,128)(2,1)S(1)}, u32[]{:S(2)}, u32[]{:S(2)}) collective-permute-start(bf16[4,224,256]{2,1,0:T(8,128)(2,1)} %get-tuple-element.82), channel_id=1, source_target_pairs={{0,6},{1,25},{2,0},{3,27},{4,2},{5,29},{6,4},{7,31},{8,14},{9,1},{... | collective-permute-start | bytes 1376264 | tf_op jit(solution)/shard_map/ppermute | solution.py:479
  95.9 22.2 %collective-permute-start = (bf16[256,1024]{1,0:T(8,128)(2,1)S(1)}, bf16[256,1024]{1,0:T(8,128)(2,1)S(1)}, u32[]{:S(2)}, u32[]{:S(2)}) collective-permute-start(bf16[256,1024]{1,0:T(8,128)(2,1)S(1)} %shard_map.195), channel_id=1, source_target_pairs={{0,32},{32,64},{64,96},{96,128},{128,160},{160,192},{192,224},{224... | collective-permute-start | bytes 1572872 | tf_op jit(solution)/shard_map/ppermute | solution.py:485
  100.9 17.2 %collective-permute-start.2 = (bf16[256,1024]{1,0:T(8,128)(2,1)S(1)}, bf16[256,1024]{1,0:T(8,128)(2,1)S(1)}, u32[]{:S(2)}, u32[]{:S(2)}) collective-permute-start(bf16[256,1024]{1,0:T(8,128)(2,1)S(1)} %shard_map.199), channel_id=1, source_target_pairs={{32,0},{64,32},{96,64},{128,96},{160,128},{192,160},{224,192},{33,... | collective-permute-start | bytes 1572872 | tf_op jit(solution)/shard_map/ppermute | solution.py:485
  108.8 6.6 %collective-permute-start.6 = (bf16[224,256]{1,0:T(8,128)(2,1)}, bf16[224,256]{1,0:T(8,128)(2,1)S(1)}, u32[]{:S(2)}, u32[]{:S(2)}) collective-permute-start(bf16[224,256]{1,0:T(8,128)(2,1)} %get-tuple-element.84), channel_id=1, source_target_pairs={{0,8},{1,3},{2,10},{3,5},{4,12},{5,7},{6,14},{7,1},{8,16},{9,11},{... | collective-permute-start | bytes 344072 | tf_op jit(solution)/shard_map/ppermute | solution.py:479
  109.7 6.3 %collective-permute-start.7 = (bf16[224,256]{1,0:T(8,128)(2,1)}, bf16[224,256]{1,0:T(8,128)(2,1)S(1)}, u32[]{:S(2)}, u32[]{:S(2)}) collective-permute-start(bf16[224,256]{1,0:T(8,128)(2,1)} %get-tuple-element.85), channel_id=1, source_target_pairs={{0,16},{1,5},{2,18},{3,7},{4,20},{5,1},{6,22},{7,3},{8,24},{9,13},... | collective-permute-start | bytes 344072 | tf_op jit(solution)/shard_map/ppermute | solution.py:479
  112.2 4.1 %collective-permute-start.8 = (bf16[224,256]{1,0:T(8,128)(2,1)}, bf16[224,256]{1,0:T(8,128)(2,1)S(1)}, u32[]{:S(2)}, u32[]{:S(2)}) collective-permute-start(bf16[224,256]{1,0:T(8,128)(2,1)} %get-tuple-element.86), channel_id=1, source_target_pairs={{0,24},{1,7},{2,26},{3,1},{4,28},{5,3},{6,30},{7,5},{8,0},{9,15},{... | collective-permute-start | bytes 344072 | tf_op jit(solution)/shard_map/ppermute | solution.py:479
